TPU v7x, 32 devices: a whole 2x2x4 slice. The times are simulated.
32 devices in a mesh: row: 4 (over z), col: 8 (over y, x, core).
Axes of the slice: x: 2, y: 2, z: 4, core: 2. Of those that a mesh axis runs over, the one named last changes fastest.
Arguments:
- gram: bfloat16 [2, 4, 256, 16, 8, 256], P(None, 'row', None, None, 'col'), as said below
Outputs:
- schur: float32 [2, 4, 256, 16, 8, 256], P(None, 'row', None, None, 'col')
Inputs may be any that keep to these rules, and one draw needn't show every extreme that they name: `gram`: the first 2048 columns of the slab form a symmetric matrix, and its leading 2 * 256 x 2 * 256 block is positive definite with smallest eigenvalue above 10.
All inputs are finite; a program needn't handle non-finite values.
Results may differ from a plain program's by a relative error of at most 0.0018.
Values may be sent and summed in bfloat16 or wider, within the bound.
No kernel may reach another device: no remote copies, remote signals or barrier semaphores. Data moves between devices by JAX's collectives and lax.ppermute only.
A program may use at most 64 MiB of HBM per device.

v0:
```python
import jax
import jax.numpy as jnp
from jax import lax
from jax.sharding import PartitionSpec as P


def from_root(block, axis, source):
    block = jnp.where(lax.axis_index(axis) == source, block, jnp.zeros_like(block))
    return lax.psum(block, axis)


def local(gram):
    n_row = lax.axis_size("row")
    n_col = lax.axis_size("col")
    my_row = lax.axis_index("row")
    my_col = lax.axis_index("col")
    row_slots = gram.shape[0]
    tile_size = gram.shape[2]
    col_slots = gram.shape[3]
    slabs = [gram[row_slot, 0, :, :, 0, :].astype(jnp.float32) for row_slot in range(row_slots)]
    col_tile = jnp.arange(col_slots) * n_col + my_col
    row_tile = jnp.arange(row_slots) * n_row + my_row
    every_slot = list(range(row_slots))
    for panel_index in range(2):
        panel_rows = slabs[panel_index // n_row]
        corner = from_root(
            panel_rows[:, panel_index // n_col, :].astype(jnp.bfloat16), "col", panel_index % n_col
        ).astype(jnp.float32)
        triangle = jnp.linalg.cholesky(corner)
        solved = jax.scipy.linalg.solve_triangular(
            triangle, panel_rows.reshape(tile_size, col_slots * tile_size), lower=True
        )
        solved = solved.reshape(tile_size, col_slots, tile_size)
        solved = jnp.where((col_tile >= panel_index)[None, :, None], solved, 0.0).astype(
            jnp.bfloat16
        )
        factor_across = from_root(solved, "row", panel_index % n_row)
        factor_transposed = []
        for factor_row_slot in range(row_slots):
            target = factor_row_slot * n_row + my_row
            chosen = lax.dynamic_index_in_dim(factor_across, target // n_col, 1, keepdims=False)
            factor_transposed.append(from_root(chosen, "col", target % n_col))
        updated = list(slabs)
        for apply_row_slot in every_slot:
            product = jnp.einsum(
                "pi,pjq->ijq",
                factor_transposed[apply_row_slot],
                factor_across,
                preferred_element_type=jnp.float32,
            )
            updated[apply_row_slot] = updated[apply_row_slot] - product
        slabs = updated
    blocks = jnp.stack(slabs, axis=0)
    retain = (row_tile >= 2)[:, None, None, None] & (col_tile >= 2)[None, None, :, None]
    result = jnp.where(retain, blocks, 0.0)
    return result[:, None, :, :, None, :]


def solution(mesh):
    in_specs = (P(None, "row", None, None, "col", None),)
    out_specs = P(None, "row", None, None, "col", None)
    return jax.shard_map(local, mesh=mesh, in_specs=in_specs, out_specs=out_specs, check_vma=False)
```

profile of v0, /device:TPU:16, one launch (start us, length us, event | category | flops | bytes accessed | tf_op | source)
XLA Modules:
  0.0 607.0 jit_solution(9396137955365741867)
XLA Ops:
  6.5 4.5 fusion.30
  11.0 3.0 copy.24
  14.8 2.5 bitcast_convert_fusion
  17.3 51.6 %all-reduce.9.cloned.1.call-done = bf16[256,256]{0,1:T(8,128)(2,1)} async-done(((bf16[256,256]{0,1:T(8,128)(2,1)}), bf16[256,256]{0,1:T(8,128)(2,1)}) %all-reduce.9.cloned.1.call-update) | async-done | bytes 131088 | tf_op jit(solution)/shard_map/psum | solution.py:9
  68.9 1.0 copy.3
  69.9 0.9 fusion.9
  70.8 11.7 %cholesky.130 = f32[128,128]{1,0:T(8,128)S(1)} custom-call(f32[128,128]{1,0:T(8,128)S(1)} %cholesky.194), custom_call_target="Cholesky" | custom-call | tf_op jit(solution)/shard_map/jit(cholesky)/cholesky | solution.py:29
  82.6 9.8 %custom-call.13 = f32[1,128,128]{1,2,0:T(8,128)S(1)} custom-call(f32[1,128,128]{2,1,0:T(8,128)S(1)} %get-tuple-element.59), custom_call_target="InvertDiagBlocksLowerTriangular" | custom-call | tf_op jit(solution)/shard_map/jit(cholesky)/cholesky | solution.py:29
  92.9 11.7 %cholesky.147 = f32[128,128]{1,0:T(8,128)S(1)} custom-call(f32[128,128]{1,0:T(8,128)S(1)} %convolution_subtract_fusion.3), custom_call_target="Cholesky" | custom-call | tf_op jit(solution)/shard_map/jit(cholesky)/cholesky | solution.py:29
  106.6 4.0 while.4
  107.4 1.3 bitcast_dynamic-update-slice_fusion.4
  109.3 1.3 bitcast_dynamic-update-slice_fusion.4
  110.6 19.7 %custom-call.14 = f32[2,128,128]{1,2,0:T(8,128)S(1)} custom-call(f32[2,128,128]{2,1,0:T(8,128)S(1)} %get-tuple-element.21), custom_call_target="InvertDiagBlocksLowerTriangular" | custom-call | tf_op jit(solution)/shard_map/jit(_solve_triangular)/triangular_solve | solution.py:30
  130.3 3.7 fusion.6
  133.9 3.5 convolution_subtract_fusion.1
  137.5 1.9 fusion.23
  139.4 1.6 pad_maximum_fusion
  141.0 4.1 copy.4
  145.1 3.5 fusion.2
  148.7 84.8 %all-reduce.11.cloned.1.call-done = bf16[256,16,256]{0,2,1:T(8,128)(2,1)} async-done(((bf16[256,16,256]{0,2,1:T(8,128)(2,1)}), bf16[256,16,256]{0,2,1:T(8,128)(2,1)}) %all-reduce.11.cloned.1.call-update) | async-done | bytes 2097168 | tf_op jit(solution)/shard_map/psum | solution.py:9
  233.5 1.7 select_bitcast_fusion.3
  235.3 54.4 %all-reduce.13.cloned.1.call-done = bf16[256,256]{0,1:T(8,128)(2,1)} async-done(((bf16[256,256]{0,1:T(8,128)(2,1)}), bf16[256,256]{0,1:T(8,128)(2,1)}) %all-reduce.13.cloned.1.call-update) | async-done | bytes 131088 | tf_op jit(solution)/shard_map/psum | solution.py:9
  289.6 2.4 convert_subtract_fusion.1
  292.0 2.0 copy-done
  295.2 52.0 %all-reduce.15.cloned.1.call-done = bf16[256,256]{0,1:T(8,128)(2,1)} async-done(((bf16[256,256]{0,1:T(8,128)(2,1)}), bf16[256,256]{0,1:T(8,128)(2,1)}) %all-reduce.15.cloned.1.call-update) | async-done | bytes 131088 | tf_op jit(solution)/shard_map/psum | solution.py:9
  347.2 1.0 copy.6
  348.2 0.9 fusion.8
  349.2 11.7 %cholesky.164 = f32[128,128]{1,0:T(8,128)S(1)} custom-call(f32[128,128]{1,0:T(8,128)S(1)} %cholesky.197), custom_call_target="Cholesky" | custom-call | tf_op jit(solution)/shard_map/jit(cholesky)/cholesky | solution.py:29
  361.6 9.8 %custom-call.15 = f32[1,128,128]{1,2,0:T(8,128)S(1)} custom-call(f32[1,128,128]{2,1,0:T(8,128)S(1)} %get-tuple-element.55), custom_call_target="InvertDiagBlocksLowerTriangular" | custom-call | tf_op jit(solution)/shard_map/jit(cholesky)/cholesky | solution.py:29
  372.0 11.7 %cholesky.181 = f32[128,128]{1,0:T(8,128)S(1)} custom-call(f32[128,128]{1,0:T(8,128)S(1)} %convolution_subtract_fusion.2), custom_call_target="Cholesky" | custom-call | tf_op jit(solution)/shard_map/jit(cholesky)/cholesky | solution.py:29
  385.7 4.3 while.5
  386.5 1.3 bitcast_dynamic-update-slice_fusion.5
  388.6 1.3 bitcast_dynamic-update-slice_fusion.5
  389.9 19.7 %custom-call.16 = f32[2,128,128]{1,2,0:T(8,128)S(1)} custom-call(f32[2,128,128]{2,1,0:T(8,128)S(1)} %get-tuple-element.22), custom_call_target="InvertDiagBlocksLowerTriangular" | custom-call | tf_op jit(solution)/shard_map/jit(_solve_triangular)/triangular_solve | solution.py:30
  409.6 3.7 fusion.4
  413.3 3.5 convolution_subtract_fusion
  416.8 1.9 fusion.19
  418.8 1.6 pad_maximum_fusion.1
  420.4 3.3 copy.7
  423.6 1.9 fusion.3
  425.6 1.5 copy-done.6
  427.2 2.9 copy.25
  430.1 80.3 %all-reduce.17.cloned.1.call-done = bf16[256,16,256]{0,2,1:T(8,128)(2,1)} async-done(((bf16[256,16,256]{0,2,1:T(8,128)(2,1)}), bf16[256,16,256]{0,2,1:T(8,128)(2,1)}) %all-reduce.17.cloned.1.call-update) | async-done | bytes 2097168 | tf_op jit(solution)/shard_map/psum | solution.py:9
  510.5 1.7 select_bitcast_fusion.2
  512.3 56.5 %all-reduce.19.cloned.1.call-done = (bf16[256,256]{0,1:T(8,128)(2,1)}, bf16[256,256]{0,1:T(8,128)(2,1)}, bf16[256,256]{0,1:T(8,128)(2,1)}) async-done(((bf16[256,256]{0,1:T(8,128)(2,1)}, bf16[256,256]{0,1:T(8,128)(2,1)}, bf16[256,256]{0,1:T(8,128)(2,1)}), (bf16[256,256]{0,1:T(8,128)(2,1)}, bf16[256,256]{0,1:T(8,128)(2,1)}, bf16[256,256]{0,1:T(8,128)(2,1)})) %all-reduce.19.cloned.1.call-update) | async-done | bytes 393232 | tf_op jit(solution)/shard_map/psum | solution.py:9
  568.8 3.7 subtract_bitcast_fusion
  575.6 3.9 maximum_select_fusion
  579.5 20.5 %copy.15 = f32[2,1,256,16,1,256]{5,4,3,2,1,0:T(1,128)} copy(f32[2,1,256,16,1,256]{2,5,3,4,1,0:T(8,128)} %maximum_select_fusion) | data formatting | bytes 16777216 | tf_op jit(solution)/shard_map/jit(_where)/select_n | solution.py:55
  (66 shorter events, 11.0 us)
Async XLA Ops:
  6.5 62.3 %all-reduce.9.cloned.1.call-start = ((), (), s32[]{:S(2)}) async-start(), calls=%async_computation | async-start | bytes 262144 | tf_op jit(solution)/shard_map/psum | solution.py:9
  14.7 218.8 %all-reduce.11.cloned.1.call-start = ((), (), s32[]{:S(2)}) async-start(), calls=%async_computation.1 | async-start | bytes 4194304 | tf_op jit(solution)/shard_map/psum | solution.py:9
  130.3 3.7 copy-start.2
  148.6 141.0 %all-reduce.13.cloned.1.call-start = ((), (), s32[]{:S(2)}) async-start(), calls=%async_computation.2 | async-start | bytes 262144 | tf_op jit(solution)/shard_map/psum | solution.py:9
  235.2 112.0 %all-reduce.15.cloned.1.call-start = ((), (), s32[]{:S(2)}) async-start(), calls=%async_computation.3 | async-start | bytes 262144 | tf_op jit(solution)/shard_map/psum | solution.py:9
  292.0 2.0 copy-start
  294.7 215.7 %all-reduce.17.cloned.1.call-start = ((), (), s32[]{:S(2)}) async-start(), calls=%async_computation.4 | async-start | bytes 4194304 | tf_op jit(solution)/shard_map/psum | solution.py:9
  409.6 3.7 copy-start.1
  425.6 1.6 copy-start.6
  425.6 143.2 %all-reduce.19.cloned.1.call-start = ((), (), s32[]{:S(2)}) async-start(), calls=%async_computation.5 | async-start | bytes 786432 | tf_op jit(solution)/shard_map/psum | solution.py:9
  568.8 3.8 copy-start.3
  568.8 3.8 copy-start.8
  572.6 1.6 copy-start.4
  572.6 2.2 copy-start.5
  572.6 2.2 copy-start.7
Sparse Core Ops, SparseCore 0:
  14.9 53.9 all-reduce.8
  148.7 84.7 all-reduce.10
  236.5 53.0 all-reduce.12
  294.8 52.3 all-reduce.14
  425.7 84.6 all-reduce.16
  514.1 54.7 all-reduce.18
where the time goes:
time: 618 us; the launch traced here: 607 us
  waiting for transfers between devices  380 us (61%)
  other arithmetic  130 us (21%)
  local copies, waits for them, and re-layouts  53.2 us (9%)
  matrix products  26.8 us (4%)
  between operations  16.5 us (3%)
    psum x6, waiting for transfers between devices, from_root(): return lax.psum(block, axis)  380 us
    another operation x13, other arithmetic, local(): triangle = jnp.linalg.cholesky(corner)  68.6 us
    another operation x7, other arithmetic, local(): jax.scipy.linalg.solve_triangular(triangle, panel_rows.reshape(tile_size,...  42.5 us
    select_n x1, local copies, waits for them, and re-layouts, local(): result = jnp.where(retain, blocks, 0.0)  20.5 us
    another operation x6, matrix products, local(): jax.scipy.linalg.solve_triangular(triangle, panel_rows.reshape(tile_size,...  18.3 us
    another operation x17, local copies, waits for them, and re-layouts, local(): jax.scipy.linalg.solve_triangular(triangle, panel_rows.reshape(tile_size,...  15.2 us
  transfers between devices with their start and end apart: 6, of which 6 were waited for; matrix products, arithmetic and copies ran while one was open for 1% of the time, Pallas kernels for 0%

commit v1 on v0

v1 whole, which is shorter than its diff:
```python
import jax
import jax.numpy as jnp
from jax import lax
from jax.experimental import pallas as pl
from jax.experimental.pallas import tpu as pltpu
from jax.sharding import PartitionSpec as P

F32 = jnp.float32
BF16 = jnp.bfloat16
HIGHEST = lax.Precision.HIGHEST
NB = 64


def lane(x, j):
    return jnp.broadcast_to(x[:, j : j + 1], x.shape)


def sublane(x, j):
    return jnp.broadcast_to(x[j : j + 1, :], x.shape)


def inverse_factor(block):
    diagonal = lax.broadcasted_iota(jnp.int32, (NB, NB), 0) == lax.broadcasted_iota(jnp.int32, (NB, NB), 1)
    wide = jnp.concatenate([block, diagonal.astype(F32)], axis=1)
    groups = NB // 8
    sub = lax.broadcasted_iota(jnp.int32, (8, 2 * NB), 0)

    def group(g, tiles):
        pivot = tiles[0]
        cols = [lane(pivot, j) for j in range(8)]
        upper, recips, rows, scale = {}, [], [], None
        for j in range(8):
            d = sublane(cols[j], j)
            recips.append(1.0 / d)
            factor = jnp.where(sub > j, cols[j] * recips[j], 0.0)
            for l in range(j + 1, 8):
                upper[j, l] = sublane(cols[l], j)
                cols[l] = cols[l] - factor * upper[j, l]
            rows.append(sublane(pivot, j))
            pivot = pivot - factor * rows[j]
            root = lax.rsqrt(d)
            scale = root if scale is None else jnp.where(sub >= j, root, scale)
        out = []
        for i in range(1, groups):
            live = i < groups - g
            tile = tiles[i]
            own = [lane(tile, j) for j in range(8)]
            for j in range(8):
                factor = own[j] * recips[j]
                for l in range(j + 1, 8):
                    own[l] = own[l] - factor * upper[j, l]
                tile = tile - jnp.where(live, factor, 0.0) * rows[j]
            out.append(tile)
        out.append(pivot * scale)
        return tuple(pltpu.roll(t, 2 * NB - 8, 1) for t in out)

    tiles = tuple(wide[8 * i : 8 * i + 8] for i in range(groups))
    tiles = lax.fori_loop(0, groups, group, tiles)
    return jnp.concatenate(tiles, axis=0)[:, :NB]


def eliminate(work, inverse):
    size = work.shape[0]
    inverse[...] = (
        lax.broadcasted_iota(jnp.int32, (size, size), 0) == lax.broadcasted_iota(jnp.int32, (size, size), 1)
    ).astype(F32)
    for j in range(size // NB):
        lo, hi = j * NB, (j + 1) * NB
        own = inverse_factor(work[lo:hi, lo:hi])
        right = jnp.dot(own, work[lo:hi, :], precision=HIGHEST, preferred_element_type=F32)
        left = jnp.dot(own, inverse[lo:hi, :], precision=HIGHEST, preferred_element_type=F32)
        inverse[lo:hi, :] = left
        if hi < size:
            down = right[:, hi:].T
            work[hi:, :] -= jnp.dot(down, right, precision=HIGHEST, preferred_element_type=F32)
            inverse[hi:, :] -= jnp.dot(down, left, precision=HIGHEST, preferred_element_type=F32)


def split(x):
    high = x.astype(BF16)
    return high, (x - high.astype(F32)).astype(BF16)


def mm(a, b):
    return jnp.dot(a, b, preferred_element_type=F32)


def mmt(a, b):
    return lax.dot_general(a, b, (((1,), (1,)), ((), ())), preferred_element_type=F32)


def first_factor(corner, high_out, mid_out, work, inverse):
    work[...] = corner[...].astype(F32)
    eliminate(work, inverse)
    high, mid = split(inverse[...])
    high_out[...] = high
    mid_out[...] = mid


def second_factor(x0h, x0m, corner01, corner11, tiles0, tiles1, x1h_out, x1m_out, u01_out, rows_out, work, inverse):
    n_row = lax.axis_size("row")
    my_row = lax.axis_index("row")
    u01 = (mm(x0h[...], corner01[...]) + mm(x0m[...], corner01[...])).astype(BF16)
    u01_out[...] = u01
    work[...] = corner11[...].astype(F32) - mm(u01.T, u01)
    eliminate(work, inverse)
    high, mid = split(inverse[...])
    x1h_out[...] = high
    x1m_out[...] = mid
    size = high.shape[0]
    for slot in range(tiles0.shape[0]):
        row0 = (mmt(tiles0[slot], x0h[...]) + mmt(tiles0[slot], x0m[...])).astype(BF16)
        th, tm = split(tiles1[slot].astype(F32) - mm(row0, u01))
        row1 = mmt(th, high) + mmt(th, mid) + mmt(tm, high)
        row1 = jnp.where(slot * n_row + my_row >= 1, row1, 0.0)
        rows_out[slot, :, :size] = row0
        rows_out[slot, :, size:] = row1.astype(BF16)


def vmem_call(body, outs, scratch, name, flops):
    return pl.pallas_call(
        body,
        out_shape=outs,
        scratch_shapes=scratch,
        name=name,
        compiler_params=pltpu.CompilerParams(vmem_limit_bytes=24 << 20),
        cost_estimate=pl.CostEstimate(flops=flops, bytes_accessed=1 << 20, transcendentals=0),
    )


def update_chunk(chunk, sizes, hops, slabs, top, bottom, x0h, x0m, x1h, x1m, u01, rows, out):
    n_row = lax.axis_size("row")
    n_col = lax.axis_size("col")
    slots, cols, size, _ = slabs.shape
    width = sum(sizes)
    n_top, n_piece = len(top) // len(sizes), len(sizes)
    operands = [slabs, *top, *bottom, x0h, x0m, x1h, x1m, u01, rows]
    if out is not None:
        operands.append(out)
    n_wire = 1 + len(top) + len(bottom)
    halves = size // 128

    def body(*refs):
        slab_ref = refs[0]
        top_refs = refs[1 : 1 + len(top)]
        bottom_refs = refs[1 + len(top) : n_wire]
        x0h_ref, x0m_ref, x1h_ref, x1m_ref, u01_ref, rows_ref = refs[n_wire : n_wire + 6]
        out_ref, p0, p1, own, result, sems, out_sem = refs[len(operands) :]
        my_row = lax.axis_index("row")
        my_col = lax.axis_index("col")
        base = chunk * width
        own_copy = pltpu.make_async_copy(slab_ref.at[:, pl.ds(base, width)], own, sems.at[2])
        own_copy.start()

        def fetch(panel, target, sem, arrived):
            @pl.when(my_row == panel)
            def _():
                pltpu.make_async_copy(slab_ref.at[0, pl.ds(base, width)], target, sem).start()

            for way in range(n_top):
                here = 1 - panel if way == 0 else way + 1

                @pl.when(my_row == here)
                def _(way=way):
                    at = 0
                    for piece in range(n_piece):
                        pltpu.make_async_copy(
                            arrived[way * n_piece + piece], target.at[pl.ds(at, sizes[piece])], sem
                        ).start()
                        at += sizes[piece]

        fetch(0, p0, sems.at[0], top_refs)
        fetch(1, p1, sems.at[1], bottom_refs)
        pltpu.make_async_copy(slab_ref.at[0, pl.ds(base, width)], p0, sems.at[0]).wait()
        pltpu.make_async_copy(slab_ref.at[0, pl.ds(base, width)], p1, sems.at[1]).wait()
        own_copy.wait()
        for b in range(width):
            col_tile = (base + b) * n_col + my_col
            u0 = (mm(x0h_ref[...], p0[b]) + mm(x0m_ref[...], p0[b])).astype(BF16)
            th, tm = split(p1[b].astype(F32) - mm(u01_ref[...].T, u0))
            u1 = mm(x1h_ref[...], th) + mm(x1h_ref[...], tm) + mm(x1m_ref[...], th)
            u1 = jnp.where(col_tile >= 1, u1, 0.0).astype(BF16)
            both = jnp.concatenate([u0, u1], axis=0)
            for slot in range(slots):
                tile = own[slot, b].astype(F32) - mm(rows_ref[slot], both)
                keep = (slot * n_row + my_row >= 2) & (col_tile >= 2)
                tile = jnp.where(keep, tile, 0.0)
                for h in range(halves):
                    result[pl.ds(slot * size, size), b * halves + h, :] = tile[:, h * 128 : (h + 1) * 128]
        out_copy = pltpu.make_async_copy(result, out_ref.at[:, chunk], out_sem)
        out_copy.start()
        out_copy.wait()

    any_spec = pl.BlockSpec(memory_space=pl.ANY)
    vmem_spec = pl.BlockSpec(memory_space=pltpu.VMEM)
    specs = [any_spec] * n_wire + [vmem_spec] * 6 + ([any_spec] if out is not None else [])
    shape = (slots * size, cols // width, width * halves, 128)
    return pl.pallas_call(
        body,
        in_specs=specs,
        out_specs=any_spec,
        out_shape=jax.ShapeDtypeStruct(shape, F32),
        scratch_shapes=[
            pltpu.VMEM((width, size, size), BF16),
            pltpu.VMEM((width, size, size), BF16),
            pltpu.VMEM((slots, width, size, size), BF16),
            pltpu.VMEM((slots * size, width * halves, 128), F32),
            pltpu.SemaphoreType.DMA((3,)),
            pltpu.SemaphoreType.DMA,
        ],
        input_output_aliases={len(operands) - 1: 0} if out is not None else {},
        name="update",
        compiler_params=pltpu.CompilerParams(vmem_limit_bytes=24 << 20),
        cost_estimate=pl.CostEstimate(flops=2 * 10 * width * size**3, bytes_accessed=6 << 20, transcendentals=0),
    )(*operands)


def over_columns(x):
    n_col = lax.axis_size("col")
    my_col = lax.axis_index("col")
    step = 2
    while step < n_col:
        got = lax.ppermute(x, "col", [(i, i + step) for i in range(step) if i + step < n_col])
        x = jnp.where(my_col >= step, got, x)
        if 2 * step < n_col:
            pass
        step *= 2
    other = lax.ppermute(x, "col", [(i, i ^ 1) for i in range(n_col)])
    even = my_col % 2 == 0
    return jnp.where(even, x, other), jnp.where(even, other, x)


def local(gram):
    n_row = lax.axis_size("row")
    my_row = lax.axis_index("row")
    slots, _, size, cols, _, _ = gram.shape
    slabs = gram[:, 0, :, :, 0, :].transpose(0, 2, 1, 3)
    width = 4 if cols % 4 == 0 else cols
    chunks = [[width]] * (cols // width)
    chunks[0] = [1, width - 1]

    def up(x, source):
        return lax.ppermute(x, "row", [(source, source + 1)])

    pieces, at = [], 0
    for chunk in chunks:
        for count in chunk:
            pieces.append(slabs[0, at : at + count] if at else gram[0, 0, :, 0, 0, :][None])
            at += count
    swap = [lax.ppermute(p, "row", [(0, 1), (1, 0)]) for p in pieces]
    bottom_ways, top_ways = [swap], [swap]
    hop_b, hop_t = pieces, swap
    for source in range(1, n_row - 1):
        hop_b = [up(p, source) for p in hop_b]
        hop_t = [up(p, source) for p in hop_t]
        bottom_ways.append(hop_b)
        top_ways.append(hop_t)

    def here(panel, ways):
        x = pieces[0]
        for way, arrived in enumerate(ways):
            row = 1 - panel if way == 0 else way + 1
            x = jnp.where(my_row == row, arrived[0], x)
        return x[0]

    tiles0, tiles1 = over_columns(gram[:, 0, :, 0, 0, :])
    corner = jnp.stack([here(0, top_ways), here(1, bottom_ways)])
    corner0, corner1 = over_columns(corner)

    square = jax.ShapeDtypeStruct((size, size), BF16)
    scratch = [pltpu.VMEM((size, size), F32), pltpu.VMEM((size, size), F32)]
    x0h, x0m = vmem_call(first_factor, [square] * 2, scratch, "first", 1 << 30)(corner0[0])
    x1h, x1m, u01, rows = vmem_call(
        second_factor,
        [square] * 3 + [jax.ShapeDtypeStruct((slots, size, 2 * size), BF16)],
        scratch,
        "second",
        1 << 30,
    )(x0h, x0m, corner1[0], corner1[1], tiles0, tiles1)

    out, at = None, 0
    for chunk, sizes in enumerate(chunks):
        stop = at + len(sizes)
        top = [p for way in top_ways for p in way[at:stop]]
        bottom = [p for way in bottom_ways for p in way[at:stop]]
        out = update_chunk(chunk, sizes, n_row, slabs, top, bottom, x0h, x0m, x1h, x1m, u01, rows, out)
        at = stop
    return out.reshape(slots, 1, size, cols, 1, size)


def solution(mesh):
    spec = P(None, "row", None, None, "col", None)
    return jax.shard_map(local, mesh=mesh, in_specs=(spec,), out_specs=spec, check_vma=False)
```

time: 618 us -> 163 us (0.26); the launches traced: 607 us -> 161 us
  waiting for transfers between devices: 380 us -> 48.6 us
  other arithmetic: 130 us -> 7.32 us
  Pallas kernels: 0 us -> 48.7 us
  starting transfers between devices: 0.62 us -> 43.5 us
  local copies, waits for them, and re-layouts: 53.2 us -> 11.7 us
  matrix products: 26.8 us -> 0 us
  between operations: 16.5 us -> 0.75 us
    psum x6 -> x0, waiting for transfers between devices: 380 us -> none  [from_root(): return lax.psum(block, axis)]
    another operation x20 -> x1, other arithmetic: 111 us -> 0.03 us  [local(): corner = jnp.stack([here(0, top_ways), here(1, bottom_ways)])]
    pallas_call x0 -> x6, Pallas kernels: none -> 48.7 us  [the longest x4 24 us: update_chunk(): pl.pallas_call(body, in_specs=specs, out_specs=any_spec, out_shape=jax.Sh...]
    ppermute x0 -> x31, waiting for transfers between devices: none -> 48.6 us  [the longest x20 41 us: up(): return lax.ppermute(x, 'row', [(source, source + 1)])]
    ppermute x0 -> x31, starting transfers between devices: none -> 43.5 us  [the longest x20 26.6 us: up(): return lax.ppermute(x, 'row', [(source, source + 1)])]
    select_n x1 -> x0, local copies, waits for them, and re-layouts: 20.5 us -> none  [local(): result = jnp.where(retain, blocks, 0.0)]
    another operation x10 -> x0, matrix products: 19.2 us -> none  [the longest x6 18.3 us: local(): jax.scipy.linalg.solve_triangular(triangle, panel_rows.reshape(tile_size,...]
    another operation x21 -> x0, local copies, waits for them, and re-layouts: 15.2 us -> none  [the longest x17 15.2 us: local(): jax.scipy.linalg.solve_triangular(triangle, panel_rows.reshape(tile_size,...]
  transfers between devices with their start and end apart: 6 -> 31, of which waited for: 6 -> 10; matrix products, arithmetic and copies ran while one was open for 1% -> 9% of each run, Pallas kernels for 0% -> 26%
where the time goes in v1:
time: 163 us; the launch traced here: 161 us
  Pallas kernels  48.7 us (30%)
  waiting for transfers between devices  48.6 us (30%)
  starting transfers between devices  43.5 us (27%)
  local copies, waits for them, and re-layouts  11.7 us (7%)
  other arithmetic  7.32 us (4%)
    ppermute x20, waiting for transfers between devices, up(): return lax.ppermute(x, 'row', [(source, source + 1)])  41 us
    ppermute x20, starting transfers between devices, up(): return lax.ppermute(x, 'row', [(source, source + 1)])  26.6 us
    pallas_call x4, Pallas kernels, update_chunk(): pl.pallas_call(body, in_specs=specs, out_specs=any_spec, out_shape=jax.Sh...  24 us
    ppermute x4, starting transfers between devices, over_columns(): lax.ppermute(x, 'col', [(i, i + step) for i in range(step) if i + step <...  13.6 us
    pallas_call x1, Pallas kernels, local(): vmem_call(second_factor, [square] * 3 + [jax.ShapeDtypeStruct((slots, siz...  12.9 us
    pallas_call x1, Pallas kernels, local(): vmem_call(first_factor, [square] * 2, scratch, 'first', 1 << 30)(corner0[0])  11.8 us
    ppermute x4, waiting for transfers between devices, over_columns(): lax.ppermute(x, 'col', [(i, i + step) for i in range(step) if i + step <...  7.51 us
    unnamed x17, local copies, waits for them, and re-layouts  6.51 us
  transfers between devices with their start and end apart: 31, of which 10 were waited for; matrix products, arithmetic and copies ran while one was open for 9% of the time, Pallas kernels for 26%

profile of v1, /device:TPU:16, one launch (start us, length us, event | category | flops | bytes accessed | tf_op | source)
XLA Modules:
  0.0 160.6 jit_solution(15762618176996541790)
XLA Ops:
  0.0 1.4 slice.28
  2.1 1.3 collective-permute-start.8
  3.4 3.7 %copy.18 = bf16[2,1,256,16,1,256]{5,2,3,0,4,1:T(8,128)(2,1)S(1)} copy(bf16[2,1,256,16,1,256]{5,3,4,2,1,0:T(8,128)(2,1)} %param.1) | data formatting | bytes 8388608 | tf_op args[0]
  7.1 1.3 collective-permute-start.6
  9.9 1.3 collective-permute-start.29
  11.2 1.6 %collective-permute-start.9 = (bf16[1,256,256]{2,1,0:T(8,128)(2,1)S(1)}, bf16[1,256,256]{2,1,0:T(8,128)(2,1)S(1)}, u32[]{:S(2)}, u32[]{:S(2)}) collective-permute-start(bf16[1,256,256]{2,1,0:T(8,128)(2,1)S(1)} %collective-permute-done.8.refs_9_), channel_id=1, source_target_pairs={{16,24},{17,25},{18,26},{19,27},{20,28},{21,29},{22,30},{23,31}} | collective-permute-start | bytes 393224 | tf_op jit(solution)/shard_map/ppermute | solution.py:243
  12.8 1.4 collective-permute-done.6.refs_3_
  14.2 1.3 collective-permute-start.7
  15.5 1.2 slice_bitcast_fusion
  16.7 2.0 %copy-done = bf16[2,1,256,16,1,256]{5,2,3,0,4,1:T(8,128)(2,1)} copy-done((bf16[2,1,256,16,1,256]{5,2,3,0,4,1:T(8,128)(2,1)}, bf16[2,1,256,16,1,256]{5,2,3,0,4,1:T(8,128)(2,1)S(1)}, u32[]{:S(2)}) %copy-start) | copy-done | bytes 4194328
  19.4 1.9 %slice.32 = bf16[2,1,256,1,1,256]{5,3,4,2,1,0:T(2,128)(2,1)S(1)} slice(bf16[2,1,256,16,1,256]{5,3,4,2,1,0:T(8,128)(2,1)} %param.1), slice={[0:2], [0:1], [0:256], [0:1], [0:1], [0:256]} | slice | bytes 524288 | tf_op jit(solution)/shard_map/slice | solution.py:266
  21.3 1.3 collective-permute-start.24
  22.7 3.4 %collective-permute-start.13 = (bf16[2,256,256]{2,1,0:T(8,128)(2,1)S(1)}, bf16[2,256,256]{2,1,0:T(8,128)(2,1)S(1)}, u32[]{:S(2)}, u32[]{:S(2)}) collective-permute-start(bf16[2,256,256]{2,1,0:T(8,128)(2,1)S(1)} %bitcast.36), channel_id=1, source_target_pairs={{0,2},{1,3},{8,10},{9,11},{16,18},{17,19},{24,26},{25,27}} | collective-permute-start | bytes 786440 | tf_op jit(solution)/shard_map/ppermute | solution.py:223
  26.2 4.5 %collective-permute-done.13 = bf16[2,256,256]{2,1,0:T(8,128)(2,1)S(1)} collective-permute-done((bf16[2,256,256]{2,1,0:T(8,128)(2,1)S(1)}, bf16[2,256,256]{2,1,0:T(8,128)(2,1)S(1)}, u32[]{:S(2)}, u32[]{:S(2)}) %collective-permute-start.13) | collective-permute-done | bytes 262176 | tf_op jit(solution)/shard_map/ppermute | solution.py:223
  31.4 4.4 %collective-permute-start.10 = (bf16[2,256,256]{2,1,0:T(8,128)(2,1)S(1)}, bf16[2,256,256]{2,1,0:T(8,128)(2,1)S(1)}, u32[]{:S(2)}, u32[]{:S(2)}) collective-permute-start(bf16[2,256,256]{2,1,0:T(8,128)(2,1)S(1)} %pad_maximum_fusion), channel_id=1, source_target_pairs={{0,2},{1,3},{8,10},{9,11},{16,18},{17,19},{24,26},{25,27}} | collective-permute-start | bytes 786440 | tf_op jit(solution)/shard_map/ppermute | solution.py:223
  35.9 1.3 collective-permute-start.14
  37.2 2.5 %collective-permute-done.10 = bf16[2,256,256]{2,1,0:T(8,128)(2,1)S(1)} collective-permute-done((bf16[2,256,256]{2,1,0:T(8,128)(2,1)S(1)}, bf16[2,256,256]{2,1,0:T(8,128)(2,1)S(1)}, u32[]{:S(2)}, u32[]{:S(2)}) %collective-permute-start.10) | collective-permute-done | bytes 262176 | tf_op jit(solution)/shard_map/ppermute | solution.py:223
  39.7 1.3 collective-permute-start.19
  43.1 1.3 collective-permute-start.3
  44.5 4.4 %collective-permute-start.11 = (bf16[2,256,256]{2,1,0:T(8,128)(2,1)}, bf16[2,256,256]{2,1,0:T(8,128)(2,1)}, u32[]{:S(2)}, u32[]{:S(2)}) collective-permute-start(bf16[2,256,256]{2,1,0:T(8,128)(2,1)} %broadcast_select_fusion.1), channel_id=1, source_target_pairs={{0,4},{1,5},{2,6},{3,7},{8,12},{9,13},{10,14},{11,15},{16,20},{17,... | collective-permute-start | bytes 786440 | tf_op jit(solution)/shard_map/ppermute | solution.py:223
  48.9 1.3 collective-permute-start.27
  50.2 1.7 %broadcast_select_fusion.2 = bf16[2,256,256]{2,1,0:T(8,128)(2,1)} fusion(bf16[2,256,256]{2,1,0:T(8,128)(2,1)} %copy-done.6, bf16[2,256,256]{2,1,0:T(8,128)(2,1)} %copy-done.5, pred[]{:T(512)S(6)} %ge.8), kind=kLoop, calls=%fused_computation.9 | loop fusion | flops 131072 | bytes 786433 | tf_op jit(solution)/shard_map/jit(_where)/select_n | solution.py:224
  52.4 1.7 %broadcast_select_fusion.3 = bf16[2,256,256]{2,1,0:T(8,128)(2,1)} fusion(bf16[2,256,256]{2,1,0:T(8,128)(2,1)} %collective-permute-done.11, pred[]{:T(512)S(6)} %ge.8, bf16[2,256,256]{2,1,0:T(8,128)(2,1)} %copy-done.4, bf16[1,256,256]{2,1,0:T(8,128)(2,1)} %copy-done.3, bf16[1,256,256]{2,1,0:T(8,128)(2,1)} %copy-done.2, pred[]{:T(512)S(6)} %ge.9), kind=kLoop, calls=%fused_computation.10 | loop fusion | flops 393216 | bytes 1048578 | tf_op jit(solution)/shard_map/jit(_where)/select_n | solution.py:224
  54.1 5.1 %collective-permute-done.19.refs_5_ = bf16[4,256,256]{2,1,0:T(8,128)(2,1)} collective-permute-done((bf16[4,256,256]{2,1,0:T(8,128)(2,1)}, bf16[4,256,256]{2,1,0:T(8,128)(2,1)}, u32[]{:S(2)}, u32[]{:S(2)}) %collective-permute-start.19) | collective-permute-done | bytes 524320 | tf_op jit(solution)/shard_map/ppermute | solution.py:243
  59.2 1.6 collective-permute-start.30
  60.8 9.6 %collective-permute-done.3.refs_5_ = bf16[4,256,256]{2,1,0:T(8,128)(2,1)} collective-permute-done((bf16[4,256,256]{2,1,0:T(8,128)(2,1)}, bf16[4,256,256]{2,1,0:T(8,128)(2,1)}, u32[]{:S(2)}, u32[]{:S(2)}) %collective-permute-start.3) | collective-permute-done | bytes 524320 | tf_op jit(solution)/shard_map/ppermute | solution.py:243
  70.5 1.3 collective-permute-start.22
  71.8 1.3 collective-permute-start.25
  73.1 5.8 %collective-permute-done.27.refs_4_ = bf16[3,256,256]{2,1,0:T(8,128)(2,1)} collective-permute-done((bf16[3,256,256]{2,1,0:T(8,128)(2,1)S(1)}, bf16[3,256,256]{2,1,0:T(8,128)(2,1)}, u32[]{:S(2)}, u32[]{:S(2)}) %collective-permute-start.27) | collective-permute-done | bytes 393248 | tf_op jit(solution)/shard_map/ppermute | solution.py:243
  78.9 1.3 collective-permute-start.17
  80.2 1.1 broadcast_select_fusion.6
  81.2 1.3 collective-permute-start.1
  82.5 1.0 broadcast_select_fusion.5
  83.6 1.3 collective-permute-start.28
  84.9 5.1 %collective-permute-done.22.refs_2_ = bf16[4,256,256]{2,1,0:T(8,128)(2,1)S(1)} collective-permute-done((bf16[4,256,256]{2,1,0:T(8,128)(2,1)S(1)}, bf16[4,256,256]{2,1,0:T(8,128)(2,1)S(1)}, u32[]{:S(2)}, u32[]{:S(2)}) %collective-permute-start.22) | collective-permute-done | bytes 524320 | tf_op jit(solution)/shard_map/ppermute | solution.py:243
  90.0 1.3 collective-permute-start.20
  91.3 1.3 collective-permute-start.23
  92.7 8.6 %collective-permute-done.17.refs_2_ = bf16[4,256,256]{2,1,0:T(8,128)(2,1)S(1)} collective-permute-done((bf16[4,256,256]{2,1,0:T(8,128)(2,1)S(1)}, bf16[4,256,256]{2,1,0:T(8,128)(2,1)S(1)}, u32[]{:S(2)}, u32[]{:S(2)}) %collective-permute-start.17) | collective-permute-done | bytes 524320 | tf_op jit(solution)/shard_map/ppermute | solution.py:243
  101.2 1.3 collective-permute-start.18
  103.6 5.4 %collective-permute-done.1.refs_2_ = bf16[4,256,256]{2,1,0:T(8,128)(2,1)S(1)} collective-permute-done((bf16[4,256,256]{2,1,0:T(8,128)(2,1)S(1)}, bf16[4,256,256]{2,1,0:T(8,128)(2,1)S(1)}, u32[]{:S(2)}, u32[]{:S(2)}) %collective-permute-start.1) | collective-permute-done | bytes 524320 | tf_op jit(solution)/shard_map/ppermute | solution.py:243
  108.9 1.3 collective-permute-start.4
  110.3 1.3 collective-permute-start.2
  111.6 11.8 %first.1 = (bf16[256,256]{1,0:T(8,128)(2,1)S(1)}, bf16[256,256]{1,0:T(8,128)(2,1)S(1)}) custom-call(bf16[256,256]{1,0:T(8,128)(2,1)S(1)} %fusion.corner), custom_call_target="tpu_custom_call" | custom-call | flops 1073741824 | bytes 1048576 | tf_op jit(solution)/shard_map/first/pallas_call | solution.py:272
  123.4 12.9 %second.1 = (bf16[256,256]{1,0:T(8,128)(2,1)S(1)}, bf16[256,256]{1,0:T(8,128)(2,1)S(1)}, bf16[256,256]{1,0:T(8,128)(2,1)S(1)}, bf16[2,256,512]{2,1,0:T(8,128)(2,1)S(1)}) custom-call(bf16[256,256]{1,0:T(8,128)(2,1)S(1)} %get-tuple-element.11.x0h.refs_13_.refs_7_, bf16[256,256]{1,0:T(8,128)(2,1)S(1)} %get-tuple-element.12.x0m.refs_14_.refs_8_, ...), custom_call_target="tpu_custom_call" | custom-call | flops 1073741824 | bytes 1048576 | tf_op jit(solution)/shard_map/second/pallas_call | solution.py:273
  136.3 6.3 %update.4.refs_13_ = f32[512,4,8,128]{3,2,1,0:T(8,128)} custom-call(bf16[2,16,256,256]{3,2,1,0:T(8,128)(2,1)S(1)} %bitcast.32, bf16[1,256,256]{2,1,0:T(8,128)(2,1)S(1)} %collective-permute-done.5.refs_1_.refs_7_, bf16[3,256,256]{2,1,0:T(8,128)(2,1)S(1)} %collective-permute-done.26.refs_2_.refs_8_, bf16[1,256,256]{2,1,0:T(8,128)(2,1)S(1)} %collective-permute-done.6.refs_3_, ...), custom_call_target="tpu_custom_call" | custom-call | flops 1342177280 | bytes 6291456 | tf_op jit(solution)/shard_map/update/pallas_call | solution.py:198
  142.7 5.2 %update.5.refs_13_ = f32[512,4,8,128]{3,2,1,0:T(8,128)} custom-call(bf16[2,16,256,256]{3,2,1,0:T(8,128)(2,1)S(1)} %bitcast.33, bf16[4,256,256]{2,1,0:T(8,128)(2,1)S(1)} %collective-permute-done.21.refs_1_.refs_4_, bf16[4,256,256]{2,1,0:T(8,128)(2,1)S(1)} %collective-permute-done.22.refs_2_, ...), custom_call_target="tpu_custom_call", output_to_operand_aliasing={{}: (13, {})} | custom-call | flops 1342177280 | bytes 6291456 | tf_op jit(solution)/shard_map/update/pallas_call | solution.py:198
  147.9 6.2 %update.6.refs_13_ = f32[512,4,8,128]{3,2,1,0:T(8,128)} custom-call(bf16[2,16,256,256]{3,2,1,0:T(8,128)(2,1)S(1)} %bitcast.34, bf16[4,256,256]{2,1,0:T(8,128)(2,1)S(1)} %collective-permute-done.16.refs_1_.refs_4_, bf16[4,256,256]{2,1,0:T(8,128)(2,1)S(1)} %collective-permute-done.17.refs_2_, ...), custom_call_target="tpu_custom_call", output_to_operand_aliasing={{}: (13, {})} | custom-call | flops 1342177280 | bytes 6291456 | tf_op jit(solution)/shard_map/update/pallas_call | solution.py:198
  154.2 6.2 %update.7 = f32[512,4,8,128]{3,2,1,0:T(8,128)} custom-call(bf16[2,16,256,256]{3,2,1,0:T(8,128)(2,1)S(1)} %bitcast.35, bf16[4,256,256]{2,1,0:T(8,128)(2,1)S(1)} %collective-permute-done.refs_1_.refs_4_, bf16[4,256,256]{2,1,0:T(8,128)(2,1)S(1)} %collective-permute-done.1.refs_2_, ...), custom_call_target="tpu_custom_call", output_to_operand_aliasing={{}: (13, {})} | custom-call | flops 1342177280 | bytes 6291456 | tf_op jit(solution)/shard_map/update/pallas_call | solution.py:198
  (51 shorter events, 7.4 us)
Async XLA Ops:
  1.4 5.7 %collective-permute-start.5 = (bf16[1,256,256]{2,1,0:T(8,128)(2,1)S(1)}, bf16[1,256,256]{2,1,0:T(8,128)(2,1)S(1)}, u32[]{:S(2)}, u32[]{:S(2)}) collective-permute-start(bf16[1,256,256]{2,1,0:T(8,128)(2,1)S(1)} %bitcast.37), channel_id=1, source_target_pairs={{0,8},{8,0},{1,9},{9,1},{2,10},{10,2},{3,11},{11,3},{4,12},{12,4},... | collective-permute-start | bytes 393224 | tf_op jit(solution)/shard_map/ppermute | solution.py:250
  2.1 9.1 %collective-permute-start.8 = (bf16[1,256,256]{2,1,0:T(8,128)(2,1)S(1)}, bf16[1,256,256]{2,1,0:T(8,128)(2,1)S(1)}, u32[]{:S(2)}, u32[]{:S(2)}) collective-permute-start(bf16[1,256,256]{2,1,0:T(8,128)(2,1)S(1)} %bitcast.38), channel_id=1, source_target_pairs={{8,16},{9,17},{10,18},{11,19},{12,20},{13,21},{14,22},{15,23}} | collective-permute-start | bytes 393224 | tf_op jit(solution)/shard_map/ppermute | solution.py:243
  7.1 7.1 %collective-permute-start.6 = (bf16[1,256,256]{2,1,0:T(8,128)(2,1)S(1)}, bf16[1,256,256]{2,1,0:T(8,128)(2,1)S(1)}, u32[]{:S(2)}, u32[]{:S(2)}) collective-permute-start(bf16[1,256,256]{2,1,0:T(8,128)(2,1)S(1)} %collective-permute-done.5.refs_1_.refs_7_), channel_id=1, source_target_pairs={{8,16},{9,17},{10,18},{11,19},{12,20},{13,21},{14,22},{15,23}} | collective-permute-start | bytes 393224 | tf_op jit(solution)/shard_map/ppermute | solution.py:243
  9.2 22.2 %collective-permute-start.26 = (bf16[3,256,256]{2,1,0:T(8,128)(2,1)}, bf16[3,256,256]{2,1,0:T(8,128)(2,1)S(1)}, u32[]{:S(2)}, u32[]{:S(2)}) collective-permute-start(bf16[3,256,256]{2,1,0:T(8,128)(2,1)} %slice_bitcast_fusion.3), channel_id=1, source_target_pairs={{0,8},{8,0},{1,9},{9,1},{2,10},{10,2},{3,11},{11,3},{4,12},{12,4},... | collective-permute-start | bytes 1179656 | tf_op jit(solution)/shard_map/ppermute | solution.py:250
  9.9 26.0 %collective-permute-start.29 = (bf16[3,256,256]{2,1,0:T(8,128)(2,1)}, bf16[3,256,256]{2,1,0:T(8,128)(2,1)S(1)}, u32[]{:S(2)}, u32[]{:S(2)}) collective-permute-start(bf16[3,256,256]{2,1,0:T(8,128)(2,1)} %slice_bitcast_fusion.3), channel_id=1, source_target_pairs={{8,16},{9,17},{10,18},{11,19},{12,20},{13,21},{14,22},{15,23}} | collective-permute-start | bytes 1179656 | tf_op jit(solution)/shard_map/ppermute | solution.py:243
  11.2 10.2 %collective-permute-start.9 = (bf16[1,256,256]{2,1,0:T(8,128)(2,1)S(1)}, bf16[1,256,256]{2,1,0:T(8,128)(2,1)S(1)}, u32[]{:S(2)}, u32[]{:S(2)}) collective-permute-start(bf16[1,256,256]{2,1,0:T(8,128)(2,1)S(1)} %collective-permute-done.8.refs_9_), channel_id=1, source_target_pairs={{16,24},{17,25},{18,26},{19,27},{20,28},{21,29},{22,30},{23,31}} | collective-permute-start | bytes 393224 | tf_op jit(solution)/shard_map/ppermute | solution.py:243
  14.2 8.4 %collective-permute-start.7 = (bf16[1,256,256]{2,1,0:T(8,128)(2,1)S(1)}, bf16[1,256,256]{2,1,0:T(8,128)(2,1)S(1)}, u32[]{:S(2)}, u32[]{:S(2)}) collective-permute-start(bf16[1,256,256]{2,1,0:T(8,128)(2,1)S(1)} %collective-permute-done.6.refs_3_), channel_id=1, source_target_pairs={{16,24},{17,25},{18,26},{19,27},{20,28},{21,29},{22,30},{23,31}} | collective-permute-start | bytes 393224 | tf_op jit(solution)/shard_map/ppermute | solution.py:243
  16.7 2.0 %copy-start = (bf16[2,1,256,16,1,256]{5,2,3,0,4,1:T(8,128)(2,1)}, bf16[2,1,256,16,1,256]{5,2,3,0,4,1:T(8,128)(2,1)S(1)}, u32[]{:S(2)}) copy-start(bf16[2,1,256,16,1,256]{5,2,3,0,4,1:T(8,128)(2,1)S(1)} %copy.18) | copy-start | bytes 12582916
  18.7 24.4 %collective-permute-start.21 = (bf16[4,256,256]{2,1,0:T(8,128)(2,1)}, bf16[4,256,256]{2,1,0:T(8,128)(2,1)S(1)}, u32[]{:S(2)}, u32[]{:S(2)}) collective-permute-start(bf16[4,256,256]{2,1,0:T(8,128)(2,1)} %get-tuple-element.17), channel_id=1, source_target_pairs={{0,8},{8,0},{1,9},{9,1},{2,10},{10,2},{3,11},{11,3},{4,12},{12,4},... | collective-permute-start | bytes 1572872 | tf_op jit(solution)/shard_map/ppermute | solution.py:250
  21.3 23.1 %collective-permute-start.24 = (bf16[4,256,256]{2,1,0:T(8,128)(2,1)}, bf16[4,256,256]{2,1,0:T(8,128)(2,1)S(1)}, u32[]{:S(2)}, u32[]{:S(2)}) collective-permute-start(bf16[4,256,256]{2,1,0:T(8,128)(2,1)} %get-tuple-element.17), channel_id=1, source_target_pairs={{8,16},{9,17},{10,18},{11,19},{12,20},{13,21},{14,22},{15,23}} | collective-permute-start | bytes 1572872 | tf_op jit(solution)/shard_map/ppermute | solution.py:243
  22.7 8.1 %collective-permute-start.13 = (bf16[2,256,256]{2,1,0:T(8,128)(2,1)S(1)}, bf16[2,256,256]{2,1,0:T(8,128)(2,1)S(1)}, u32[]{:S(2)}, u32[]{:S(2)}) collective-permute-start(bf16[2,256,256]{2,1,0:T(8,128)(2,1)S(1)} %bitcast.36), channel_id=1, source_target_pairs={{0,2},{1,3},{8,10},{9,11},{16,18},{17,19},{24,26},{25,27}} | collective-permute-start | bytes 786440 | tf_op jit(solution)/shard_map/ppermute | solution.py:223
  26.1 18.3 %copy-start.2 = (bf16[1,256,256]{2,1,0:T(8,128)(2,1)}, bf16[1,256,256]{2,1,0:T(8,128)(2,1)S(1)}, u32[]{:S(2)}) copy-start(bf16[1,256,256]{2,1,0:T(8,128)(2,1)S(1)} %get-tuple-element.24) | copy-start | bytes 393220
  26.1 18.3 %copy-start.3 = (bf16[1,256,256]{2,1,0:T(8,128)(2,1)}, bf16[1,256,256]{2,1,0:T(8,128)(2,1)S(1)}, u32[]{:S(2)}) copy-start(bf16[1,256,256]{2,1,0:T(8,128)(2,1)S(1)} %get-tuple-element.25) | copy-start | bytes 393220
  30.7 18.2 %collective-permute-start.16 = (bf16[4,256,256]{2,1,0:T(8,128)(2,1)}, bf16[4,256,256]{2,1,0:T(8,128)(2,1)S(1)}, u32[]{:S(2)}, u32[]{:S(2)}) collective-permute-start(bf16[4,256,256]{2,1,0:T(8,128)(2,1)} %get-tuple-element.18), channel_id=1, source_target_pairs={{0,8},{8,0},{1,9},{9,1},{2,10},{10,2},{3,11},{11,3},{4,12},{12,4},... | collective-permute-start | bytes 1572872 | tf_op jit(solution)/shard_map/ppermute | solution.py:250
  31.4 8.3 %collective-permute-start.10 = (bf16[2,256,256]{2,1,0:T(8,128)(2,1)S(1)}, bf16[2,256,256]{2,1,0:T(8,128)(2,1)S(1)}, u32[]{:S(2)}, u32[]{:S(2)}) collective-permute-start(bf16[2,256,256]{2,1,0:T(8,128)(2,1)S(1)} %pad_maximum_fusion), channel_id=1, source_target_pairs={{0,2},{1,3},{8,10},{9,11},{16,18},{17,19},{24,26},{25,27}} | collective-permute-start | bytes 786440 | tf_op jit(solution)/shard_map/ppermute | solution.py:223
  35.9 8.6 %copy-start.5 = (bf16[2,256,256]{2,1,0:T(8,128)(2,1)}, bf16[2,256,256]{2,1,0:T(8,128)(2,1)S(1)}, u32[]{:S(2)}) copy-start(bf16[2,256,256]{2,1,0:T(8,128)(2,1)S(1)} %broadcast_select_fusion) | copy-start | bytes 786436
  35.9 5.8 %collective-permute-start.14 = (bf16[2,256,256]{2,1,0:T(8,128)(2,1)S(1)}, bf16[2,256,256]{2,1,0:T(8,128)(2,1)S(1)}, u32[]{:S(2)}, u32[]{:S(2)}) collective-permute-start(bf16[2,256,256]{2,1,0:T(8,128)(2,1)S(1)} %broadcast_select_fusion), channel_id=1, source_target_pairs={{0,4},{1,5},{2,6},{3,7},{8,12},{9,13},{10,14},{11,15},{16,20},{17,... | collective-permute-start | bytes 786440 | tf_op jit(solution)/shard_map/ppermute | solution.py:223
  39.7 4.8 %copy-start.4 = (bf16[2,256,256]{2,1,0:T(8,128)(2,1)}, bf16[2,256,256]{2,1,0:T(8,128)(2,1)S(1)}, u32[]{:S(2)}) copy-start(bf16[2,256,256]{2,1,0:T(8,128)(2,1)S(1)} %collective-permute-done.10) | copy-start | bytes 786436
  39.7 19.5 %collective-permute-start.19 = (bf16[4,256,256]{2,1,0:T(8,128)(2,1)}, bf16[4,256,256]{2,1,0:T(8,128)(2,1)}, u32[]{:S(2)}, u32[]{:S(2)}) collective-permute-start(bf16[4,256,256]{2,1,0:T(8,128)(2,1)} %get-tuple-element.18), channel_id=1, source_target_pairs={{8,16},{9,17},{10,18},{11,19},{12,20},{13,21},{14,22},{15,23}} | collective-permute-start | bytes 1572872 | tf_op jit(solution)/shard_map/ppermute | solution.py:243
  41.7 0.7 copy-start.6
  42.4 16.8 %collective-permute-start = (bf16[4,256,256]{2,1,0:T(8,128)(2,1)}, bf16[4,256,256]{2,1,0:T(8,128)(2,1)S(1)}, u32[]{:S(2)}, u32[]{:S(2)}) collective-permute-start(bf16[4,256,256]{2,1,0:T(8,128)(2,1)} %get-tuple-element.19), channel_id=1, source_target_pairs={{0,8},{8,0},{1,9},{9,1},{2,10},{10,2},{3,11},{11,3},{4,12},{12,4},... | collective-permute-start | bytes 1572872 | tf_op jit(solution)/shard_map/ppermute | solution.py:250
  43.1 27.3 %collective-permute-start.3 = (bf16[4,256,256]{2,1,0:T(8,128)(2,1)}, bf16[4,256,256]{2,1,0:T(8,128)(2,1)}, u32[]{:S(2)}, u32[]{:S(2)}) collective-permute-start(bf16[4,256,256]{2,1,0:T(8,128)(2,1)} %get-tuple-element.19), channel_id=1, source_target_pairs={{8,16},{9,17},{10,18},{11,19},{12,20},{13,21},{14,22},{15,23}} | collective-permute-start | bytes 1572872 | tf_op jit(solution)/shard_map/ppermute | solution.py:243
  44.5 7.9 %collective-permute-start.11 = (bf16[2,256,256]{2,1,0:T(8,128)(2,1)}, bf16[2,256,256]{2,1,0:T(8,128)(2,1)}, u32[]{:S(2)}, u32[]{:S(2)}) collective-permute-start(bf16[2,256,256]{2,1,0:T(8,128)(2,1)} %broadcast_select_fusion.1), channel_id=1, source_target_pairs={{0,4},{1,5},{2,6},{3,7},{8,12},{9,13},{10,14},{11,15},{16,20},{17,... | collective-permute-start | bytes 786440 | tf_op jit(solution)/shard_map/ppermute | solution.py:223
  48.9 29.9 %collective-permute-start.27 = (bf16[3,256,256]{2,1,0:T(8,128)(2,1)S(1)}, bf16[3,256,256]{2,1,0:T(8,128)(2,1)}, u32[]{:S(2)}, u32[]{:S(2)}) collective-permute-start(bf16[3,256,256]{2,1,0:T(8,128)(2,1)S(1)} %collective-permute-done.26.refs_2_.refs_8_), channel_id=1, source_target_pairs={{8,16},{9,17},{10,18},{11,19},{12,20},{13,21},{14,22},{15,23}} | collective-permute-start | bytes 1179656 | tf_op jit(solution)/shard_map/ppermute | solution.py:243
  52.4 19.3 %collective-permute-start.15 = (bf16[2,256,256]{2,1,0:T(8,128)(2,1)}, bf16[2,256,256]{2,1,0:T(8,128)(2,1)}, u32[]{:S(2)}, u32[]{:S(2)}) collective-permute-start(bf16[2,256,256]{2,1,0:T(8,128)(2,1)} %broadcast_select_fusion.2), channel_id=1, source_target_pairs={{0,1},{1,0},{2,3},{3,2},{4,5},{5,4},{6,7},{7,6},{8,9},{9,8},{10,11... | collective-permute-start | bytes 786440 | tf_op jit(solution)/shard_map/ppermute | solution.py:228
  59.2 22.0 %collective-permute-start.12 = (bf16[2,256,256]{2,1,0:T(8,128)(2,1)}, bf16[2,256,256]{2,1,0:T(8,128)(2,1)}, u32[]{:S(2)}, u32[]{:S(2)}) collective-permute-start(bf16[2,256,256]{2,1,0:T(8,128)(2,1)} %broadcast_select_fusion.3), channel_id=1, source_target_pairs={{0,1},{1,0},{2,3},{3,2},{4,5},{5,4},{6,7},{7,6},{8,9},{9,8},{10,11... | collective-permute-start | bytes 786440 | tf_op jit(solution)/shard_map/ppermute | solution.py:228
  59.2 77.1 %copy-start.1 = (bf16[2,1,256,16,1,256]{5,2,3,0,4,1:T(8,128)(2,1)S(1)}, bf16[2,1,256,16,1,256]{5,2,3,0,4,1:T(8,128)(2,1)}, u32[]{:S(2)}) copy-start(bf16[2,1,256,16,1,256]{5,2,3,0,4,1:T(8,128)(2,1)} %copy-done) | copy-start | bytes 12582916
  59.2 24.3 %collective-permute-start.30 = (bf16[3,256,256]{2,1,0:T(8,128)(2,1)S(1)}, bf16[3,256,256]{2,1,0:T(8,128)(2,1)S(1)}, u32[]{:S(2)}, u32[]{:S(2)}) collective-permute-start(bf16[3,256,256]{2,1,0:T(8,128)(2,1)S(1)} %collective-permute-done.29.refs_10_), channel_id=1, source_target_pairs={{16,24},{17,25},{18,26},{19,27},{20,28},{21,29},{22,30},{23,31}} | collective-permute-start | bytes 1179656 | tf_op jit(solution)/shard_map/ppermute | solution.py:243
  70.5 19.6 %collective-permute-start.22 = (bf16[4,256,256]{2,1,0:T(8,128)(2,1)S(1)}, bf16[4,256,256]{2,1,0:T(8,128)(2,1)S(1)}, u32[]{:S(2)}, u32[]{:S(2)}) collective-permute-start(bf16[4,256,256]{2,1,0:T(8,128)(2,1)S(1)} %collective-permute-done.21.refs_1_.refs_4_), channel_id=1, source_target_pairs={{8,16},{9,17},{10,18},{11,19},{12,20},{13,21},{14,22},{15,23}} | collective-permute-start | bytes 1572872 | tf_op jit(solution)/shard_map/ppermute | solution.py:243
  71.8 19.6 %collective-permute-start.25 = (bf16[4,256,256]{2,1,0:T(8,128)(2,1)S(1)}, bf16[4,256,256]{2,1,0:T(8,128)(2,1)S(1)}, u32[]{:S(2)}, u32[]{:S(2)}) collective-permute-start(bf16[4,256,256]{2,1,0:T(8,128)(2,1)S(1)} %collective-permute-done.24.refs_5_), channel_id=1, source_target_pairs={{16,24},{17,25},{18,26},{19,27},{20,28},{21,29},{22,30},{23,31}} | collective-permute-start | bytes 1572872 | tf_op jit(solution)/shard_map/ppermute | solution.py:243
  78.9 22.4 %collective-permute-start.17 = (bf16[4,256,256]{2,1,0:T(8,128)(2,1)S(1)}, bf16[4,256,256]{2,1,0:T(8,128)(2,1)S(1)}, u32[]{:S(2)}, u32[]{:S(2)}) collective-permute-start(bf16[4,256,256]{2,1,0:T(8,128)(2,1)S(1)} %collective-permute-done.16.refs_1_.refs_4_), channel_id=1, source_target_pairs={{8,16},{9,17},{10,18},{11,19},{12,20},{13,21},{14,22},{15,23}} | collective-permute-start | bytes 1572872 | tf_op jit(solution)/shard_map/ppermute | solution.py:243
  81.2 27.7 %collective-permute-start.1 = (bf16[4,256,256]{2,1,0:T(8,128)(2,1)S(1)}, bf16[4,256,256]{2,1,0:T(8,128)(2,1)S(1)}, u32[]{:S(2)}, u32[]{:S(2)}) collective-permute-start(bf16[4,256,256]{2,1,0:T(8,128)(2,1)S(1)} %collective-permute-done.refs_1_.refs_4_), channel_id=1, source_target_pairs={{8,16},{9,17},{10,18},{11,19},{12,20},{13,21},{14,22},{15,23}} | collective-permute-start | bytes 1572872 | tf_op jit(solution)/shard_map/ppermute | solution.py:243
  83.6 26.7 %collective-permute-start.28 = (bf16[3,256,256]{2,1,0:T(8,128)(2,1)}, bf16[3,256,256]{2,1,0:T(8,128)(2,1)S(1)}, u32[]{:S(2)}, u32[]{:S(2)}) collective-permute-start(bf16[3,256,256]{2,1,0:T(8,128)(2,1)} %collective-permute-done.27.refs_4_), channel_id=1, source_target_pairs={{16,24},{17,25},{18,26},{19,27},{20,28},{21,29},{22,30},{23,31}} | collective-permute-start | bytes 1179656 | tf_op jit(solution)/shard_map/ppermute | solution.py:243
  90.0 57.9 %collective-permute-start.20 = (bf16[4,256,256]{2,1,0:T(8,128)(2,1)}, bf16[4,256,256]{2,1,0:T(8,128)(2,1)S(1)}, u32[]{:S(2)}, u32[]{:S(2)}) collective-permute-start(bf16[4,256,256]{2,1,0:T(8,128)(2,1)} %collective-permute-done.19.refs_5_), channel_id=1, source_target_pairs={{16,24},{17,25},{18,26},{19,27},{20,28},{21,29},{22,30},{23,31}} | collective-permute-start | bytes 1572872 | tf_op jit(solution)/shard_map/ppermute | solution.py:243
  91.3 51.3 %collective-permute-start.23 = (bf16[4,256,256]{2,1,0:T(8,128)(2,1)S(1)}, bf16[4,256,256]{2,1,0:T(8,128)(2,1)S(1)}, u32[]{:S(2)}, u32[]{:S(2)}) collective-permute-start(bf16[4,256,256]{2,1,0:T(8,128)(2,1)S(1)} %collective-permute-done.22.refs_2_), channel_id=1, source_target_pairs={{16,24},{17,25},{18,26},{19,27},{20,28},{21,29},{22,30},{23,31}} | collective-permute-start | bytes 1572872 | tf_op jit(solution)/shard_map/ppermute | solution.py:243
  101.2 46.7 %collective-permute-start.18 = (bf16[4,256,256]{2,1,0:T(8,128)(2,1)S(1)}, bf16[4,256,256]{2,1,0:T(8,128)(2,1)S(1)}, u32[]{:S(2)}, u32[]{:S(2)}) collective-permute-start(bf16[4,256,256]{2,1,0:T(8,128)(2,1)S(1)} %collective-permute-done.17.refs_2_), channel_id=1, source_target_pairs={{16,24},{17,25},{18,26},{19,27},{20,28},{21,29},{22,30},{23,31}} | collective-permute-start | bytes 1572872 | tf_op jit(solution)/shard_map/ppermute | solution.py:243
  108.9 45.2 %collective-permute-start.4 = (bf16[4,256,256]{2,1,0:T(8,128)(2,1)}, bf16[4,256,256]{2,1,0:T(8,128)(2,1)S(1)}, u32[]{:S(2)}, u32[]{:S(2)}) collective-permute-start(bf16[4,256,256]{2,1,0:T(8,128)(2,1)} %collective-permute-done.3.refs_5_), channel_id=1, source_target_pairs={{16,24},{17,25},{18,26},{19,27},{20,28},{21,29},{22,30},{23,31}} | collective-permute-start | bytes 1572872 | tf_op jit(solution)/shard_map/ppermute | solution.py:243
  110.3 43.9 %collective-permute-start.2 = (bf16[4,256,256]{2,1,0:T(8,128)(2,1)S(1)}, bf16[4,256,256]{2,1,0:T(8,128)(2,1)S(1)}, u32[]{:S(2)}, u32[]{:S(2)}) collective-permute-start(bf16[4,256,256]{2,1,0:T(8,128)(2,1)S(1)} %collective-permute-done.1.refs_2_), channel_id=1, source_target_pairs={{16,24},{17,25},{18,26},{19,27},{20,28},{21,29},{22,30},{23,31}} | collective-permute-start | bytes 1572872 | tf_op jit(solution)/shard_map/ppermute | solution.py:243

commit v2 on v1

v2 whole, which is shorter than its diff:
```python
import jax
import jax.numpy as jnp
from jax import lax
from jax.experimental import pallas as pl
from jax.experimental.pallas import tpu as pltpu
from jax.sharding import PartitionSpec as P

F32 = jnp.float32
BF16 = jnp.bfloat16
HIGHEST = lax.Precision.HIGHEST
NB = 64


def lane(x, j):
    return jnp.broadcast_to(x[:, j : j + 1], x.shape)


def sublane(x, j):
    return jnp.broadcast_to(x[j : j + 1, :], x.shape)


def inverse_factor(block):
    diagonal = lax.broadcasted_iota(jnp.int32, (NB, NB), 0) == lax.broadcasted_iota(jnp.int32, (NB, NB), 1)
    wide = jnp.concatenate([block, diagonal.astype(F32)], axis=1)
    groups = NB // 8
    sub = lax.broadcasted_iota(jnp.int32, (8, 2 * NB), 0)

    def group(g, tiles):
        pivot = tiles[0]
        cols = [lane(pivot, j) for j in range(8)]
        upper, recips, rows, scale = {}, [], [], None
        for j in range(8):
            d = sublane(cols[j], j)
            recips.append(1.0 / d)
            factor = jnp.where(sub > j, cols[j] * recips[j], 0.0)
            for l in range(j + 1, 8):
                upper[j, l] = sublane(cols[l], j)
                cols[l] = cols[l] - factor * upper[j, l]
            rows.append(sublane(pivot, j))
            pivot = pivot - factor * rows[j]
            root = lax.rsqrt(d)
            scale = root if scale is None else jnp.where(sub >= j, root, scale)
        out = []
        for i in range(1, groups):
            live = i < groups - g
            tile = tiles[i]
            own = [lane(tile, j) for j in range(8)]
            for j in range(8):
                factor = own[j] * recips[j]
                for l in range(j + 1, 8):
                    own[l] = own[l] - factor * upper[j, l]
                tile = tile - jnp.where(live, factor, 0.0) * rows[j]
            out.append(tile)
        out.append(pivot * scale)
        return tuple(pltpu.roll(t, 2 * NB - 8, 1) for t in out)

    tiles = tuple(wide[8 * i : 8 * i + 8] for i in range(groups))
    tiles = lax.fori_loop(0, groups, group, tiles)
    return jnp.concatenate(tiles, axis=0)[:, :NB]


def eliminate(work, inverse):
    size = work.shape[0]
    inverse[...] = (
        lax.broadcasted_iota(jnp.int32, (size, size), 0) == lax.broadcasted_iota(jnp.int32, (size, size), 1)
    ).astype(F32)
    for j in range(size // NB):
        lo, hi = j * NB, (j + 1) * NB
        own = inverse_factor(work[lo:hi, lo:hi])
        right = jnp.dot(own, work[lo:hi, :], precision=HIGHEST, preferred_element_type=F32)
        left = jnp.dot(own, inverse[lo:hi, :], precision=HIGHEST, preferred_element_type=F32)
        inverse[lo:hi, :] = left
        if hi < size:
            down = right[:, hi:].T
            work[hi:, :] -= jnp.dot(down, right, precision=HIGHEST, preferred_element_type=F32)
            inverse[hi:, :] -= jnp.dot(down, left, precision=HIGHEST, preferred_element_type=F32)


def split(x):
    high = x.astype(BF16)
    return high, (x - high.astype(F32)).astype(BF16)


def mm(a, b):
    return jnp.dot(a, b, preferred_element_type=F32)


def mmt(a, b):
    return lax.dot_general(a, b, (((1,), (1,)), ((), ())), preferred_element_type=F32)


def from_column(column, mine, other, k):
    even = lax.axis_index("col") % 2 == column
    return jnp.where(even, mine[k].astype(F32), other[k].astype(F32))


def first_factor(mine, other, high_out, mid_out, work, inverse):
    work[...] = from_column(0, mine, other, 0)
    eliminate(work, inverse)
    high, mid = split(inverse[...])
    high_out[...] = high
    mid_out[...] = mid


def second_factor(x0h, x0m, mine, other, high_out, mid_out, u01_out, work, inverse):
    corner01 = from_column(1, mine, other, 0).astype(BF16)
    u01 = (mm(x0h[...], corner01) + mm(x0m[...], corner01)).astype(BF16)
    u01_out[...] = u01
    work[...] = from_column(1, mine, other, 1) - mm(u01.T, u01)
    eliminate(work, inverse)
    high, mid = split(inverse[...])
    high_out[...] = high
    mid_out[...] = mid


def row_factor(x0h, x0m, x1h, x1m, u01, mine, other, out):
    n_row = lax.axis_size("row")
    my_row = lax.axis_index("row")
    slots, size, _ = out.shape
    for slot in range(slots):
        tile0 = from_column(0, mine, other, slot).astype(BF16)
        row0 = (mmt(tile0, x0h[...]) + mmt(tile0, x0m[...])).astype(BF16)
        th, tm = split(from_column(1, mine, other, slot) - mm(row0, u01[...]))
        row1 = mmt(th, x1h[...]) + mmt(th, x1m[...]) + mmt(tm, x1h[...])
        row1 = jnp.where(slot * n_row + my_row >= 1, row1, 0.0)
        out[slot, :, :size] = row0
        out[slot, :, size:] = row1.astype(BF16)


def vmem_call(body, outs, scratch, name):
    return pl.pallas_call(
        body,
        out_shape=outs,
        scratch_shapes=scratch,
        name=name,
        compiler_params=pltpu.CompilerParams(vmem_limit_bytes=24 << 20),
        cost_estimate=pl.CostEstimate(flops=0, bytes_accessed=0, transcendentals=0),
    )


def update_chunk(base, width, slab0, slab1, top, bottom, x0h, x0m, x1h, x1m, u01, rows, out):
    n_row = lax.axis_size("row")
    n_col = lax.axis_size("col")
    cols, size, _ = slab0.shape
    slots = 1 + len(slab1)
    halves = size // 128
    wires = []
    for _, array, _, _ in top + bottom:
        if not any(array is w for w in wires):
            wires.append(array)

    def place(array):
        return next(i for i, w in enumerate(wires) if w is array)

    fetches = [
        [(row, place(array), first, count) for row, array, first, count in ways] for ways in (top, bottom)
    ]
    n_any = 1 + len(slab1) + len(wires)
    operands = [slab0, *slab1, *wires, x0h, x0m, x1h, x1m, u01, rows]
    if out is not None:
        operands.append(out)

    def body(*refs):
        slab_refs = refs[:slots]
        wire_refs = refs[slots:n_any]
        x0h_ref, x0m_ref, x1h_ref, x1m_ref, u01_ref, rows_ref = refs[n_any : n_any + 6]
        out_ref, p0, p1, own, result, sems, out_sem = refs[len(operands) :]
        my_row = lax.axis_index("row")
        my_col = lax.axis_index("col")
        for slot in range(slots):
            pltpu.make_async_copy(slab_refs[slot].at[pl.ds(base, width)], own.at[slot], sems.at[2 + slot]).start()
        for panel, target in enumerate((p0, p1)):

            @pl.when(my_row == panel)
            def _(panel=panel, target=target):
                pltpu.make_async_copy(slab_refs[0].at[pl.ds(base, width)], target, sems.at[panel]).start()

            for row in range(n_row):
                parts = [f[1:] for f in fetches[panel] if f[0] == row]
                if not parts:
                    continue

                @pl.when(my_row == row)
                def _(panel=panel, target=target, parts=parts):
                    at = 0
                    for wire, first, count in parts:
                        pltpu.make_async_copy(
                            wire_refs[wire].at[pl.ds(first, count)], target.at[pl.ds(at, count)], sems.at[panel]
                        ).start()
                        at += count

        for panel, target in enumerate((p0, p1)):
            pltpu.make_async_copy(slab_refs[0].at[pl.ds(base, width)], target, sems.at[panel]).wait()
        for slot in range(slots):
            pltpu.make_async_copy(slab_refs[slot].at[pl.ds(base, width)], own.at[slot], sems.at[2 + slot]).wait()
        for b in range(width):
            col_tile = (base + b) * n_col + my_col
            u0 = (mm(x0h_ref[...], p0[b]) + mm(x0m_ref[...], p0[b])).astype(BF16)
            th, tm = split(p1[b].astype(F32) - mm(u01_ref[...].T, u0))
            u1 = mm(x1h_ref[...], th) + mm(x1h_ref[...], tm) + mm(x1m_ref[...], th)
            u1 = jnp.where(col_tile >= 1, u1, 0.0).astype(BF16)
            both = jnp.concatenate([u0, u1], axis=0)
            for slot in range(slots):
                tile = own[slot, b].astype(F32) - mm(rows_ref[slot], both)
                keep = (slot * n_row + my_row >= 2) & (col_tile >= 2)
                tile = jnp.where(keep, tile, 0.0)
                for h in range(halves):
                    result[b, pl.ds(slot * size, size), h, :] = tile[:, h * 128 : (h + 1) * 128]
            pltpu.make_async_copy(result.at[b], out_ref.at[:, base + b], out_sem.at[b]).start()
        for b in range(width):
            pltpu.make_async_copy(result.at[b], out_ref.at[:, base + b], out_sem.at[b]).wait()

    any_spec = pl.BlockSpec(memory_space=pl.ANY)
    vmem_spec = pl.BlockSpec(memory_space=pltpu.VMEM)
    return pl.pallas_call(
        body,
        in_specs=[any_spec] * n_any + [vmem_spec] * 6 + ([any_spec] if out is not None else []),
        out_specs=any_spec,
        out_shape=jax.ShapeDtypeStruct((slots * size, cols, halves, 128), F32),
        scratch_shapes=[
            pltpu.VMEM((width, size, size), BF16),
            pltpu.VMEM((width, size, size), BF16),
            pltpu.VMEM((slots, width, size, size), BF16),
            pltpu.VMEM((width, slots * size, halves, 128), F32),
            pltpu.SemaphoreType.DMA((2 + slots,)),
            pltpu.SemaphoreType.DMA((width,)),
        ],
        input_output_aliases={len(operands) - 1: 0} if out is not None else {},
        name="update",
        compiler_params=pltpu.CompilerParams(vmem_limit_bytes=24 << 20),
        cost_estimate=pl.CostEstimate(flops=0, bytes_accessed=0, transcendentals=0),
    )(*operands)


def over_columns(name, tokens, x):
    n_col = lax.axis_size("col")
    my_col = lax.axis_index("col")
    tokens = list(tokens)
    step = 2
    while step < n_col:
        x = after(x, *(tokens.pop(0) if tokens else []))
        with jax.named_scope(f"{name}{step}"):
            got = lax.ppermute(x, "col", [(i, i + step) for i in range(step) if i + step < n_col])
        x = jnp.where(my_col >= step, got, x)
        step *= 2
    x = after(x, *(tokens.pop(0) if tokens else []))
    with jax.named_scope(f"{name}1"):
        return x, lax.ppermute(x, "col", [(i, i ^ 1) for i in range(n_col)])


def after(x, *tokens):
    return lax.optimization_barrier((x, *tokens))[0]


def local(gram):
    n_row = lax.axis_size("row")
    my_row = lax.axis_index("row")
    slots, _, size, cols, _, _ = gram.shape
    slab0 = gram[0, 0, :, :, 0, :].transpose(1, 0, 2)
    if cols % 8 == 0:
        first_counts = [1, cols // 2 - 1, cols // 2]
        second_counts = [1, 3] + [4] * (cols // 4 - 2) + [2, 2]
        widths = [4] * (cols // 4 - 1) + [2, 2]
    else:
        first_counts = second_counts = [1] * cols
        widths = [cols]

    def spans(counts):
        starts = [sum(counts[:i]) for i in range(len(counts))]
        return list(zip(starts, counts))

    corner_piece = gram[0, 0, :, 0, 0, :][None]
    cut = {(0, 1): corner_piece}
    for start, count in spans(first_counts) + spans(second_counts):
        if (start, count) not in cut:
            cut[start, count] = slab0[start : start + count]

    def send(name, x, *pairs):
        with jax.named_scope(name):
            return lax.ppermute(x, "row", [p for p in pairs])

    far_spans, near_spans = spans(first_counts), spans(second_counts)
    tile_rows = gram[:, 0, :, 0, 0, :]
    far = {s: send(f"far{s[0]}", cut[s], (0, 3), (1, 0)) for s in far_spans}
    near = {s: send(f"near{s[0]}", cut[s], (1, 2), (0, 1)) for s in near_spans[:2]}
    ready = [cut[s] for s in far_spans + near_spans[:2]]
    cross = send("cross", corner_piece, (0, 2), (1, 3))
    back = {}

    def tokens(i):
        return [d[s] for s in far_spans[i : i + 1] for d in (far, back) if s in d]

    top_ways = {1: near, 3: far, 2: {(0, 1): cross}}
    bottom_ways = {0: far, 2: near, 3: {(0, 1): cross}}
    hop_top, hop_bottom = {(0, 1): far[0, 1]}, {(0, 1): cross}
    for row in range(4, n_row):
        hop_top = {s: send(f"top{s[0]}", x, (row - 1, row)) for s, x in hop_top.items()}
        hop_bottom = {s: send(f"bottom{s[0]}", x, (row - 1, row)) for s, x in hop_bottom.items()}
        top_ways[row], bottom_ways[row] = hop_top, hop_bottom

    def here(ways):
        x = corner_piece
        for row, arrived in ways.items():
            x = jnp.where(my_row == row, arrived[0, 1], x)
        return x

    payload = jnp.concatenate([here(top_ways), here(bottom_ways)])
    corners = over_columns("corner", [], after(payload, tile_rows, *ready))

    square = jax.ShapeDtypeStruct((size, size), BF16)
    scratch = [pltpu.VMEM((size, size), F32), pltpu.VMEM((size, size), F32)]
    x0h, x0m = vmem_call(first_factor, [square] * 2, scratch, "first")(*corners)
    x1h, x1m, u01 = vmem_call(second_factor, [square] * 3, scratch, "second")(
        after(x0h, *tokens(1)), x0m, *corners
    )
    for i, s in enumerate(near_spans[2:]):
        gate = [x0h] if i < 2 else [x1h, near[near_spans[i - 1]]]
        near[s] = send(f"near{s[0]}", after(cut[s], *gate), (1, 2), (0, 1))
    back[0, 1] = cross
    for i, s in enumerate(far_spans[1:]):
        back[s] = send(f"back{s[0]}", after(far[s], x1h if i else x0h), (3, 2))
    on = {(0, 1): cross}
    for s in near_spans[1:3]:
        on[s] = send(f"on{s[0]}", after(near[s], x1h), (2, 3))
    tiles = over_columns("tiles", [[corners[0]], [], [x0h]], tile_rows)
    panels = jax.ShapeDtypeStruct((slots, size, 2 * size), BF16)
    rows = vmem_call(row_factor, panels, [], "rows")(after(x0h, on[near_spans[1]], *[back[s] for s in far_spans[1:2]], *[near[s] for s in near_spans[2:3]]), x0m, x1h, x1m, u01, *tiles)
    for s in near_spans[3:]:
        on[s] = send(f"on{s[0]}", after(near[s], rows), (2, 3))
    slab1 = [after(gram, x1h)[a, 0, :, :, 0, :].transpose(1, 0, 2) for a in range(1, slots)]

    top_ways, bottom_ways = {1: near, 3: far, 2: back}, {0: far, 2: near, 3: on}
    hop_top, hop_bottom = far, on
    for row in range(4, n_row):
        hop_top = {s: send(f"top{s[0]}", x, (row - 1, row)) for s, x in hop_top.items()}
        hop_bottom = {s: send(f"bottom{s[0]}", x, (row - 1, row)) for s, x in hop_bottom.items()}
        top_ways[row], bottom_ways[row] = hop_top, hop_bottom

    def parts(ways, base, width):
        out = []
        for row, arrived in ways.items():
            for (start, count), array in sorted(arrived.items(), key=lambda item: item[0]):
                lo, hi = max(start, base), min(start + count, base + width)
                if lo < hi:
                    out.append((row, array, lo - start, hi - lo))
        return out

    out = None
    for base, width in spans(widths):
        top, bottom = parts(top_ways, base, width), parts(bottom_ways, base, width)
        out = update_chunk(base, width, slab0, slab1, top, bottom, x0h, x0m, x1h, x1m, u01, rows, out)
    return out.reshape(slots, 1, size, cols, 1, size)


def solution(mesh):
    spec = P(None, "row", None, None, "col", None)
    return jax.shard_map(local, mesh=mesh, in_specs=(spec,), out_specs=spec, check_vma=False)
```

time: 163 us -> 138 us (0.85); the launches traced: 161 us -> 138 us
  starting transfers between devices: 43.5 us -> 32.3 us
  other arithmetic: 7.32 us -> 2.82 us
  local copies, waits for them, and re-layouts: 11.7 us -> 7.85 us
  Pallas kernels: 48.7 us -> 46.1 us
    ppermute x27 -> x19, starting transfers between devices: 30 us -> 21.2 us  [the longest x17 21.1 us: send(): return lax.ppermute(x, 'row', [p for p in pairs])]
    unnamed x17 -> x7, local copies, waits for them, and re-layouts: 6.51 us -> 1.48 us
    pallas_call x6 -> x8, Pallas kernels: 48.7 us -> 46.1 us  [the longest x5 21.1 us: update_chunk(): pl.pallas_call(body, in_specs=[any_spec] * n_any + [vmem_spec] * 6 + ([an...]
    ppermute x4, starting transfers between devices: 13.6 us -> 11.1 us  [over_columns(): lax.ppermute(x, 'col', [(i, i + step) for i in range(step) if i + step <...]
    select_n x3 -> x1, other arithmetic: 2.11 us -> 0.04 us  [here(): x = jnp.where(my_row == row, arrived[0, 1], x)]
    squeeze x3 -> x0, local copies, waits for them, and re-layouts: 1.98 us -> none  [the longest x2 1.96 us: local(): slabs[0, at:at + count]]
    slice x2 -> x9, local copies, waits for them, and re-layouts: 3.23 us -> 4.7 us  [the longest x5 2.91 us: local(): cut[start, count] = slab0[start:start + count]]
    ppermute x27 -> x19, waiting for transfers between devices: 41 us -> 40.1 us  [the longest x17 40.1 us: send(): return lax.ppermute(x, 'row', [p for p in pairs])]
  transfers between devices with their start and end apart: 31 -> 23, of which waited for: 10 -> 10; matrix products, arithmetic and copies ran while one was open for 9% -> 7% of each run, Pallas kernels for 26% -> 31%
where the time goes in v2:
time: 138 us
  waiting for transfers between devices  48.2 us (35%)
  Pallas kernels  46.1 us (33%)
  starting transfers between devices  32.3 us (23%)
  local copies, waits for them, and re-layouts  7.85 us (6%)
  other arithmetic  2.82 us (2%)
    ppermute x17, waiting for transfers between devices, send(): return lax.ppermute(x, 'row', [p for p in pairs])  40.1 us
    ppermute x17, starting transfers between devices, send(): return lax.ppermute(x, 'row', [p for p in pairs])  21.1 us
    pallas_call x5, Pallas kernels, update_chunk(): pl.pallas_call(body, in_specs=[any_spec] * n_any + [vmem_spec] * 6 + ([an...  21.1 us
    pallas_call x1, Pallas kernels, local(): vmem_call(second_factor, [square] * 3, scratch, 'second')  12.2 us
    pallas_call x1, Pallas kernels, local(): x0h, x0m = vmem_call(first_factor, [square] * 2, scratch, 'first')(*corners)  11.8 us
    ppermute x4, starting transfers between devices, over_columns(): lax.ppermute(x, 'col', [(i, i + step) for i in range(step) if i + step <...  11.1 us
    ppermute x4, waiting for transfers between devices, over_columns(): lax.ppermute(x, 'col', [(i, i + step) for i in range(step) if i + step <...  8.16 us
    slice x5, local copies, waits for them, and re-layouts, local(): cut[start, count] = slab0[start:start + count]  2.91 us
  transfers between devices with their start and end apart: 23, of which 10 were waited for; matrix products, arithmetic and copies ran while one was open for 7% of the time, Pallas kernels for 31%

profile of v2, /device:TPU:16, one launch (start us, length us, event | category | flops | bytes accessed | tf_op | source)
XLA Modules:
  0.0 137.9 jit_solution(12087802125006060311)
XLA Ops:
  0.0 1.5 %slice.34 = bf16[1,1,256,1,1,256]{5,3,4,2,1,0:T(2,128)(2,1)S(1)} slice(bf16[2,1,256,16,1,256]{5,3,4,2,1,0:T(8,128)(2,1)} %param.1), slice={[0:1], [0:1], [0:256], [0:1], [0:1], [0:256]} | slice | bytes 262144 | tf_op jit(solution)/shard_map/slice | solution.py:272
  1.5 1.3 collective-permute-start
  3.5 1.3 collective-permute-start.2
  4.8 0.7 copy.19
  5.6 1.0 slice.45
  6.6 1.0 slice.44
  7.6 0.8 slice.46
  8.7 0.7 copy.20
  9.4 0.8 collective-permute-done.refs_6_
  10.2 7.8 %collective-permute-done.2.refs_2_ = bf16[1,256,256]{2,1,0:T(8,128)(2,1)S(1)} collective-permute-done((bf16[1,256,256]{2,1,0:T(8,128)(2,1)S(1)}, bf16[1,256,256]{2,1,0:T(8,128)(2,1)S(1)}, u32[]{:S(2)}, u32[]{:S(2)}) %collective-permute-start.2) | collective-permute-done | bytes 131104 | tf_op jit(solution)/shard_map/near0/ppermute | solution.py:280
  18.1 3.4 %collective-permute-start.3 = (bf16[2,256,256]{2,1,0:T(8,128)(2,1)S(1)}, bf16[2,256,256]{2,1,0:T(8,128)(2,1)S(1)}, u32[]{:S(2)}, u32[]{:S(2)}) collective-permute-start(bf16[2,256,256]{2,1,0:T(8,128)(2,1)S(1)} %pad_maximum_fusion), channel_id=1, source_target_pairs={{0,2},{1,3},{8,10},{9,11},{16,18},{17,19},{24,26},{25,27}} | collective-permute-start | bytes 786440 | tf_op jit(solution)/shard_map/corner2/ppermute | solution.py:243
  21.5 1.6 %collective-permute-start.6 = (bf16[7,256,256]{2,1,0:T(8,128)(2,1)}, bf16[7,256,256]{2,1,0:T(8,128)(2,1)}, u32[]{:S(2)}, u32[]{:S(2)}) collective-permute-start(bf16[7,256,256]{2,1,0:T(8,128)(2,1)} %slice.44), channel_id=1, source_target_pairs={{0,24},{8,0},{1,25},{9,1},{2,26},{10,2},{3,27},{11,3},{4,28},{12,4... | collective-permute-start | bytes 2752520 | tf_op jit(solution)/shard_map/far1/ppermute | solution.py:280
  23.1 4.1 %collective-permute-done.3 = bf16[2,256,256]{2,1,0:T(8,128)(2,1)S(1)} collective-permute-done((bf16[2,256,256]{2,1,0:T(8,128)(2,1)S(1)}, bf16[2,256,256]{2,1,0:T(8,128)(2,1)S(1)}, u32[]{:S(2)}, u32[]{:S(2)}) %collective-permute-start.3) | collective-permute-done | bytes 262176 | tf_op jit(solution)/shard_map/corner2/ppermute | solution.py:243
  27.2 0.7 broadcast_select_fusion.1
  28.0 2.0 %collective-permute-start.4 = (bf16[2,256,256]{2,1,0:T(8,128)(2,1)}, bf16[2,256,256]{2,1,0:T(8,128)(2,1)}, u32[]{:S(2)}, u32[]{:S(2)}) collective-permute-start(bf16[2,256,256]{2,1,0:T(8,128)(2,1)} %broadcast_select_fusion.1), channel_id=1, source_target_pairs={{0,4},{1,5},{2,6},{3,7},{8,12},{9,13},{10,14},{11,15},{16,20},{17,... | collective-permute-start | bytes 786440 | tf_op jit(solution)/shard_map/corner4/ppermute | solution.py:243
  29.9 0.7 collective-permute-start.9
  30.7 4.0 %collective-permute-done.4 = bf16[2,256,256]{2,1,0:T(8,128)(2,1)} collective-permute-done((bf16[2,256,256]{2,1,0:T(8,128)(2,1)}, bf16[2,256,256]{2,1,0:T(8,128)(2,1)}, u32[]{:S(2)}, u32[]{:S(2)}) %collective-permute-start.4) | collective-permute-done | bytes 262176 | tf_op jit(solution)/shard_map/corner4/ppermute | solution.py:243
  34.7 1.0 broadcast_select_fusion.3.mine
  35.8 4.4 %collective-permute-start.14 = (bf16[2,256,256]{2,1,0:T(8,128)(2,1)}, bf16[2,256,256]{2,1,0:T(8,128)(2,1)S(1)}, u32[]{:S(2)}, u32[]{:S(2)}) collective-permute-start(bf16[2,256,256]{2,1,0:T(8,128)(2,1)} %bitcast.28), channel_id=1, source_target_pairs={{0,2},{1,3},{8,10},{9,11},{16,18},{17,19},{24,26},{25,27}} | collective-permute-start | bytes 786440 | tf_op jit(solution)/shard_map/tiles2/ppermute | solution.py:243
  40.2 1.3 collective-permute-start.11
  41.5 11.8 %first.1 = (bf16[256,256]{1,0:T(8,128)(2,1)S(1)}, bf16[256,256]{1,0:T(8,128)(2,1)S(1)}) custom-call(bf16[2,256,256]{2,1,0:T(8,128)(2,1)S(1)} %broadcast_select_fusion.3.mine, bf16[2,256,256]{2,1,0:T(8,128)(2,1)S(1)} %collective-permute-done.5.other), custom_call_target="tpu_custom_call" | custom-call | tf_op jit(solution)/shard_map/first/pallas_call | solution.py:312
  53.3 1.3 collective-permute-start.13
  54.6 1.0 broadcast_select_fusion
  55.6 1.3 collective-permute-start.15
  56.9 12.2 %second.1 = (bf16[256,256]{1,0:T(8,128)(2,1)S(1)}, bf16[256,256]{1,0:T(8,128)(2,1)S(1)}, bf16[256,256]{1,0:T(8,128)(2,1)S(1)}) custom-call(bf16[256,256]{1,0:T(8,128)(2,1)S(1)} %get-tuple-element.38.x0h.refs_9_.refs_6_, bf16[256,256]{1,0:T(8,128)(2,1)S(1)} %get-tuple-element.30.x0m.refs_10_.refs_7_, bf16[2,256,256]{2,1,0:T(8,128)(2,1)S(1)} %broadcast_select_fusion.3.mine, ...), custom_call_target="tpu_custom_call" | custom-call | tf_op jit(solution)/shard_map/second/pallas_call | solution.py:313
  69.2 6.3 %collective-permute-done.11.refs_3_ = bf16[3,256,256]{2,1,0:T(8,128)(2,1)S(1)} collective-permute-done((bf16[3,256,256]{2,1,0:T(8,128)(2,1)}, bf16[3,256,256]{2,1,0:T(8,128)(2,1)S(1)}, u32[]{:S(2)}, u32[]{:S(2)}) %collective-permute-start.11) | collective-permute-done | bytes 393248 | tf_op jit(solution)/shard_map/near1/ppermute | solution.py:280
  75.5 1.3 collective-permute-start.12
  76.9 1.3 collective-permute-start.7
  78.2 1.3 collective-permute-start.20
  79.5 1.3 collective-permute-start.10
  80.8 4.8 %collective-permute-done.12.refs_8_ = bf16[3,256,256]{2,1,0:T(8,128)(2,1)S(1)} collective-permute-done((bf16[3,256,256]{2,1,0:T(8,128)(2,1)S(1)}, bf16[3,256,256]{2,1,0:T(8,128)(2,1)S(1)}, u32[]{:S(2)}, u32[]{:S(2)}) %collective-permute-start.12) | collective-permute-done | bytes 393248 | tf_op jit(solution)/shard_map/on1/ppermute | solution.py:280
  85.7 7.9 %collective-permute-done.7.refs_2_ = bf16[4,256,256]{2,1,0:T(8,128)(2,1)S(1)} collective-permute-done((bf16[4,256,256]{2,1,0:T(8,128)(2,1)S(1)}, bf16[4,256,256]{2,1,0:T(8,128)(2,1)S(1)}, u32[]{:S(2)}, u32[]{:S(2)}) %collective-permute-start.7) | collective-permute-done | bytes 524320 | tf_op jit(solution)/shard_map/near4/ppermute | solution.py:280
  93.6 1.3 collective-permute-start.18
  94.9 1.3 collective-permute-start.8
  96.2 1.3 collective-permute-start.22
  97.5 1.0 rows.1.refs_14_.refs_11_
  98.5 6.3 %collective-permute-done.20.refs_2_ = bf16[4,256,256]{2,1,0:T(8,128)(2,1)S(1)} collective-permute-done((bf16[4,256,256]{2,1,0:T(8,128)(2,1)S(1)}, bf16[4,256,256]{2,1,0:T(8,128)(2,1)S(1)}, u32[]{:S(2)}, u32[]{:S(2)}) %collective-permute-start.20) | collective-permute-done | bytes 524320 | tf_op jit(solution)/shard_map/near8/ppermute | solution.py:280
  104.8 1.3 collective-permute-start.21
  106.1 1.5 %copy.9 = bf16[2,1,256,16,1,256]{5,2,3,4,1,0:T(8,128)(2,1)S(1)} copy(bf16[2,1,256,16,1,256]{5,3,4,2,1,0:T(8,128)(2,1)S(1)} %copy-done.1) | data formatting | bytes 8388608 | tf_op jit(solution)/shard_map/optimization_barrier | solution.py:252
  107.7 2.8 %collective-permute-done.18.refs_2_ = bf16[2,256,256]{2,1,0:T(8,128)(2,1)S(1)} collective-permute-done((bf16[2,256,256]{2,1,0:T(8,128)(2,1)S(1)}, bf16[2,256,256]{2,1,0:T(8,128)(2,1)S(1)}, u32[]{:S(2)}, u32[]{:S(2)}) %collective-permute-start.18) | collective-permute-done | bytes 262176 | tf_op jit(solution)/shard_map/near12/ppermute | solution.py:280
  110.4 1.3 collective-permute-start.19
  111.7 3.4 %collective-permute-done.8.refs_2_ = bf16[2,256,256]{2,1,0:T(8,128)(2,1)S(1)} collective-permute-done((bf16[2,256,256]{2,1,0:T(8,128)(2,1)S(1)}, bf16[2,256,256]{2,1,0:T(8,128)(2,1)S(1)}, u32[]{:S(2)}, u32[]{:S(2)}) %collective-permute-start.8) | collective-permute-done | bytes 262176 | tf_op jit(solution)/shard_map/near14/ppermute | solution.py:280
  115.1 1.3 collective-permute-start.17
  116.6 5.6 %update.5.refs_12_ = f32[512,16,2,128]{3,2,1,0:T(2,128)} custom-call(bf16[16,256,256]{2,1,0:T(8,128)(2,1)S(1)} %bitcast.23, bf16[16,256,256]{2,1,0:T(8,128)(2,1)S(1)} %slice_bitcast_fusion.refs_1_, bf16[1,256,256]{2,1,0:T(8,128)(2,1)S(1)} %collective-permute-done.2.refs_2_, bf16[3,256,256]{2,1,0:T(8,128)(2,1)S(1)} %collective-permute-done.11.refs_3_, ...), custom_call_target="tpu_custom_call" | custom-call | tf_op jit(solution)/shard_map/update/pallas_call | solution.py:215
  122.2 4.7 %update.6.refs_12_ = f32[512,16,2,128]{3,2,1,0:T(2,128)} custom-call(bf16[16,256,256]{2,1,0:T(8,128)(2,1)S(1)} %bitcast.24, bf16[16,256,256]{2,1,0:T(8,128)(2,1)S(1)} %slice_bitcast_fusion.refs_1_, bf16[4,256,256]{2,1,0:T(8,128)(2,1)S(1)} %collective-permute-done.7.refs_2_, ...), custom_call_target="tpu_custom_call", output_to_operand_aliasing={{}: (12, {})} | custom-call | tf_op jit(solution)/shard_map/update/pallas_call | solution.py:215
  126.9 4.8 %update.7.refs_12_ = f32[512,16,2,128]{3,2,1,0:T(2,128)} custom-call(bf16[16,256,256]{2,1,0:T(8,128)(2,1)S(1)} %bitcast.25, bf16[16,256,256]{2,1,0:T(8,128)(2,1)S(1)} %slice_bitcast_fusion.refs_1_, bf16[4,256,256]{2,1,0:T(8,128)(2,1)S(1)} %collective-permute-done.20.refs_2_, ...), custom_call_target="tpu_custom_call", output_to_operand_aliasing={{}: (12, {})} | custom-call | tf_op jit(solution)/shard_map/update/pallas_call | solution.py:215
  131.7 3.0 %update.8.refs_12_ = f32[512,16,2,128]{3,2,1,0:T(2,128)} custom-call(bf16[16,256,256]{2,1,0:T(8,128)(2,1)S(1)} %bitcast.26, bf16[16,256,256]{2,1,0:T(8,128)(2,1)S(1)} %slice_bitcast_fusion.refs_1_, bf16[2,256,256]{2,1,0:T(8,128)(2,1)S(1)} %collective-permute-done.18.refs_2_, ...), custom_call_target="tpu_custom_call", output_to_operand_aliasing={{}: (12, {})} | custom-call | tf_op jit(solution)/shard_map/update/pallas_call | solution.py:215
  134.7 3.0 %update.9 = f32[512,16,2,128]{3,2,1,0:T(2,128)} custom-call(bf16[16,256,256]{2,1,0:T(8,128)(2,1)S(1)} %bitcast.27, bf16[16,256,256]{2,1,0:T(8,128)(2,1)S(1)} %slice_bitcast_fusion.refs_1_, bf16[2,256,256]{2,1,0:T(8,128)(2,1)S(1)} %collective-permute-done.8.refs_2_, ...), custom_call_target="tpu_custom_call", output_to_operand_aliasing={{}: (12, {})} | custom-call | tf_op jit(solution)/shard_map/update/pallas_call | solution.py:215
  (30 shorter events, 1.4 us)
Async XLA Ops:
  0.0 4.8 %slice-start = ((bf16[2,1,256,16,1,256]{5,3,4,2,1,0:T(8,128)(2,1)}), bf16[1,1,256,16,1,256]{5,3,4,2,1,0:T(8,128)(2,1)S(1)}, s32[]{:S(2)}) async-start(bf16[2,1,256,16,1,256]{5,3,4,2,1,0:T(8,128)(2,1)} %param.1), calls=%async_computation | async-start | bytes 4194304 | tf_op jit(solution)/shard_map/slice | solution.py:259
  1.5 8.6 %collective-permute-start = (bf16[1,256,256]{2,1,0:T(8,128)(2,1)S(1)}, bf16[1,256,256]{2,1,0:T(8,128)(2,1)S(1)}, u32[]{:S(2)}, u32[]{:S(2)}) collective-permute-start(bf16[1,256,256]{2,1,0:T(8,128)(2,1)S(1)} %bitcast.30), channel_id=1, source_target_pairs={{0,16},{8,24},{1,17},{9,25},{2,18},{10,26},{3,19},{11,27},{4,20},{... | collective-permute-start | bytes 393224 | tf_op jit(solution)/shard_map/cross/ppermute | solution.py:280
  2.8 7.3 %collective-permute-start.1 = (bf16[1,256,256]{2,1,0:T(8,128)(2,1)S(1)}, bf16[1,256,256]{2,1,0:T(8,128)(2,1)S(1)}, u32[]{:S(2)}, u32[]{:S(2)}) collective-permute-start(bf16[1,256,256]{2,1,0:T(8,128)(2,1)S(1)} %bitcast.31), channel_id=1, source_target_pairs={{0,24},{8,0},{1,25},{9,1},{2,26},{10,2},{3,27},{11,3},{4,28},{12,4... | collective-permute-start | bytes 393224 | tf_op jit(solution)/shard_map/far0/ppermute | solution.py:280
  3.5 14.5 %collective-permute-start.2 = (bf16[1,256,256]{2,1,0:T(8,128)(2,1)S(1)}, bf16[1,256,256]{2,1,0:T(8,128)(2,1)S(1)}, u32[]{:S(2)}, u32[]{:S(2)}) collective-permute-start(bf16[1,256,256]{2,1,0:T(8,128)(2,1)S(1)} %bitcast.32), channel_id=1, source_target_pairs={{8,16},{0,8},{9,17},{1,9},{10,18},{2,10},{11,19},{3,11},{12,20},{4... | collective-permute-start | bytes 393224 | tf_op jit(solution)/shard_map/near0/ppermute | solution.py:280
  4.8 3.5 %copy-start = (bf16[2,1,256,16,1,256]{5,3,4,2,1,0:T(8,128)(2,1)S(1)}, bf16[2,1,256,16,1,256]{5,3,4,2,1,0:T(8,128)(2,1)}, u32[]{:S(2)}) copy-start(bf16[2,1,256,16,1,256]{5,3,4,2,1,0:T(8,128)(2,1)} %param.1) | copy-start | bytes 12582916
  18.1 9.1 %collective-permute-start.3 = (bf16[2,256,256]{2,1,0:T(8,128)(2,1)S(1)}, bf16[2,256,256]{2,1,0:T(8,128)(2,1)S(1)}, u32[]{:S(2)}, u32[]{:S(2)}) collective-permute-start(bf16[2,256,256]{2,1,0:T(8,128)(2,1)S(1)} %pad_maximum_fusion), channel_id=1, source_target_pairs={{0,2},{1,3},{8,10},{9,11},{16,18},{17,19},{24,26},{25,27}} | collective-permute-start | bytes 786440 | tf_op jit(solution)/shard_map/corner2/ppermute | solution.py:243
  21.5 31.8 %collective-permute-start.6 = (bf16[7,256,256]{2,1,0:T(8,128)(2,1)}, bf16[7,256,256]{2,1,0:T(8,128)(2,1)}, u32[]{:S(2)}, u32[]{:S(2)}) collective-permute-start(bf16[7,256,256]{2,1,0:T(8,128)(2,1)} %slice.44), channel_id=1, source_target_pairs={{0,24},{8,0},{1,25},{9,1},{2,26},{10,2},{3,27},{11,3},{4,28},{12,4... | collective-permute-start | bytes 2752520 | tf_op jit(solution)/shard_map/far1/ppermute | solution.py:280
  28.0 6.8 %collective-permute-start.4 = (bf16[2,256,256]{2,1,0:T(8,128)(2,1)}, bf16[2,256,256]{2,1,0:T(8,128)(2,1)}, u32[]{:S(2)}, u32[]{:S(2)}) collective-permute-start(bf16[2,256,256]{2,1,0:T(8,128)(2,1)} %broadcast_select_fusion.1), channel_id=1, source_target_pairs={{0,4},{1,5},{2,6},{3,7},{8,12},{9,13},{10,14},{11,15},{16,20},{17,... | collective-permute-start | bytes 786440 | tf_op jit(solution)/shard_map/corner4/ppermute | solution.py:243
  29.9 48.2 %collective-permute-start.9 = (bf16[8,256,256]{2,1,0:T(8,128)(2,1)}, bf16[8,256,256]{2,1,0:T(8,128)(2,1)S(1)}, u32[]{:S(2)}, u32[]{:S(2)}) collective-permute-start(bf16[8,256,256]{2,1,0:T(8,128)(2,1)} %slice.45), channel_id=1, source_target_pairs={{0,24},{8,0},{1,25},{9,1},{2,26},{10,2},{3,27},{11,3},{4,28},{12,4... | collective-permute-start | bytes 3145736 | tf_op jit(solution)/shard_map/far8/ppermute | solution.py:280
  30.7 75.4 %copy-start.1 = (bf16[2,1,256,16,1,256]{5,3,4,2,1,0:T(8,128)(2,1)S(1)}, bf16[2,1,256,16,1,256]{5,3,4,2,1,0:T(8,128)(2,1)}, u32[]{:S(2)}) copy-start(bf16[2,1,256,16,1,256]{5,3,4,2,1,0:T(8,128)(2,1)} %param.1) | copy-start | bytes 12582916
  35.7 5.8 %collective-permute-start.5 = (bf16[2,256,256]{2,1,0:T(8,128)(2,1)S(1)}, bf16[2,256,256]{2,1,0:T(8,128)(2,1)S(1)}, u32[]{:S(2)}, u32[]{:S(2)}) collective-permute-start(bf16[2,256,256]{2,1,0:T(8,128)(2,1)S(1)} %broadcast_select_fusion.3.mine), channel_id=1, source_target_pairs={{0,1},{1,0},{2,3},{3,2},{4,5},{5,4},{6,7},{7,6},{8,9},{9,8},{10,11... | collective-permute-start | bytes 786440 | tf_op jit(solution)/shard_map/corner1/ppermute | solution.py:248
  35.8 18.8 %collective-permute-start.14 = (bf16[2,256,256]{2,1,0:T(8,128)(2,1)}, bf16[2,256,256]{2,1,0:T(8,128)(2,1)S(1)}, u32[]{:S(2)}, u32[]{:S(2)}) collective-permute-start(bf16[2,256,256]{2,1,0:T(8,128)(2,1)} %bitcast.28), channel_id=1, source_target_pairs={{0,2},{1,3},{8,10},{9,11},{16,18},{17,19},{24,26},{25,27}} | collective-permute-start | bytes 786440 | tf_op jit(solution)/shard_map/tiles2/ppermute | solution.py:243
  40.2 35.3 %collective-permute-start.11 = (bf16[3,256,256]{2,1,0:T(8,128)(2,1)}, bf16[3,256,256]{2,1,0:T(8,128)(2,1)S(1)}, u32[]{:S(2)}, u32[]{:S(2)}) collective-permute-start(bf16[3,256,256]{2,1,0:T(8,128)(2,1)} %slice.46), channel_id=1, source_target_pairs={{8,16},{0,8},{9,17},{1,9},{10,18},{2,10},{11,19},{3,11},{12,20},{4... | collective-permute-start | bytes 1179656 | tf_op jit(solution)/shard_map/near1/ppermute | solution.py:280
  53.3 41.5 %collective-permute-start.13 = (bf16[7,256,256]{2,1,0:T(8,128)(2,1)}, bf16[7,256,256]{2,1,0:T(8,128)(2,1)S(1)}, u32[]{:S(2)}, u32[]{:S(2)}) collective-permute-start(bf16[7,256,256]{2,1,0:T(8,128)(2,1)} %collective-permute-done.6.refs_5_.refs_3_), channel_id=1, source_target_pairs={{24,16},{25,17},{26,18},{27,19},{28,20},{29,21},{30,22},{31,23}} | collective-permute-start | bytes 2752520 | tf_op jit(solution)/shard_map/back1/ppermute | solution.py:280
  55.6 23.9 %collective-permute-start.15 = (bf16[2,256,256]{2,1,0:T(8,128)(2,1)S(1)}, bf16[2,256,256]{2,1,0:T(8,128)(2,1)S(1)}, u32[]{:S(2)}, u32[]{:S(2)}) collective-permute-start(bf16[2,256,256]{2,1,0:T(8,128)(2,1)S(1)} %broadcast_select_fusion), channel_id=1, source_target_pairs={{0,4},{1,5},{2,6},{3,7},{8,12},{9,13},{10,14},{11,15},{16,20},{17,... | collective-permute-start | bytes 786440 | tf_op jit(solution)/shard_map/tiles4/ppermute | solution.py:243
  75.5 10.1 %collective-permute-start.12 = (bf16[3,256,256]{2,1,0:T(8,128)(2,1)S(1)}, bf16[3,256,256]{2,1,0:T(8,128)(2,1)S(1)}, u32[]{:S(2)}, u32[]{:S(2)}) collective-permute-start(bf16[3,256,256]{2,1,0:T(8,128)(2,1)S(1)} %collective-permute-done.11.refs_3_), channel_id=1, source_target_pairs={{16,24},{17,25},{18,26},{19,27},{20,28},{21,29},{22,30},{23,31}} | collective-permute-start | bytes 1179656 | tf_op jit(solution)/shard_map/on1/ppermute | solution.py:280
  76.9 16.7 %collective-permute-start.7 = (bf16[4,256,256]{2,1,0:T(8,128)(2,1)S(1)}, bf16[4,256,256]{2,1,0:T(8,128)(2,1)S(1)}, u32[]{:S(2)}, u32[]{:S(2)}) collective-permute-start(bf16[4,256,256]{2,1,0:T(8,128)(2,1)S(1)} %get-tuple-element.33), channel_id=1, source_target_pairs={{8,16},{0,8},{9,17},{1,9},{10,18},{2,10},{11,19},{3,11},{12,20},{4... | collective-permute-start | bytes 1572872 | tf_op jit(solution)/shard_map/near4/ppermute | solution.py:280
  78.2 26.6 %collective-permute-start.20 = (bf16[4,256,256]{2,1,0:T(8,128)(2,1)S(1)}, bf16[4,256,256]{2,1,0:T(8,128)(2,1)S(1)}, u32[]{:S(2)}, u32[]{:S(2)}) collective-permute-start(bf16[4,256,256]{2,1,0:T(8,128)(2,1)S(1)} %get-tuple-element.46), channel_id=1, source_target_pairs={{8,16},{0,8},{9,17},{1,9},{10,18},{2,10},{11,19},{3,11},{12,20},{4... | collective-permute-start | bytes 1572872 | tf_op jit(solution)/shard_map/near8/ppermute | solution.py:280
  79.5 47.4 %collective-permute-start.10 = (bf16[8,256,256]{2,1,0:T(8,128)(2,1)S(1)}, bf16[8,256,256]{2,1,0:T(8,128)(2,1)S(1)}, u32[]{:S(2)}, u32[]{:S(2)}) collective-permute-start(bf16[8,256,256]{2,1,0:T(8,128)(2,1)S(1)} %collective-permute-done.9.refs_3_), channel_id=1, source_target_pairs={{24,16},{25,17},{26,18},{27,19},{28,20},{29,21},{30,22},{31,23}} | collective-permute-start | bytes 3145736 | tf_op jit(solution)/shard_map/back8/ppermute | solution.py:280
  85.6 10.5 %collective-permute-start.16 = (bf16[2,256,256]{2,1,0:T(8,128)(2,1)S(1)}, bf16[2,256,256]{2,1,0:T(8,128)(2,1)S(1)}, u32[]{:S(2)}, u32[]{:S(2)}) collective-permute-start(bf16[2,256,256]{2,1,0:T(8,128)(2,1)S(1)} %broadcast_select_fusion.2.mine), channel_id=1, source_target_pairs={{0,1},{1,0},{2,3},{3,2},{4,5},{5,4},{6,7},{7,6},{8,9},{9,8},{10,11... | collective-permute-start | bytes 786440 | tf_op jit(solution)/shard_map/tiles1/ppermute | solution.py:248
  93.6 16.9 %collective-permute-start.18 = (bf16[2,256,256]{2,1,0:T(8,128)(2,1)S(1)}, bf16[2,256,256]{2,1,0:T(8,128)(2,1)S(1)}, u32[]{:S(2)}, u32[]{:S(2)}) collective-permute-start(bf16[2,256,256]{2,1,0:T(8,128)(2,1)S(1)} %get-tuple-element.44), channel_id=1, source_target_pairs={{8,16},{0,8},{9,17},{1,9},{10,18},{2,10},{11,19},{3,11},{12,20},{4... | collective-permute-start | bytes 786440 | tf_op jit(solution)/shard_map/near12/ppermute | solution.py:280
  94.9 20.3 %collective-permute-start.8 = (bf16[2,256,256]{2,1,0:T(8,128)(2,1)S(1)}, bf16[2,256,256]{2,1,0:T(8,128)(2,1)S(1)}, u32[]{:S(2)}, u32[]{:S(2)}) collective-permute-start(bf16[2,256,256]{2,1,0:T(8,128)(2,1)S(1)} %get-tuple-element.34), channel_id=1, source_target_pairs={{8,16},{0,8},{9,17},{1,9},{10,18},{2,10},{11,19},{3,11},{12,20},{4... | collective-permute-start | bytes 786440 | tf_op jit(solution)/shard_map/near14/ppermute | solution.py:280
  96.2 26.0 %collective-permute-start.22 = (bf16[4,256,256]{2,1,0:T(8,128)(2,1)S(1)}, bf16[4,256,256]{2,1,0:T(8,128)(2,1)S(1)}, u32[]{:S(2)}, u32[]{:S(2)}) collective-permute-start(bf16[4,256,256]{2,1,0:T(8,128)(2,1)S(1)} %collective-permute-done.7.refs_2_), channel_id=1, source_target_pairs={{16,24},{17,25},{18,26},{19,27},{20,28},{21,29},{22,30},{23,31}} | collective-permute-start | bytes 1572872 | tf_op jit(solution)/shard_map/on4/ppermute | solution.py:280
  104.8 22.1 %collective-permute-start.21 = (bf16[4,256,256]{2,1,0:T(8,128)(2,1)S(1)}, bf16[4,256,256]{2,1,0:T(8,128)(2,1)S(1)}, u32[]{:S(2)}, u32[]{:S(2)}) collective-permute-start(bf16[4,256,256]{2,1,0:T(8,128)(2,1)S(1)} %collective-permute-done.20.refs_2_), channel_id=1, source_target_pairs={{16,24},{17,25},{18,26},{19,27},{20,28},{21,29},{22,30},{23,31}} | collective-permute-start | bytes 1572872 | tf_op jit(solution)/shard_map/on8/ppermute | solution.py:280
  110.4 21.3 %collective-permute-start.19 = (bf16[2,256,256]{2,1,0:T(8,128)(2,1)S(1)}, bf16[2,256,256]{2,1,0:T(8,128)(2,1)S(1)}, u32[]{:S(2)}, u32[]{:S(2)}) collective-permute-start(bf16[2,256,256]{2,1,0:T(8,128)(2,1)S(1)} %collective-permute-done.18.refs_2_), channel_id=1, source_target_pairs={{16,24},{17,25},{18,26},{19,27},{20,28},{21,29},{22,30},{23,31}} | collective-permute-start | bytes 786440 | tf_op jit(solution)/shard_map/on12/ppermute | solution.py:280
  115.1 19.6 %collective-permute-start.17 = (bf16[2,256,256]{2,1,0:T(8,128)(2,1)S(1)}, bf16[2,256,256]{2,1,0:T(8,128)(2,1)S(1)}, u32[]{:S(2)}, u32[]{:S(2)}) collective-permute-start(bf16[2,256,256]{2,1,0:T(8,128)(2,1)S(1)} %collective-permute-done.8.refs_2_), channel_id=1, source_target_pairs={{16,24},{17,25},{18,26},{19,27},{20,28},{21,29},{22,30},{23,31}} | collective-permute-start | bytes 786440 | tf_op jit(solution)/shard_map/on14/ppermute | solution.py:280

commit v3 on v2

--- a/solution.py
+++ b/solution.py
@@ -105,7 +105,7 @@
 def second_factor(x0h, x0m, mine, other, high_out, mid_out, u01_out, work, inverse):
     corner01 = from_column(1, mine, other, 0).astype(BF16)
     u01 = (mm(x0h[...], corner01) + mm(x0m[...], corner01)).astype(BF16)
-    u01_out[...] = u01
+    u01_out[...] = u01.T
     work[...] = from_column(1, mine, other, 1) - mm(u01.T, u01)
     eliminate(work, inverse)
     high, mid = split(inverse[...])
@@ -120,7 +120,7 @@
     for slot in range(slots):
         tile0 = from_column(0, mine, other, slot).astype(BF16)
         row0 = (mmt(tile0, x0h[...]) + mmt(tile0, x0m[...])).astype(BF16)
-        th, tm = split(from_column(1, mine, other, slot) - mm(row0, u01[...]))
+        th, tm = split(from_column(1, mine, other, slot) - mmt(row0, u01[...]))
         row1 = mmt(th, x1h[...]) + mmt(th, x1m[...]) + mmt(tm, x1h[...])
         row1 = jnp.where(slot * n_row + my_row >= 1, row1, 0.0)
         out[slot, :, :size] = row0
@@ -193,15 +193,21 @@
             pltpu.make_async_copy(slab_refs[0].at[pl.ds(base, width)], target, sems.at[panel]).wait()
         for slot in range(slots):
             pltpu.make_async_copy(slab_refs[slot].at[pl.ds(base, width)], own.at[slot], sems.at[2 + slot]).wait()
+        wide0 = jnp.concatenate([p0[b] for b in range(width)], axis=1)
+        wide1 = jnp.concatenate([p1[b] for b in range(width)], axis=1).astype(F32)
+        pair = mm(jnp.concatenate([x0h_ref[...], x0m_ref[...]], axis=0), wide0)
+        u0 = (pair[:size] + pair[size:]).astype(BF16)
+        th, tm = split(wide1 - mm(u01_ref[...], u0))
+        pair = mm(jnp.concatenate([x1h_ref[...], x1m_ref[...]], axis=0), th)
+        u1 = pair[:size] + pair[size:] + mm(x1h_ref[...], tm)
+        all_rows = jnp.concatenate([rows_ref[slot] for slot in range(slots)], axis=0)
         for b in range(width):
             col_tile = (base + b) * n_col + my_col
-            u0 = (mm(x0h_ref[...], p0[b]) + mm(x0m_ref[...], p0[b])).astype(BF16)
-            th, tm = split(p1[b].astype(F32) - mm(u01_ref[...].T, u0))
-            u1 = mm(x1h_ref[...], th) + mm(x1h_ref[...], tm) + mm(x1m_ref[...], th)
-            u1 = jnp.where(col_tile >= 1, u1, 0.0).astype(BF16)
-            both = jnp.concatenate([u0, u1], axis=0)
+            span = slice(b * size, (b + 1) * size)
+            second = jnp.where(col_tile >= 1, u1[:, span], 0.0).astype(BF16)
+            product = mm(all_rows, jnp.concatenate([u0[:, span], second], axis=0))
             for slot in range(slots):
-                tile = own[slot, b].astype(F32) - mm(rows_ref[slot], both)
+                tile = own[slot, b].astype(F32) - product[slot * size : (slot + 1) * size]
                 keep = (slot * n_row + my_row >= 2) & (col_tile >= 2)
                 tile = jnp.where(keep, tile, 0.0)
                 for h in range(halves):
@@ -281,74 +287,93 @@
 
     far_spans, near_spans = spans(first_counts), spans(second_counts)
     tile_rows = gram[:, 0, :, 0, 0, :]
-    far = {s: send(f"far{s[0]}", cut[s], (0, 3), (1, 0)) for s in far_spans}
-    near = {s: send(f"near{s[0]}", cut[s], (1, 2), (0, 1)) for s in near_spans[:2]}
-    ready = [cut[s] for s in far_spans + near_spans[:2]]
-    cross = send("cross", corner_piece, (0, 2), (1, 3))
-    back = {}
-
-    def tokens(i):
-        return [d[s] for s in far_spans[i : i + 1] for d in (far, back) if s in d]
-
-    top_ways = {1: near, 3: far, 2: {(0, 1): cross}}
-    bottom_ways = {0: far, 2: near, 3: {(0, 1): cross}}
-    hop_top, hop_bottom = {(0, 1): far[0, 1]}, {(0, 1): cross}
+    far, near, back, on = {}, {}, {}, {}
+    top_ways, bottom_ways = {1: near, 3: far, 2: back}, {0: far, 2: near, 3: on}
     for row in range(4, n_row):
-        hop_top = {s: send(f"top{s[0]}", x, (row - 1, row)) for s, x in hop_top.items()}
-        hop_bottom = {s: send(f"bottom{s[0]}", x, (row - 1, row)) for s, x in hop_bottom.items()}
-        top_ways[row], bottom_ways[row] = hop_top, hop_bottom
+        top_ways[row], bottom_ways[row] = {}, {}
+
+    def send_far(s, *tokens):
+        far[s] = send(f"far{s[0]}", after(cut[s], *tokens), (0, 3), (1, 0))
+        for row in range(4, n_row):
+            top_ways[row][s] = send(f"top{row}_{s[0]}", top_ways[row - 1][s], (row - 1, row))
+
+    def send_near(s, *tokens):
+        near[s] = send(f"near{s[0]}", after(cut[s], *tokens), (1, 2), (0, 1))
+
+    def send_back(s, *tokens):
+        back[s] = send(f"back{s[0]}", after(far[s], *tokens), (3, 2))
+
+    def send_on(s, *tokens):
+        on[s] = send(f"on{s[0]}", after(near[s], *tokens), (2, 3))
+        for row in range(4, n_row):
+            bottom_ways[row][s] = send(f"bottom{row}_{s[0]}", bottom_ways[row - 1][s], (row - 1, row))
+
+    def arrived(s):
+        return [near[s]] if s in near else []
+
+    corner_span = far_spans[0]
+    send_far(corner_span)
+    send_near(corner_span)
+    back[corner_span] = on[corner_span] = send("cross", corner_piece, (0, 2), (1, 3))
+    for row in range(4, n_row):
+        x = bottom_ways[row - 1][corner_span]
+        bottom_ways[row][corner_span] = send(f"bottom{row}", x, (row - 1, row))
+    for s in near_spans[1:3]:
+        send_near(s)
 
     def here(ways):
         x = corner_piece
-        for row, arrived in ways.items():
-            x = jnp.where(my_row == row, arrived[0, 1], x)
+        for row, pieces in ways.items():
+            x = jnp.where(my_row == row, pieces[corner_span], x)
         return x
 
     payload = jnp.concatenate([here(top_ways), here(bottom_ways)])
+    ready = [cut[s] for s in far_spans + near_spans[:3]]
     corners = over_columns("corner", [], after(payload, tile_rows, *ready))
+    for s in far_spans[1:]:
+        send_far(s)
 
     square = jax.ShapeDtypeStruct((size, size), BF16)
     scratch = [pltpu.VMEM((size, size), F32), pltpu.VMEM((size, size), F32)]
     x0h, x0m = vmem_call(first_factor, [square] * 2, scratch, "first")(*corners)
+    for s in far_spans[1:2]:
+        send_back(s, x0h)
+    for s in near_spans[3:4]:
+        send_near(s, x0h)
+    second_gate = [far[s] for s in far_spans[1:2]]
     x1h, x1m, u01 = vmem_call(second_factor, [square] * 3, scratch, "second")(
-        after(x0h, *tokens(1)), x0m, *corners
+        after(x0h, *second_gate), x0m, *corners
     )
-    for i, s in enumerate(near_spans[2:]):
-        gate = [x0h] if i < 2 else [x1h, near[near_spans[i - 1]]]
-        near[s] = send(f"near{s[0]}", after(cut[s], *gate), (1, 2), (0, 1))
-    back[0, 1] = cross
-    for i, s in enumerate(far_spans[1:]):
-        back[s] = send(f"back{s[0]}", after(far[s], x1h if i else x0h), (3, 2))
-    on = {(0, 1): cross}
+    for i, s in enumerate(near_spans[4:]):
+        send_near(s, x1h, near[near_spans[i + 1]])
+    for s in far_spans[2:]:
+        send_back(s, x1h)
     for s in near_spans[1:3]:
-        on[s] = send(f"on{s[0]}", after(near[s], x1h), (2, 3))
+        send_on(s, x1h)
     tiles = over_columns("tiles", [[corners[0]], [], [x0h]], tile_rows)
     panels = jax.ShapeDtypeStruct((slots, size, 2 * size), BF16)
-    rows = vmem_call(row_factor, panels, [], "rows")(after(x0h, on[near_spans[1]], *[back[s] for s in far_spans[1:2]], *[near[s] for s in near_spans[2:3]]), x0m, x1h, x1m, u01, *tiles)
-    for s in near_spans[3:]:
-        on[s] = send(f"on{s[0]}", after(near[s], rows), (2, 3))
+    rows_gate = [d[s] for d, k in ((on, near_spans[1:2]), (back, far_spans[1:2]), (near, near_spans[2:3])) for s in k]
+    rows = vmem_call(row_factor, panels, [], "rows")(after(x0h, *rows_gate), x0m, x1h, x1m, u01, *tiles)
     slab1 = [after(gram, x1h)[a, 0, :, :, 0, :].transpose(1, 0, 2) for a in range(1, slots)]
 
-    top_ways, bottom_ways = {1: near, 3: far, 2: back}, {0: far, 2: near, 3: on}
-    hop_top, hop_bottom = far, on
-    for row in range(4, n_row):
-        hop_top = {s: send(f"top{s[0]}", x, (row - 1, row)) for s, x in hop_top.items()}
-        hop_bottom = {s: send(f"bottom{s[0]}", x, (row - 1, row)) for s, x in hop_bottom.items()}
-        top_ways[row], bottom_ways[row] = hop_top, hop_bottom
-
     def parts(ways, base, width):
-        out = []
-        for row, arrived in ways.items():
-            for (start, count), array in sorted(arrived.items(), key=lambda item: item[0]):
+        found = []
+        for row, pieces in ways.items():
+            for (start, count), array in sorted(pieces.items(), key=lambda item: item[0]):
                 lo, hi = max(start, base), min(start + count, base + width)
                 if lo < hi:
-                    out.append((row, array, lo - start, hi - lo))
-        return out
+                    found.append((row, array, lo - start, hi - lo))
+        return found
 
     out = None
+    waiting = [s for s in near_spans if s not in on]
     for base, width in spans(widths):
         top, bottom = parts(top_ways, base, width), parts(bottom_ways, base, width)
         out = update_chunk(base, width, slab0, slab1, top, bottom, x0h, x0m, x1h, x1m, u01, rows, out)
+        for s in waiting[:1] if base == 0 else waiting:
+            near[s], out = lax.optimization_barrier((near[s], out))
+            send_on(s)
+        waiting = waiting[1:] if base == 0 else []
     return out.reshape(slots, 1, size, cols, 1, size)
 
 

time: 138 us -> 133 us (0.964); the launches traced: 138 us -> 131 us
  waiting for transfers between devices: 48.2 us -> 40.5 us
  local copies, waits for them, and re-layouts: 7.85 us -> 11 us
  Pallas kernels: 46.1 us -> 43.9 us
    ppermute x17, waiting for transfers between devices: 40.1 us -> 34.6 us  [send(): return lax.ppermute(x, 'row', [p for p in pairs])]
    ppermute x4, waiting for transfers between devices: 8.16 us -> 5.86 us  [over_columns(): lax.ppermute(x, 'col', [(i, i + step) for i in range(step) if i + step <...]
    optimization_barrier x1, local copies, waits for them, and re-layouts: 1.52 us -> 3.76 us  [after(): return lax.optimization_barrier((x, *tokens))[0]]
    pallas_call x5, Pallas kernels: 21.1 us -> 18.9 us  [update_chunk(): pl.pallas_call(body, in_specs=[any_spec] * n_any + [vmem_spec] * 6 + ([an...]
  transfers between devices with their start and end apart: 23 -> 23, of which waited for: 10 -> 11; matrix products, arithmetic and copies ran while one was open for 7% -> 9% of each run, Pallas kernels for 31% -> 31%
where the time goes in v3:
time: 133 us; the launch traced here: 131 us
  Pallas kernels  43.9 us (33%)
  waiting for transfers between devices  40.5 us (30%)
  starting transfers between devices  32.4 us (24%)
  local copies, waits for them, and re-layouts  11 us (8%)
  other arithmetic  2.79 us (2%)
    ppermute x17, waiting for transfers between devices, send(): return lax.ppermute(x, 'row', [p for p in pairs])  34.6 us
    ppermute x17, starting transfers between devices, send(): return lax.ppermute(x, 'row', [p for p in pairs])  21.1 us
    pallas_call x5, Pallas kernels, update_chunk(): pl.pallas_call(body, in_specs=[any_spec] * n_any + [vmem_spec] * 6 + ([an...  18.9 us
    pallas_call x1, Pallas kernels, local(): vmem_call(second_factor, [square] * 3, scratch, 'second')  12.2 us
    pallas_call x1, Pallas kernels, local(): x0h, x0m = vmem_call(first_factor, [square] * 2, scratch, 'first')(*corners)  11.8 us
    ppermute x4, starting transfers between devices, over_columns(): lax.ppermute(x, 'col', [(i, i + step) for i in range(step) if i + step <...  11.1 us
    ppermute x4, waiting for transfers between devices, over_columns(): lax.ppermute(x, 'col', [(i, i + step) for i in range(step) if i + step <...  5.86 us
    slice x5, local copies, waits for them, and re-layouts, local(): cut[start, count] = slab0[start:start + count]  3.87 us
  transfers between devices with their start and end apart: 23, of which 11 were waited for; matrix products, arithmetic and copies ran while one was open for 9% of the time, Pallas kernels for 31%

profile of v3, /device:TPU:16, one launch (start us, length us, event | category | flops | bytes accessed | tf_op | source)
XLA Modules:
  0.0 131.2 jit_solution(18141588786264837824)
XLA Ops:
  0.0 1.5 %slice.34 = bf16[1,1,256,1,1,256]{5,3,4,2,1,0:T(2,128)(2,1)S(1)} slice(bf16[2,1,256,16,1,256]{5,3,4,2,1,0:T(8,128)(2,1)} %param.1), slice={[0:1], [0:1], [0:256], [0:1], [0:1], [0:256]} | slice | bytes 262144 | tf_op jit(solution)/shard_map/slice | solution.py:278
  2.2 1.3 collective-permute-start.2
  3.5 1.3 collective-permute-start
  5.6 1.0 fusion
  6.6 1.0 slice.45
  7.6 1.0 slice.44
  8.6 0.8 slice.46
  9.7 0.7 copy.20
  10.4 3.9 %collective-permute-done.2.refs_2_ = bf16[1,256,256]{2,1,0:T(8,128)(2,1)S(1)} collective-permute-done((bf16[1,256,256]{2,1,0:T(8,128)(2,1)S(1)}, bf16[1,256,256]{2,1,0:T(8,128)(2,1)S(1)}, u32[]{:S(2)}, u32[]{:S(2)}) %collective-permute-start.2) | collective-permute-done | bytes 131104 | tf_op jit(solution)/shard_map/near0/ppermute | solution.py:286
  14.3 2.1 %collective-permute-done.refs_6_ = bf16[1,256,256]{2,1,0:T(8,128)(2,1)S(1)} collective-permute-done((bf16[1,256,256]{2,1,0:T(8,128)(2,1)S(1)}, bf16[1,256,256]{2,1,0:T(8,128)(2,1)S(1)}, u32[]{:S(2)}, u32[]{:S(2)}) %collective-permute-start) | collective-permute-done | bytes 131104 | tf_op jit(solution)/shard_map/cross/ppermute | solution.py:286
  16.4 3.4 %collective-permute-start.3 = (bf16[2,256,256]{2,1,0:T(8,128)(2,1)S(1)}, bf16[2,256,256]{2,1,0:T(8,128)(2,1)S(1)}, u32[]{:S(2)}, u32[]{:S(2)}) collective-permute-start(bf16[2,256,256]{2,1,0:T(8,128)(2,1)S(1)} %pad_maximum_fusion), channel_id=1, source_target_pairs={{0,2},{1,3},{8,10},{9,11},{16,18},{17,19},{24,26},{25,27}} | collective-permute-start | bytes 786440 | tf_op jit(solution)/shard_map/corner2/ppermute | solution.py:249
  19.8 1.6 %collective-permute-start.6 = (bf16[7,256,256]{2,1,0:T(8,128)(2,1)}, bf16[7,256,256]{2,1,0:T(8,128)(2,1)}, u32[]{:S(2)}, u32[]{:S(2)}) collective-permute-start(bf16[7,256,256]{2,1,0:T(8,128)(2,1)} %slice.44), channel_id=1, source_target_pairs={{0,24},{8,0},{1,25},{9,1},{2,26},{10,2},{3,27},{11,3},{4,28},{12,4... | collective-permute-start | bytes 2752520 | tf_op jit(solution)/shard_map/far1/ppermute | solution.py:286
  21.5 3.0 %collective-permute-done.3 = bf16[2,256,256]{2,1,0:T(8,128)(2,1)S(1)} collective-permute-done((bf16[2,256,256]{2,1,0:T(8,128)(2,1)S(1)}, bf16[2,256,256]{2,1,0:T(8,128)(2,1)S(1)}, u32[]{:S(2)}, u32[]{:S(2)}) %collective-permute-start.3) | collective-permute-done | bytes 262176 | tf_op jit(solution)/shard_map/corner2/ppermute | solution.py:249
  24.5 0.7 broadcast_select_fusion.1
  25.2 2.0 %collective-permute-start.4 = (bf16[2,256,256]{2,1,0:T(8,128)(2,1)}, bf16[2,256,256]{2,1,0:T(8,128)(2,1)}, u32[]{:S(2)}, u32[]{:S(2)}) collective-permute-start(bf16[2,256,256]{2,1,0:T(8,128)(2,1)} %broadcast_select_fusion.1), channel_id=1, source_target_pairs={{0,4},{1,5},{2,6},{3,7},{8,12},{9,13},{10,14},{11,15},{16,20},{17,... | collective-permute-start | bytes 786440 | tf_op jit(solution)/shard_map/corner4/ppermute | solution.py:249
  27.2 0.7 collective-permute-start.18
  27.9 2.9 %collective-permute-done.4 = bf16[2,256,256]{2,1,0:T(8,128)(2,1)} collective-permute-done((bf16[2,256,256]{2,1,0:T(8,128)(2,1)}, bf16[2,256,256]{2,1,0:T(8,128)(2,1)}, u32[]{:S(2)}, u32[]{:S(2)}) %collective-permute-start.4) | collective-permute-done | bytes 262176 | tf_op jit(solution)/shard_map/corner4/ppermute | solution.py:249
  30.7 1.0 broadcast_select_fusion.3.mine
  31.8 4.4 %collective-permute-start.14 = (bf16[2,256,256]{2,1,0:T(8,128)(2,1)}, bf16[2,256,256]{2,1,0:T(8,128)(2,1)S(1)}, u32[]{:S(2)}, u32[]{:S(2)}) collective-permute-start(bf16[2,256,256]{2,1,0:T(8,128)(2,1)} %bitcast.28), channel_id=1, source_target_pairs={{0,2},{1,3},{8,10},{9,11},{16,18},{17,19},{24,26},{25,27}} | collective-permute-start | bytes 786440 | tf_op jit(solution)/shard_map/tiles2/ppermute | solution.py:249
  36.2 1.3 collective-permute-start.9
  37.5 1.3 collective-permute-start.7
  38.8 11.8 %first.1 = (bf16[256,256]{1,0:T(8,128)(2,1)S(1)}, bf16[256,256]{1,0:T(8,128)(2,1)S(1)}) custom-call(bf16[2,256,256]{2,1,0:T(8,128)(2,1)S(1)} %broadcast_select_fusion.3.mine, bf16[2,256,256]{2,1,0:T(8,128)(2,1)S(1)} %collective-permute-done.5.other), custom_call_target="tpu_custom_call" | custom-call | tf_op jit(solution)/shard_map/first/pallas_call | solution.py:338
  50.6 1.3 collective-permute-start.11
  51.9 1.0 broadcast_select_fusion
  52.9 1.3 collective-permute-start.15
  54.2 12.2 %second.1 = (bf16[256,256]{1,0:T(8,128)(2,1)S(1)}, bf16[256,256]{1,0:T(8,128)(2,1)S(1)}, bf16[256,256]{1,0:T(8,128)(2,1)S(1)}) custom-call(bf16[256,256]{1,0:T(8,128)(2,1)S(1)} %get-tuple-element.42.x0h.refs_9_.refs_6_, bf16[256,256]{1,0:T(8,128)(2,1)S(1)} %get-tuple-element.32.x0m.refs_10_.refs_7_, bf16[2,256,256]{2,1,0:T(8,128)(2,1)S(1)} %broadcast_select_fusion.3.mine, ...), custom_call_target="tpu_custom_call" | custom-call | tf_op jit(solution)/shard_map/second/pallas_call | solution.py:344
  66.5 10.8 %collective-permute-done.9.refs_3_ = bf16[3,256,256]{2,1,0:T(8,128)(2,1)S(1)} collective-permute-done((bf16[3,256,256]{2,1,0:T(8,128)(2,1)}, bf16[3,256,256]{2,1,0:T(8,128)(2,1)S(1)}, u32[]{:S(2)}, u32[]{:S(2)}) %collective-permute-start.9) | collective-permute-done | bytes 393248 | tf_op jit(solution)/shard_map/near1/ppermute | solution.py:286
  77.2 1.3 collective-permute-start.13
  78.6 3.8 %copy.9 = bf16[2,1,256,16,1,256]{5,2,3,4,1,0:T(8,128)(2,1)S(1)} copy(bf16[2,1,256,16,1,256]{5,3,4,2,1,0:T(8,128)(2,1)} %param.1) | data formatting | bytes 8388608 | tf_op jit(solution)/shard_map/optimization_barrier | solution.py:258
  82.4 6.0 %collective-permute-done.7.refs_2_ = bf16[4,256,256]{2,1,0:T(8,128)(2,1)S(1)} collective-permute-done((bf16[4,256,256]{2,1,0:T(8,128)(2,1)}, bf16[4,256,256]{2,1,0:T(8,128)(2,1)S(1)}, u32[]{:S(2)}, u32[]{:S(2)}) %collective-permute-start.7) | collective-permute-done | bytes 524320 | tf_op jit(solution)/shard_map/near4/ppermute | solution.py:286
  88.4 1.3 collective-permute-start.17
  89.7 1.3 %collective-permute-start.12 = (bf16[4,256,256]{2,1,0:T(8,128)(2,1)S(1)}, bf16[4,256,256]{2,1,0:T(8,128)(2,1)S(1)}, u32[]{:S(2)}, u32[]{:S(2)}) collective-permute-start(bf16[4,256,256]{2,1,0:T(8,128)(2,1)S(1)} %collective-permute-done.7.refs_2_), channel_id=1, source_target_pairs={{16,24},{17,25},{18,26},{19,27},{20,28},{21,29},{22,30},{23,31}} | collective-permute-start | bytes 1572872 | tf_op jit(solution)/shard_map/on4/ppermute | solution.py:286
  91.0 1.3 collective-permute-start.19
  92.7 1.3 collective-permute-start.10
  94.0 1.3 collective-permute-start.8
  95.3 1.0 rows.1.refs_14_.refs_11_
  96.2 5.0 %update.5.refs_12_ = f32[512,16,2,128]{3,2,1,0:T(2,128)} custom-call(bf16[16,256,256]{2,1,0:T(8,128)(2,1)S(1)} %bitcast.23, bf16[16,256,256]{2,1,0:T(8,128)(2,1)S(1)} %slice_bitcast_fusion.refs_1_, bf16[1,256,256]{2,1,0:T(8,128)(2,1)S(1)} %collective-permute-done.2.refs_2_, bf16[3,256,256]{2,1,0:T(8,128)(2,1)S(1)} %collective-permute-done.9.refs_3_, ...), custom_call_target="tpu_custom_call" | custom-call | tf_op jit(solution)/shard_map/update/pallas_call | solution.py:221
  101.2 3.8 %collective-permute-done.17.refs_2_ = bf16[4,256,256]{2,1,0:T(8,128)(2,1)S(1)} collective-permute-done((bf16[4,256,256]{2,1,0:T(8,128)(2,1)S(1)}, bf16[4,256,256]{2,1,0:T(8,128)(2,1)S(1)}, u32[]{:S(2)}, u32[]{:S(2)}) %collective-permute-start.17) | collective-permute-done | bytes 524320 | tf_op jit(solution)/shard_map/near8/ppermute | solution.py:286
  105.1 1.3 collective-permute-start.22
  106.4 4.1 %update.6.refs_12_ = f32[512,16,2,128]{3,2,1,0:T(2,128)} custom-call(bf16[16,256,256]{2,1,0:T(8,128)(2,1)S(1)} %bitcast.24, bf16[16,256,256]{2,1,0:T(8,128)(2,1)S(1)} %slice_bitcast_fusion.refs_1_, bf16[4,256,256]{2,1,0:T(8,128)(2,1)S(1)} %collective-permute-done.7.refs_2_, ...), custom_call_target="tpu_custom_call", output_to_operand_aliasing={{}: (12, {})} | custom-call | tf_op jit(solution)/shard_map/update/pallas_call | solution.py:221
  110.7 4.7 %collective-permute-done.8.refs_2_ = bf16[2,256,256]{2,1,0:T(8,128)(2,1)S(1)} collective-permute-done((bf16[2,256,256]{2,1,0:T(8,128)(2,1)S(1)}, bf16[2,256,256]{2,1,0:T(8,128)(2,1)S(1)}, u32[]{:S(2)}, u32[]{:S(2)}) %collective-permute-start.8) | collective-permute-done | bytes 262176 | tf_op jit(solution)/shard_map/near14/ppermute | solution.py:286
  115.4 1.3 collective-permute-start.21
  116.7 1.3 collective-permute-start.20
  118.0 4.1 %update.7.refs_12_ = f32[512,16,2,128]{3,2,1,0:T(2,128)} custom-call(bf16[16,256,256]{2,1,0:T(8,128)(2,1)S(1)} %bitcast.25, bf16[16,256,256]{2,1,0:T(8,128)(2,1)S(1)} %slice_bitcast_fusion.refs_1_, bf16[4,256,256]{2,1,0:T(8,128)(2,1)S(1)} %collective-permute-done.17.refs_2_, ...), custom_call_target="tpu_custom_call", output_to_operand_aliasing={{}: (12, {})} | custom-call | tf_op jit(solution)/shard_map/update/pallas_call | solution.py:221
  122.2 1.2 collective-permute-done.21.refs_5_
  123.4 2.9 %update.8.refs_12_ = f32[512,16,2,128]{3,2,1,0:T(2,128)} custom-call(bf16[16,256,256]{2,1,0:T(8,128)(2,1)S(1)} %bitcast.26, bf16[16,256,256]{2,1,0:T(8,128)(2,1)S(1)} %slice_bitcast_fusion.refs_1_, bf16[2,256,256]{2,1,0:T(8,128)(2,1)S(1)} %collective-permute-done.10.refs_2_, ...), custom_call_target="tpu_custom_call", output_to_operand_aliasing={{}: (12, {})} | custom-call | tf_op jit(solution)/shard_map/update/pallas_call | solution.py:221
  126.3 1.9 %collective-permute-done.20.refs_5_ = bf16[2,256,256]{2,1,0:T(8,128)(2,1)S(1)} collective-permute-done((bf16[2,256,256]{2,1,0:T(8,128)(2,1)S(1)}, bf16[2,256,256]{2,1,0:T(8,128)(2,1)S(1)}, u32[]{:S(2)}, u32[]{:S(2)}) %collective-permute-start.20) | collective-permute-done | bytes 262176 | tf_op jit(solution)/shard_map/on14/ppermute | solution.py:286
  128.2 2.8 %update.9 = f32[512,16,2,128]{3,2,1,0:T(2,128)} custom-call(bf16[16,256,256]{2,1,0:T(8,128)(2,1)S(1)} %bitcast.27, bf16[16,256,256]{2,1,0:T(8,128)(2,1)S(1)} %slice_bitcast_fusion.refs_1_, bf16[2,256,256]{2,1,0:T(8,128)(2,1)S(1)} %collective-permute-done.8.refs_2_, ...), custom_call_target="tpu_custom_call", output_to_operand_aliasing={{}: (12, {})} | custom-call | tf_op jit(solution)/shard_map/update/pallas_call | solution.py:221
  (30 shorter events, 2.4 us)
Async XLA Ops:
  0.0 4.8 %slice-start = ((bf16[2,1,256,16,1,256]{5,3,4,2,1,0:T(8,128)(2,1)}), bf16[1,1,256,16,1,256]{5,3,4,2,1,0:T(8,128)(2,1)S(1)}, s32[]{:S(2)}) async-start(bf16[2,1,256,16,1,256]{5,3,4,2,1,0:T(8,128)(2,1)} %param.1), calls=%async_computation | async-start | bytes 4194304 | tf_op jit(solution)/shard_map/slice | solution.py:265
  1.5 8.9 %collective-permute-start.1 = (bf16[1,256,256]{2,1,0:T(8,128)(2,1)S(1)}, bf16[1,256,256]{2,1,0:T(8,128)(2,1)S(1)}, u32[]{:S(2)}, u32[]{:S(2)}) collective-permute-start(bf16[1,256,256]{2,1,0:T(8,128)(2,1)S(1)} %bitcast.30), channel_id=1, source_target_pairs={{0,24},{8,0},{1,25},{9,1},{2,26},{10,2},{3,27},{11,3},{4,28},{12,4... | collective-permute-start | bytes 393224 | tf_op jit(solution)/shard_map/far0/ppermute | solution.py:286
  2.2 12.1 %collective-permute-start.2 = (bf16[1,256,256]{2,1,0:T(8,128)(2,1)S(1)}, bf16[1,256,256]{2,1,0:T(8,128)(2,1)S(1)}, u32[]{:S(2)}, u32[]{:S(2)}) collective-permute-start(bf16[1,256,256]{2,1,0:T(8,128)(2,1)S(1)} %bitcast.31), channel_id=1, source_target_pairs={{8,16},{0,8},{9,17},{1,9},{10,18},{2,10},{11,19},{3,11},{12,20},{4... | collective-permute-start | bytes 393224 | tf_op jit(solution)/shard_map/near0/ppermute | solution.py:286
  3.5 12.8 %collective-permute-start = (bf16[1,256,256]{2,1,0:T(8,128)(2,1)S(1)}, bf16[1,256,256]{2,1,0:T(8,128)(2,1)S(1)}, u32[]{:S(2)}, u32[]{:S(2)}) collective-permute-start(bf16[1,256,256]{2,1,0:T(8,128)(2,1)S(1)} %bitcast.32), channel_id=1, source_target_pairs={{0,16},{8,24},{1,17},{9,25},{2,18},{10,26},{3,19},{11,27},{4,20},{... | collective-permute-start | bytes 393224 | tf_op jit(solution)/shard_map/cross/ppermute | solution.py:286
  5.5 3.9 %copy-start = (bf16[2,1,256,16,1,256]{5,3,4,2,1,0:T(8,128)(2,1)S(1)}, bf16[2,1,256,16,1,256]{5,3,4,2,1,0:T(8,128)(2,1)}, u32[]{:S(2)}) copy-start(bf16[2,1,256,16,1,256]{5,3,4,2,1,0:T(8,128)(2,1)} %param.1) | copy-start | bytes 12582916
  16.4 8.0 %collective-permute-start.3 = (bf16[2,256,256]{2,1,0:T(8,128)(2,1)S(1)}, bf16[2,256,256]{2,1,0:T(8,128)(2,1)S(1)}, u32[]{:S(2)}, u32[]{:S(2)}) collective-permute-start(bf16[2,256,256]{2,1,0:T(8,128)(2,1)S(1)} %pad_maximum_fusion), channel_id=1, source_target_pairs={{0,2},{1,3},{8,10},{9,11},{16,18},{17,19},{24,26},{25,27}} | collective-permute-start | bytes 786440 | tf_op jit(solution)/shard_map/corner2/ppermute | solution.py:249
  19.8 30.8 %collective-permute-start.6 = (bf16[7,256,256]{2,1,0:T(8,128)(2,1)}, bf16[7,256,256]{2,1,0:T(8,128)(2,1)}, u32[]{:S(2)}, u32[]{:S(2)}) collective-permute-start(bf16[7,256,256]{2,1,0:T(8,128)(2,1)} %slice.44), channel_id=1, source_target_pairs={{0,24},{8,0},{1,25},{9,1},{2,26},{10,2},{3,27},{11,3},{4,28},{12,4... | collective-permute-start | bytes 2752520 | tf_op jit(solution)/shard_map/far1/ppermute | solution.py:286
  25.2 5.6 %collective-permute-start.4 = (bf16[2,256,256]{2,1,0:T(8,128)(2,1)}, bf16[2,256,256]{2,1,0:T(8,128)(2,1)}, u32[]{:S(2)}, u32[]{:S(2)}) collective-permute-start(bf16[2,256,256]{2,1,0:T(8,128)(2,1)} %broadcast_select_fusion.1), channel_id=1, source_target_pairs={{0,4},{1,5},{2,6},{3,7},{8,12},{9,13},{10,14},{11,15},{16,20},{17,... | collective-permute-start | bytes 786440 | tf_op jit(solution)/shard_map/corner4/ppermute | solution.py:249
  27.2 62.5 %collective-permute-start.18 = (bf16[8,256,256]{2,1,0:T(8,128)(2,1)}, bf16[8,256,256]{2,1,0:T(8,128)(2,1)S(1)}, u32[]{:S(2)}, u32[]{:S(2)}) collective-permute-start(bf16[8,256,256]{2,1,0:T(8,128)(2,1)} %slice.45), channel_id=1, source_target_pairs={{0,24},{8,0},{1,25},{9,1},{2,26},{10,2},{3,27},{11,3},{4,28},{12,4... | collective-permute-start | bytes 3145736 | tf_op jit(solution)/shard_map/far8/ppermute | solution.py:286
  31.7 5.8 %collective-permute-start.5 = (bf16[2,256,256]{2,1,0:T(8,128)(2,1)S(1)}, bf16[2,256,256]{2,1,0:T(8,128)(2,1)S(1)}, u32[]{:S(2)}, u32[]{:S(2)}) collective-permute-start(bf16[2,256,256]{2,1,0:T(8,128)(2,1)S(1)} %broadcast_select_fusion.3.mine), channel_id=1, source_target_pairs={{0,1},{1,0},{2,3},{3,2},{4,5},{5,4},{6,7},{7,6},{8,9},{9,8},{10,11... | collective-permute-start | bytes 786440 | tf_op jit(solution)/shard_map/corner1/ppermute | solution.py:254
  31.8 20.1 %collective-permute-start.14 = (bf16[2,256,256]{2,1,0:T(8,128)(2,1)}, bf16[2,256,256]{2,1,0:T(8,128)(2,1)S(1)}, u32[]{:S(2)}, u32[]{:S(2)}) collective-permute-start(bf16[2,256,256]{2,1,0:T(8,128)(2,1)} %bitcast.28), channel_id=1, source_target_pairs={{0,2},{1,3},{8,10},{9,11},{16,18},{17,19},{24,26},{25,27}} | collective-permute-start | bytes 786440 | tf_op jit(solution)/shard_map/tiles2/ppermute | solution.py:249
  36.2 41.0 %collective-permute-start.9 = (bf16[3,256,256]{2,1,0:T(8,128)(2,1)}, bf16[3,256,256]{2,1,0:T(8,128)(2,1)S(1)}, u32[]{:S(2)}, u32[]{:S(2)}) collective-permute-start(bf16[3,256,256]{2,1,0:T(8,128)(2,1)} %slice.46), channel_id=1, source_target_pairs={{8,16},{0,8},{9,17},{1,9},{10,18},{2,10},{11,19},{3,11},{12,20},{4... | collective-permute-start | bytes 1179656 | tf_op jit(solution)/shard_map/near1/ppermute | solution.py:286
  37.5 50.9 %collective-permute-start.7 = (bf16[4,256,256]{2,1,0:T(8,128)(2,1)}, bf16[4,256,256]{2,1,0:T(8,128)(2,1)S(1)}, u32[]{:S(2)}, u32[]{:S(2)}) collective-permute-start(bf16[4,256,256]{2,1,0:T(8,128)(2,1)} %get-tuple-element.54), channel_id=1, source_target_pairs={{8,16},{0,8},{9,17},{1,9},{10,18},{2,10},{11,19},{3,11},{12,20},{4... | collective-permute-start | bytes 1572872 | tf_op jit(solution)/shard_map/near4/ppermute | solution.py:286
  50.6 42.0 %collective-permute-start.11 = (bf16[7,256,256]{2,1,0:T(8,128)(2,1)}, bf16[7,256,256]{2,1,0:T(8,128)(2,1)S(1)}, u32[]{:S(2)}, u32[]{:S(2)}) collective-permute-start(bf16[7,256,256]{2,1,0:T(8,128)(2,1)} %collective-permute-done.6.refs_5_.refs_3_), channel_id=1, source_target_pairs={{24,16},{25,17},{26,18},{27,19},{28,20},{29,21},{30,22},{31,23}} | collective-permute-start | bytes 2752520 | tf_op jit(solution)/shard_map/back1/ppermute | solution.py:286
  52.9 38.1 %collective-permute-start.15 = (bf16[2,256,256]{2,1,0:T(8,128)(2,1)S(1)}, bf16[2,256,256]{2,1,0:T(8,128)(2,1)S(1)}, u32[]{:S(2)}, u32[]{:S(2)}) collective-permute-start(bf16[2,256,256]{2,1,0:T(8,128)(2,1)S(1)} %broadcast_select_fusion), channel_id=1, source_target_pairs={{0,4},{1,5},{2,6},{3,7},{8,12},{9,13},{10,14},{11,15},{16,20},{17,... | collective-permute-start | bytes 786440 | tf_op jit(solution)/shard_map/tiles4/ppermute | solution.py:249
  77.2 15.2 %collective-permute-start.13 = (bf16[3,256,256]{2,1,0:T(8,128)(2,1)S(1)}, bf16[3,256,256]{2,1,0:T(8,128)(2,1)S(1)}, u32[]{:S(2)}, u32[]{:S(2)}) collective-permute-start(bf16[3,256,256]{2,1,0:T(8,128)(2,1)S(1)} %collective-permute-done.9.refs_3_), channel_id=1, source_target_pairs={{16,24},{17,25},{18,26},{19,27},{20,28},{21,29},{22,30},{23,31}} | collective-permute-start | bytes 1179656 | tf_op jit(solution)/shard_map/on1/ppermute | solution.py:286
  78.6 9.8 %copy-start.1 = (bf16[4,256,256]{2,1,0:T(8,128)(2,1)S(1)}, bf16[4,256,256]{2,1,0:T(8,128)(2,1)}, u32[]{:S(2)}) copy-start(bf16[4,256,256]{2,1,0:T(8,128)(2,1)} %get-tuple-element.45) | copy-start | bytes 1572868
  88.4 16.7 %collective-permute-start.17 = (bf16[4,256,256]{2,1,0:T(8,128)(2,1)S(1)}, bf16[4,256,256]{2,1,0:T(8,128)(2,1)S(1)}, u32[]{:S(2)}, u32[]{:S(2)}) collective-permute-start(bf16[4,256,256]{2,1,0:T(8,128)(2,1)S(1)} %copy-done.1), channel_id=1, source_target_pairs={{8,16},{0,8},{9,17},{1,9},{10,18},{2,10},{11,19},{3,11},{12,20},{4... | collective-permute-start | bytes 1572872 | tf_op jit(solution)/shard_map/near8/ppermute | solution.py:286
  89.7 16.7 %collective-permute-start.12 = (bf16[4,256,256]{2,1,0:T(8,128)(2,1)S(1)}, bf16[4,256,256]{2,1,0:T(8,128)(2,1)S(1)}, u32[]{:S(2)}, u32[]{:S(2)}) collective-permute-start(bf16[4,256,256]{2,1,0:T(8,128)(2,1)S(1)} %collective-permute-done.7.refs_2_), channel_id=1, source_target_pairs={{16,24},{17,25},{18,26},{19,27},{20,28},{21,29},{22,30},{23,31}} | collective-permute-start | bytes 1572872 | tf_op jit(solution)/shard_map/on4/ppermute | solution.py:286
  91.0 27.0 %collective-permute-start.19 = (bf16[8,256,256]{2,1,0:T(8,128)(2,1)S(1)}, bf16[8,256,256]{2,1,0:T(8,128)(2,1)S(1)}, u32[]{:S(2)}, u32[]{:S(2)}) collective-permute-start(bf16[8,256,256]{2,1,0:T(8,128)(2,1)S(1)} %collective-permute-done.18.refs_3_), channel_id=1, source_target_pairs={{24,16},{25,17},{26,18},{27,19},{28,20},{29,21},{30,22},{31,23}} | collective-permute-start | bytes 3145736 | tf_op jit(solution)/shard_map/back8/ppermute | solution.py:286
  92.4 1.6 %collective-permute-start.16 = (bf16[2,256,256]{2,1,0:T(8,128)(2,1)S(1)}, bf16[2,256,256]{2,1,0:T(8,128)(2,1)S(1)}, u32[]{:S(2)}, u32[]{:S(2)}) collective-permute-start(bf16[2,256,256]{2,1,0:T(8,128)(2,1)S(1)} %broadcast_select_fusion.2.mine), channel_id=1, source_target_pairs={{0,1},{1,0},{2,3},{3,2},{4,5},{5,4},{6,7},{7,6},{8,9},{9,8},{10,11... | collective-permute-start | bytes 786440 | tf_op jit(solution)/shard_map/tiles1/ppermute | solution.py:254
  92.7 18.0 %collective-permute-start.10 = (bf16[2,256,256]{2,1,0:T(8,128)(2,1)S(1)}, bf16[2,256,256]{2,1,0:T(8,128)(2,1)S(1)}, u32[]{:S(2)}, u32[]{:S(2)}) collective-permute-start(bf16[2,256,256]{2,1,0:T(8,128)(2,1)S(1)} %get-tuple-element.36), channel_id=1, source_target_pairs={{8,16},{0,8},{9,17},{1,9},{10,18},{2,10},{11,19},{3,11},{12,20},{4... | collective-permute-start | bytes 786440 | tf_op jit(solution)/shard_map/near12/ppermute | solution.py:286
  94.0 21.4 %collective-permute-start.8 = (bf16[2,256,256]{2,1,0:T(8,128)(2,1)S(1)}, bf16[2,256,256]{2,1,0:T(8,128)(2,1)S(1)}, u32[]{:S(2)}, u32[]{:S(2)}) collective-permute-start(bf16[2,256,256]{2,1,0:T(8,128)(2,1)S(1)} %get-tuple-element.35), channel_id=1, source_target_pairs={{8,16},{0,8},{9,17},{1,9},{10,18},{2,10},{11,19},{3,11},{12,20},{4... | collective-permute-start | bytes 786440 | tf_op jit(solution)/shard_map/near14/ppermute | solution.py:286
  105.1 13.0 %collective-permute-start.22 = (bf16[4,256,256]{2,1,0:T(8,128)(2,1)S(1)}, bf16[4,256,256]{2,1,0:T(8,128)(2,1)S(1)}, u32[]{:S(2)}, u32[]{:S(2)}) collective-permute-start(bf16[4,256,256]{2,1,0:T(8,128)(2,1)S(1)} %collective-permute-done.17.refs_2_), channel_id=1, source_target_pairs={{16,24},{17,25},{18,26},{19,27},{20,28},{21,29},{22,30},{23,31}} | collective-permute-start | bytes 1572872 | tf_op jit(solution)/shard_map/on8/ppermute | solution.py:286
  115.4 8.0 %collective-permute-start.21 = (bf16[2,256,256]{2,1,0:T(8,128)(2,1)S(1)}, bf16[2,256,256]{2,1,0:T(8,128)(2,1)S(1)}, u32[]{:S(2)}, u32[]{:S(2)}) collective-permute-start(bf16[2,256,256]{2,1,0:T(8,128)(2,1)S(1)} %collective-permute-done.10.refs_2_), channel_id=1, source_target_pairs={{16,24},{17,25},{18,26},{19,27},{20,28},{21,29},{22,30},{23,31}} | collective-permute-start | bytes 786440 | tf_op jit(solution)/shard_map/on12/ppermute | solution.py:286
  116.7 11.5 %collective-permute-start.20 = (bf16[2,256,256]{2,1,0:T(8,128)(2,1)S(1)}, bf16[2,256,256]{2,1,0:T(8,128)(2,1)S(1)}, u32[]{:S(2)}, u32[]{:S(2)}) collective-permute-start(bf16[2,256,256]{2,1,0:T(8,128)(2,1)S(1)} %collective-permute-done.8.refs_2_), channel_id=1, source_target_pairs={{16,24},{17,25},{18,26},{19,27},{20,28},{21,29},{22,30},{23,31}} | collective-permute-start | bytes 786440 | tf_op jit(solution)/shard_map/on14/ppermute | solution.py:286

commit v4 on v3

--- a/solution.py
+++ b/solution.py
@@ -118,9 +118,9 @@
     my_row = lax.axis_index("row")
     slots, size, _ = out.shape
     for slot in range(slots):
-        tile0 = from_column(0, mine, other, slot).astype(BF16)
+        tile0 = from_column(0, mine, other, 2 + slot).astype(BF16)
         row0 = (mmt(tile0, x0h[...]) + mmt(tile0, x0m[...])).astype(BF16)
-        th, tm = split(from_column(1, mine, other, slot) - mmt(row0, u01[...]))
+        th, tm = split(from_column(1, mine, other, 2 + slot) - mmt(row0, u01[...]))
         row1 = mmt(th, x1h[...]) + mmt(th, x1m[...]) + mmt(tm, x1h[...])
         row1 = jnp.where(slot * n_row + my_row >= 1, row1, 0.0)
         out[slot, :, :size] = row0
@@ -287,18 +287,18 @@
 
     far_spans, near_spans = spans(first_counts), spans(second_counts)
     tile_rows = gram[:, 0, :, 0, 0, :]
-    far, near, back, on = {}, {}, {}, {}
-    top_ways, bottom_ways = {1: near, 3: far, 2: back}, {0: far, 2: near, 3: on}
+    far, near, near_top, back, on = {}, {}, {}, {}, {}
+    top_ways, bottom_ways = {1: near_top, 3: far, 2: back}, {0: far, 2: near, 3: on}
     for row in range(4, n_row):
         top_ways[row], bottom_ways[row] = {}, {}
 
     def send_far(s, *tokens):
         far[s] = send(f"far{s[0]}", after(cut[s], *tokens), (0, 3), (1, 0))
-        for row in range(4, n_row):
+        for row in range(4, n_row) if s != far_spans[0] else ():
             top_ways[row][s] = send(f"top{row}_{s[0]}", top_ways[row - 1][s], (row - 1, row))
 
     def send_near(s, *tokens):
-        near[s] = send(f"near{s[0]}", after(cut[s], *tokens), (1, 2), (0, 1))
+        near[s] = near_top[s] = send(f"near{s[0]}", after(cut[s], *tokens), (1, 2), (0, 1))
 
     def send_back(s, *tokens):
         back[s] = send(f"back{s[0]}", after(far[s], *tokens), (3, 2))
@@ -312,48 +312,47 @@
         return [near[s]] if s in near else []
 
     corner_span = far_spans[0]
+    near_top[corner_span] = on[corner_span] = send("corner13", corner_piece, (1, 3), (0, 1))
     send_far(corner_span)
-    send_near(corner_span)
-    back[corner_span] = on[corner_span] = send("cross", corner_piece, (0, 2), (1, 3))
+    top_piece = jnp.where(my_row == 0, corner_piece, jnp.where(my_row == 1, on[corner_span], far[corner_span]))
+    bottom_piece = jnp.where(my_row == 0, far[corner_span], jnp.where(my_row == 1, corner_piece, on[corner_span]))
+    pair = jnp.concatenate([top_piece, bottom_piece])
+    got = send("pair", after(pair, *[cut[s] for s in far_spans[1:2]]), (3, 2))
+    back[corner_span], near[corner_span] = got[:1], got[1:]
+    pair = jnp.where(my_row == 2, got, pair)
     for row in range(4, n_row):
-        x = bottom_ways[row - 1][corner_span]
-        bottom_ways[row][corner_span] = send(f"bottom{row}", x, (row - 1, row))
+        got = send(f"pair{row}", pair, (row - 1, row))
+        top_ways[row][corner_span], bottom_ways[row][corner_span] = got[:1], got[1:]
+        pair = jnp.where(my_row == row, got, pair)
     for s in near_spans[1:3]:
         send_near(s)
 
-    def here(ways):
-        x = corner_piece
-        for row, pieces in ways.items():
-            x = jnp.where(my_row == row, pieces[corner_span], x)
-        return x
-
-    payload = jnp.concatenate([here(top_ways), here(bottom_ways)])
+    payload = jnp.concatenate([pair, tile_rows])
     ready = [cut[s] for s in far_spans + near_spans[:3]]
-    corners = over_columns("corner", [], after(payload, tile_rows, *ready))
     for s in far_spans[1:]:
         send_far(s)
+    corners = over_columns("corner", [[], *[[far[s]] for s in far_spans[1:3]]], after(payload, *ready))
 
     square = jax.ShapeDtypeStruct((size, size), BF16)
     scratch = [pltpu.VMEM((size, size), F32), pltpu.VMEM((size, size), F32)]
     x0h, x0m = vmem_call(first_factor, [square] * 2, scratch, "first")(*corners)
-    for s in far_spans[1:2]:
-        send_back(s, x0h)
     for s in near_spans[3:4]:
         send_near(s, x0h)
-    second_gate = [far[s] for s in far_spans[1:2]]
+    for s in far_spans[1:]:
+        send_back(s, *[x0h] * (s != far_spans[1]))
+    for s in near_spans[1:3]:
+        send_on(s, x0h)
+    second_gate = [d[s] for d, k in ((near, near_spans[2:3]), (back, far_spans[1:2])) for s in k]
     x1h, x1m, u01 = vmem_call(second_factor, [square] * 3, scratch, "second")(
         after(x0h, *second_gate), x0m, *corners
     )
     for i, s in enumerate(near_spans[4:]):
-        send_near(s, x1h, near[near_spans[i + 1]])
-    for s in far_spans[2:]:
-        send_back(s, x1h)
-    for s in near_spans[1:3]:
+        send_near(s, near[near_spans[i + 2]], x1h)
+    for s in near_spans[3:4]:
         send_on(s, x1h)
-    tiles = over_columns("tiles", [[corners[0]], [], [x0h]], tile_rows)
     panels = jax.ShapeDtypeStruct((slots, size, 2 * size), BF16)
-    rows_gate = [d[s] for d, k in ((on, near_spans[1:2]), (back, far_spans[1:2]), (near, near_spans[2:3])) for s in k]
-    rows = vmem_call(row_factor, panels, [], "rows")(after(x0h, *rows_gate), x0m, x1h, x1m, u01, *tiles)
+    rows_gate = [d[s] for d, k in ((on, near_spans[2:3]),) for s in k]
+    rows = vmem_call(row_factor, panels, [], "rows")(after(x0h, *rows_gate), x0m, x1h, x1m, u01, *corners)
     slab1 = [after(gram, x1h)[a, 0, :, :, 0, :].transpose(1, 0, 2) for a in range(1, slots)]
 
     def parts(ways, base, width):
@@ -370,10 +369,10 @@
     for base, width in spans(widths):
         top, bottom = parts(top_ways, base, width), parts(bottom_ways, base, width)
         out = update_chunk(base, width, slab0, slab1, top, bottom, x0h, x0m, x1h, x1m, u01, rows, out)
-        for s in waiting[:1] if base == 0 else waiting:
+        for s in waiting[:1]:
             near[s], out = lax.optimization_barrier((near[s], out))
             send_on(s)
-        waiting = waiting[1:] if base == 0 else []
+        waiting = waiting[1:]
     return out.reshape(slots, 1, size, cols, 1, size)
 
 

time: 133 us -> 128 us (0.962)
  the two profiles are of different devices: /device:TPU:16 before, /device:TPU:0 now
where the time goes in v4:
time: 128 us; the launch traced here: 127 us
  Pallas kernels  45.2 us (35%)
  starting transfers between devices  44.6 us (35%)
  waiting for transfers between devices  23.5 us (18%)
  local copies, waits for them, and re-layouts  9.11 us (7%)
  other arithmetic  3.94 us (3%)
    ppermute x17, starting transfers between devices, send(): return lax.ppermute(x, 'row', [p for p in pairs])  36.1 us
    pallas_call x5, Pallas kernels, update_chunk(): pl.pallas_call(body, in_specs=[any_spec] * n_any + [vmem_spec] * 6 + ([an...  20.3 us
    ppermute x17, waiting for transfers between devices, send(): return lax.ppermute(x, 'row', [p for p in pairs])  12.8 us
    pallas_call x1, Pallas kernels, local(): vmem_call(second_factor, [square] * 3, scratch, 'second')  12.2 us
    pallas_call x1, Pallas kernels, local(): x0h, x0m = vmem_call(first_factor, [square] * 2, scratch, 'first')(*corners)  11.8 us
    ppermute x2, waiting for transfers between devices, over_columns(): lax.ppermute(x, 'col', [(i, i + step) for i in range(step) if i + step <...  10.7 us
    ppermute x2, starting transfers between devices, over_columns(): lax.ppermute(x, 'col', [(i, i + step) for i in range(step) if i + step <...  8.43 us
    slice x5, local copies, waits for them, and re-layouts, local(): cut[start, count] = slab0[start:start + count]  3.89 us
  transfers between devices with their start and end apart: 20, of which 5 were waited for; matrix products, arithmetic and copies ran while one was open for 9% of the time, Pallas kernels for 33%

profile of v4, /device:TPU:0, one launch (start us, length us, event | category | flops | bytes accessed | tf_op | source)
XLA Modules:
  0.0 127.0 jit_solution(5778249601724678707)
XLA Ops:
  0.0 1.5 %slice.40 = bf16[1,1,256,1,1,256]{5,3,4,2,1,0:T(2,128)(2,1)S(1)} slice(bf16[2,1,256,16,1,256]{5,3,4,2,1,0:T(8,128)(2,1)} %param.1), slice={[0:1], [0:1], [0:256], [0:1], [0:1], [0:256]} | slice | bytes 262144 | tf_op jit(solution)/shard_map/slice | solution.py:278
  1.5 0.0 copy-start
  1.6 5.2 %collective-permute-start = (bf16[1,256,256]{2,1,0:T(8,128)(2,1)S(1)}, bf16[1,256,256]{2,1,0:T(8,128)(2,1)S(1)}, u32[]{:S(2)}, u32[]{:S(2)}) collective-permute-start(bf16[1,256,256]{2,1,0:T(8,128)(2,1)S(1)} %bitcast.29), channel_id=1, source_target_pairs={{8,24},{0,8},{9,25},{1,9},{10,26},{2,10},{11,27},{3,11},{12,28},{4... | collective-permute-start | bytes 393224 | tf_op jit(solution)/shard_map/corner13/ppermute | solution.py:286
  6.8 3.3 %collective-permute-start.1 = (bf16[1,256,256]{2,1,0:T(8,128)(2,1)S(1)}, bf16[1,256,256]{2,1,0:T(8,128)(2,1)S(1)}, u32[]{:S(2)}, u32[]{:S(2)}) collective-permute-start(bf16[1,256,256]{2,1,0:T(8,128)(2,1)S(1)} %bitcast.30), channel_id=1, source_target_pairs={{0,24},{8,0},{1,25},{9,1},{2,26},{10,2},{3,27},{11,3},{4,28},{12,4... | collective-permute-start | bytes 393224 | tf_op jit(solution)/shard_map/far0/ppermute | solution.py:286
  10.1 0.7 copy.19
  10.8 1.0 slice.52
  11.8 1.9 %collective-permute-start.4 = (bf16[7,256,256]{2,1,0:T(8,128)(2,1)}, bf16[7,256,256]{2,1,0:T(8,128)(2,1)}, u32[]{:S(2)}, u32[]{:S(2)}) collective-permute-start(bf16[7,256,256]{2,1,0:T(8,128)(2,1)} %slice.52), channel_id=1, source_target_pairs={{0,24},{8,0},{1,25},{9,1},{2,26},{10,2},{3,27},{11,3},{4,28},{12,4... | collective-permute-start | bytes 2752520 | tf_op jit(solution)/shard_map/far1/ppermute | solution.py:286
  13.7 0.3 slice.42
  14.0 1.0 slice.53
  15.0 0.8 slice.54
  15.9 0.0 collective-permute-done.refs_2_
  16.0 0.7 collective-permute-start.2
  16.7 1.0 fusion.1
  17.8 0.9 pad_maximum_fusion
  18.6 4.2 %collective-permute-start.3 = (bf16[4,256,256]{2,1,0:T(8,128)(2,1)}, bf16[4,256,256]{2,1,0:T(8,128)(2,1)}, u32[]{:S(2)}, u32[]{:S(2)}) collective-permute-start(bf16[4,256,256]{2,1,0:T(8,128)(2,1)} %pad_maximum_fusion), channel_id=1, source_target_pairs={{0,2},{1,3},{8,10},{9,11},{16,18},{17,19},{24,26},{25,27}} | collective-permute-start | bytes 1572872 | tf_op jit(solution)/shard_map/corner2/ppermute | solution.py:249
  22.8 7.7 %collective-permute-start.6 = (bf16[8,256,256]{2,1,0:T(8,128)(2,1)}, bf16[8,256,256]{2,1,0:T(8,128)(2,1)S(1)}, u32[]{:S(2)}, u32[]{:S(2)}) collective-permute-start(bf16[8,256,256]{2,1,0:T(8,128)(2,1)} %slice.53), channel_id=1, source_target_pairs={{0,24},{8,0},{1,25},{9,1},{2,26},{10,2},{3,27},{11,3},{4,28},{12,4... | collective-permute-start | bytes 3145736 | tf_op jit(solution)/shard_map/far8/ppermute | solution.py:286
  30.5 2.7 %collective-permute-done.3 = bf16[4,256,256]{2,1,0:T(8,128)(2,1)} collective-permute-done((bf16[4,256,256]{2,1,0:T(8,128)(2,1)}, bf16[4,256,256]{2,1,0:T(8,128)(2,1)}, u32[]{:S(2)}, u32[]{:S(2)}) %collective-permute-start.3) | collective-permute-done | bytes 524320 | tf_op jit(solution)/shard_map/corner2/ppermute | solution.py:249
  33.2 1.9 %broadcast_select_fusion = bf16[4,256,256]{2,1,0:T(8,128)(2,1)} fusion(bf16[4,256,256]{2,1,0:T(8,128)(2,1)} %collective-permute-done.3, bf16[4,256,256]{2,1,0:T(8,128)(2,1)} %pad_maximum_fusion, pred[]{:T(512)S(6)} %ge.7), kind=kLoop, calls=%fused_computation.3 | loop fusion | flops 262144 | bytes 1572865 | tf_op jit(solution)/shard_map/jit(_where)/select_n | solution.py:250
  35.1 2.2 %collective-permute-done.4.refs_5_.refs_3_ = bf16[7,256,256]{2,1,0:T(8,128)(2,1)} collective-permute-done((bf16[7,256,256]{2,1,0:T(8,128)(2,1)}, bf16[7,256,256]{2,1,0:T(8,128)(2,1)}, u32[]{:S(2)}, u32[]{:S(2)}) %collective-permute-start.4) | collective-permute-done | bytes 917536 | tf_op jit(solution)/shard_map/far1/ppermute | solution.py:286
  37.3 4.2 %collective-permute-start.5 = (bf16[4,256,256]{2,1,0:T(8,128)(2,1)}, bf16[4,256,256]{2,1,0:T(8,128)(2,1)}, u32[]{:S(2)}, u32[]{:S(2)}) collective-permute-start(bf16[4,256,256]{2,1,0:T(8,128)(2,1)} %broadcast_select_fusion), channel_id=1, source_target_pairs={{0,4},{1,5},{2,6},{3,7},{8,12},{9,13},{10,14},{11,15},{16,20},{17,... | collective-permute-start | bytes 1572872 | tf_op jit(solution)/shard_map/corner4/ppermute | solution.py:249
  41.5 8.0 %collective-permute-done.5 = bf16[4,256,256]{2,1,0:T(8,128)(2,1)} collective-permute-done((bf16[4,256,256]{2,1,0:T(8,128)(2,1)}, bf16[4,256,256]{2,1,0:T(8,128)(2,1)}, u32[]{:S(2)}, u32[]{:S(2)}) %collective-permute-start.5) | collective-permute-done | bytes 524320 | tf_op jit(solution)/shard_map/corner4/ppermute | solution.py:249
  49.5 1.1 broadcast_select_fusion.1.mine
  50.6 7.6 %collective-permute-done.6.refs_3_ = bf16[8,256,256]{2,1,0:T(8,128)(2,1)S(1)} collective-permute-done((bf16[8,256,256]{2,1,0:T(8,128)(2,1)}, bf16[8,256,256]{2,1,0:T(8,128)(2,1)S(1)}, u32[]{:S(2)}, u32[]{:S(2)}) %collective-permute-start.6) | collective-permute-done | bytes 1048608 | tf_op jit(solution)/shard_map/far8/ppermute | solution.py:286
  58.2 1.6 %collective-permute-start.8 = (bf16[4,256,256]{2,1,0:T(8,128)(2,1)}, bf16[4,256,256]{2,1,0:T(8,128)(2,1)S(1)}, u32[]{:S(2)}, u32[]{:S(2)}) collective-permute-start(bf16[4,256,256]{2,1,0:T(8,128)(2,1)} %get-tuple-element.54), channel_id=1, source_target_pairs={{8,16},{0,8},{9,17},{1,9},{10,18},{2,10},{11,19},{3,11},{12,20},{4... | collective-permute-start | bytes 1572872 | tf_op jit(solution)/shard_map/near4/ppermute | solution.py:286
  59.8 0.7 collective-permute-start.9
  60.5 1.9 %collective-permute-start.15 = (bf16[3,256,256]{2,1,0:T(8,128)(2,1)}, bf16[3,256,256]{2,1,0:T(8,128)(2,1)S(1)}, u32[]{:S(2)}, u32[]{:S(2)}) collective-permute-start(bf16[3,256,256]{2,1,0:T(8,128)(2,1)} %slice.54), channel_id=1, source_target_pairs={{8,16},{0,8},{9,17},{1,9},{10,18},{2,10},{11,19},{3,11},{12,20},{4... | collective-permute-start | bytes 1179656 | tf_op jit(solution)/shard_map/near1/ppermute | solution.py:286
  62.4 0.0 collective-permute-done.7.other
  62.4 11.8 %first.1 = (bf16[256,256]{1,0:T(8,128)(2,1)S(1)}, bf16[256,256]{1,0:T(8,128)(2,1)S(1)}) custom-call(bf16[4,256,256]{2,1,0:T(8,128)(2,1)S(1)} %broadcast_select_fusion.1.mine, bf16[4,256,256]{2,1,0:T(8,128)(2,1)S(1)} %collective-permute-done.7.other), custom_call_target="tpu_custom_call" | custom-call | tf_op jit(solution)/shard_map/first/pallas_call | solution.py:338
  74.2 1.9 %collective-permute-start.10 = (bf16[4,256,256]{2,1,0:T(8,128)(2,1)}, bf16[4,256,256]{2,1,0:T(8,128)(2,1)S(1)}, u32[]{:S(2)}, u32[]{:S(2)}) collective-permute-start(bf16[4,256,256]{2,1,0:T(8,128)(2,1)} %get-tuple-element.37), channel_id=1, source_target_pairs={{8,16},{0,8},{9,17},{1,9},{10,18},{2,10},{11,19},{3,11},{12,20},{4... | collective-permute-start | bytes 1572872 | tf_op jit(solution)/shard_map/near8/ppermute | solution.py:286
  76.2 0.7 collective-permute-start.13
  76.9 0.7 collective-permute-start.12
  77.6 3.0 %collective-permute-done.15.refs_3_ = bf16[3,256,256]{2,1,0:T(8,128)(2,1)S(1)} collective-permute-done((bf16[3,256,256]{2,1,0:T(8,128)(2,1)}, bf16[3,256,256]{2,1,0:T(8,128)(2,1)S(1)}, u32[]{:S(2)}, u32[]{:S(2)}) %collective-permute-start.15) | collective-permute-done | bytes 393248 | tf_op jit(solution)/shard_map/near1/ppermute | solution.py:286
  80.7 0.7 collective-permute-start.16
  81.4 1.0 fusion.2
  82.4 12.2 %second.1 = (bf16[256,256]{1,0:T(8,128)(2,1)S(1)}, bf16[256,256]{1,0:T(8,128)(2,1)S(1)}, bf16[256,256]{1,0:T(8,128)(2,1)S(1)}) custom-call(bf16[256,256]{1,0:T(8,128)(2,1)S(1)} %get-tuple-element.43.x0h.refs_10_.refs_6_.refs_7_, bf16[256,256]{1,0:T(8,128)(2,1)S(1)} %get-tuple-element.34.x0m.refs_11_.refs_7_.refs_8_, ...), custom_call_target="tpu_custom_call" | custom-call | tf_op jit(solution)/shard_map/second/pallas_call | solution.py:346
  94.6 1.5 %copy.9 = bf16[2,1,256,16,1,256]{5,2,3,4,1,0:T(8,128)(2,1)S(1)} copy(bf16[2,1,256,16,1,256]{5,3,4,2,1,0:T(8,128)(2,1)S(1)} %copy-done.1) | data formatting | bytes 8388608 | tf_op jit(solution)/shard_map/optimization_barrier | solution.py:258
  96.1 4.3 %collective-permute-start.14 = (bf16[2,256,256]{2,1,0:T(8,128)(2,1)S(1)}, bf16[2,256,256]{2,1,0:T(8,128)(2,1)S(1)}, u32[]{:S(2)}, u32[]{:S(2)}) collective-permute-start(bf16[2,256,256]{2,1,0:T(8,128)(2,1)S(1)} %get-tuple-element.44), channel_id=1, source_target_pairs={{8,16},{0,8},{9,17},{1,9},{10,18},{2,10},{11,19},{3,11},{12,20},{4... | collective-permute-start | bytes 786440 | tf_op jit(solution)/shard_map/near12/ppermute | solution.py:286
  100.4 2.8 %collective-permute-start.11 = (bf16[2,256,256]{2,1,0:T(8,128)(2,1)S(1)}, bf16[2,256,256]{2,1,0:T(8,128)(2,1)S(1)}, u32[]{:S(2)}, u32[]{:S(2)}) collective-permute-start(bf16[2,256,256]{2,1,0:T(8,128)(2,1)S(1)} %get-tuple-element.38), channel_id=1, source_target_pairs={{8,16},{0,8},{9,17},{1,9},{10,18},{2,10},{11,19},{3,11},{12,20},{4... | collective-permute-start | bytes 786440 | tf_op jit(solution)/shard_map/near14/ppermute | solution.py:286
  103.2 0.7 collective-permute-start.19
  103.9 0.1 slice_bitcast_fusion.refs_1_
  104.1 1.0 rows.1.refs_15_.refs_11_.refs_12_
  105.0 5.3 %update.5.refs_12_ = f32[512,16,2,128]{3,2,1,0:T(2,128)} custom-call(bf16[16,256,256]{2,1,0:T(8,128)(2,1)S(1)} %bitcast.23, bf16[16,256,256]{2,1,0:T(8,128)(2,1)S(1)} %slice_bitcast_fusion.refs_1_, bf16[1,256,256]{2,1,0:T(8,128)(2,1)S(1)} %collective-permute-done.refs_2_, bf16[3,256,256]{2,1,0:T(8,128)(2,1)S(1)} %collective-permute-done.15.refs_3_, ...), custom_call_target="tpu_custom_call" | custom-call | tf_op jit(solution)/shard_map/update/pallas_call | solution.py:221
  110.3 0.7 collective-permute-start.18
  111.0 5.1 %update.6.refs_12_ = f32[512,16,2,128]{3,2,1,0:T(2,128)} custom-call(bf16[16,256,256]{2,1,0:T(8,128)(2,1)S(1)} %bitcast.24, bf16[16,256,256]{2,1,0:T(8,128)(2,1)S(1)} %slice_bitcast_fusion.refs_1_, bf16[4,256,256]{2,1,0:T(8,128)(2,1)S(1)} %collective-permute-done.8.refs_2_, ...), custom_call_target="tpu_custom_call", output_to_operand_aliasing={{}: (12, {})} | custom-call | tf_op jit(solution)/shard_map/update/pallas_call | solution.py:221
  116.2 0.7 collective-permute-start.17
  116.9 4.1 %update.7.refs_13_ = f32[512,16,2,128]{3,2,1,0:T(2,128)} custom-call(bf16[16,256,256]{2,1,0:T(8,128)(2,1)S(1)} %bitcast.25, bf16[16,256,256]{2,1,0:T(8,128)(2,1)S(1)} %slice_bitcast_fusion.refs_1_, bf16[4,256,256]{2,1,0:T(8,128)(2,1)S(1)} %collective-permute-done.10.refs_2_, ...), custom_call_target="tpu_custom_call", output_to_operand_aliasing={{}: (12, {})} | custom-call | tf_op jit(solution)/shard_map/update/pallas_call | solution.py:221
  121.0 2.9 %update.8.refs_13_ = f32[512,16,2,128]{3,2,1,0:T(2,128)} custom-call(bf16[16,256,256]{2,1,0:T(8,128)(2,1)S(1)} %bitcast.26, bf16[16,256,256]{2,1,0:T(8,128)(2,1)S(1)} %slice_bitcast_fusion.refs_1_, bf16[2,256,256]{2,1,0:T(8,128)(2,1)S(1)} %collective-permute-done.14.refs_2_.refs_5_, ...), custom_call_target="tpu_custom_call", output_to_operand_aliasing={{}: (13, {})} | custom-call | tf_op jit(solution)/shard_map/update/pallas_call | solution.py:221
  123.9 2.9 %update.9 = f32[512,16,2,128]{3,2,1,0:T(2,128)} custom-call(bf16[16,256,256]{2,1,0:T(8,128)(2,1)S(1)} %bitcast.27, bf16[16,256,256]{2,1,0:T(8,128)(2,1)S(1)} %slice_bitcast_fusion.refs_1_, bf16[2,256,256]{2,1,0:T(8,128)(2,1)S(1)} %collective-permute-done.11.refs_2_.refs_5_, ...), custom_call_target="tpu_custom_call", output_to_operand_aliasing={{}: (13, {})} | custom-call | tf_op jit(solution)/shard_map/update/pallas_call | solution.py:221
  (27 shorter events, 0.2 us)
Async XLA Ops:
  0.0 10.1 %slice-start = ((bf16[2,1,256,16,1,256]{5,3,4,2,1,0:T(8,128)(2,1)}), bf16[1,1,256,16,1,256]{5,3,4,2,1,0:T(8,128)(2,1)S(1)}, s32[]{:S(2)}) async-start(bf16[2,1,256,16,1,256]{5,3,4,2,1,0:T(8,128)(2,1)} %param.1), calls=%async_computation | async-start | bytes 4194304 | tf_op jit(solution)/shard_map/slice | solution.py:265
  1.5 12.2 %copy-start = (bf16[2,1,256,16,1,256]{5,3,4,2,1,0:T(8,128)(2,1)S(1)}, bf16[2,1,256,16,1,256]{5,3,4,2,1,0:T(8,128)(2,1)}, u32[]{:S(2)}) copy-start(bf16[2,1,256,16,1,256]{5,3,4,2,1,0:T(8,128)(2,1)} %param.1) | copy-start | bytes 12582916
  1.6 14.3 %collective-permute-start = (bf16[1,256,256]{2,1,0:T(8,128)(2,1)S(1)}, bf16[1,256,256]{2,1,0:T(8,128)(2,1)S(1)}, u32[]{:S(2)}, u32[]{:S(2)}) collective-permute-start(bf16[1,256,256]{2,1,0:T(8,128)(2,1)S(1)} %bitcast.29), channel_id=1, source_target_pairs={{8,24},{0,8},{9,25},{1,9},{10,26},{2,10},{11,27},{3,11},{12,28},{4... | collective-permute-start | bytes 393224 | tf_op jit(solution)/shard_map/corner13/ppermute | solution.py:286
  6.8 9.1 %collective-permute-start.1 = (bf16[1,256,256]{2,1,0:T(8,128)(2,1)S(1)}, bf16[1,256,256]{2,1,0:T(8,128)(2,1)S(1)}, u32[]{:S(2)}, u32[]{:S(2)}) collective-permute-start(bf16[1,256,256]{2,1,0:T(8,128)(2,1)S(1)} %bitcast.30), channel_id=1, source_target_pairs={{0,24},{8,0},{1,25},{9,1},{2,26},{10,2},{3,27},{11,3},{4,28},{12,4... | collective-permute-start | bytes 393224 | tf_op jit(solution)/shard_map/far0/ppermute | solution.py:286
  11.8 25.5 %collective-permute-start.4 = (bf16[7,256,256]{2,1,0:T(8,128)(2,1)}, bf16[7,256,256]{2,1,0:T(8,128)(2,1)}, u32[]{:S(2)}, u32[]{:S(2)}) collective-permute-start(bf16[7,256,256]{2,1,0:T(8,128)(2,1)} %slice.52), channel_id=1, source_target_pairs={{0,24},{8,0},{1,25},{9,1},{2,26},{10,2},{3,27},{11,3},{4,28},{12,4... | collective-permute-start | bytes 2752520 | tf_op jit(solution)/shard_map/far1/ppermute | solution.py:286
  16.0 1.7 %collective-permute-start.2 = (bf16[2,256,256]{2,1,0:T(8,128)(2,1)S(1)}, bf16[2,256,256]{2,1,0:T(8,128)(2,1)S(1)}, u32[]{:S(2)}, u32[]{:S(2)}) collective-permute-start(bf16[2,256,256]{2,1,0:T(8,128)(2,1)S(1)} %pad_maximum_fusion.1), channel_id=1, source_target_pairs={{24,16},{25,17},{26,18},{27,19},{28,20},{29,21},{30,22},{31,23}} | collective-permute-start | bytes 786440 | tf_op jit(solution)/shard_map/pair/ppermute | solution.py:286
  17.7 0.9 copy-start.2
  18.6 14.6 %collective-permute-start.3 = (bf16[4,256,256]{2,1,0:T(8,128)(2,1)}, bf16[4,256,256]{2,1,0:T(8,128)(2,1)}, u32[]{:S(2)}, u32[]{:S(2)}) collective-permute-start(bf16[4,256,256]{2,1,0:T(8,128)(2,1)} %pad_maximum_fusion), channel_id=1, source_target_pairs={{0,2},{1,3},{8,10},{9,11},{16,18},{17,19},{24,26},{25,27}} | collective-permute-start | bytes 1572872 | tf_op jit(solution)/shard_map/corner2/ppermute | solution.py:249
  22.8 35.4 %collective-permute-start.6 = (bf16[8,256,256]{2,1,0:T(8,128)(2,1)}, bf16[8,256,256]{2,1,0:T(8,128)(2,1)S(1)}, u32[]{:S(2)}, u32[]{:S(2)}) collective-permute-start(bf16[8,256,256]{2,1,0:T(8,128)(2,1)} %slice.53), channel_id=1, source_target_pairs={{0,24},{8,0},{1,25},{9,1},{2,26},{10,2},{3,27},{11,3},{4,28},{12,4... | collective-permute-start | bytes 3145736 | tf_op jit(solution)/shard_map/far8/ppermute | solution.py:286
  37.3 12.2 %collective-permute-start.5 = (bf16[4,256,256]{2,1,0:T(8,128)(2,1)}, bf16[4,256,256]{2,1,0:T(8,128)(2,1)}, u32[]{:S(2)}, u32[]{:S(2)}) collective-permute-start(bf16[4,256,256]{2,1,0:T(8,128)(2,1)} %broadcast_select_fusion), channel_id=1, source_target_pairs={{0,4},{1,5},{2,6},{3,7},{8,12},{9,13},{10,14},{11,15},{16,20},{17,... | collective-permute-start | bytes 1572872 | tf_op jit(solution)/shard_map/corner4/ppermute | solution.py:249
  41.5 53.1 %copy-start.1 = (bf16[2,1,256,16,1,256]{5,3,4,2,1,0:T(8,128)(2,1)S(1)}, bf16[2,1,256,16,1,256]{5,3,4,2,1,0:T(8,128)(2,1)}, u32[]{:S(2)}) copy-start(bf16[2,1,256,16,1,256]{5,3,4,2,1,0:T(8,128)(2,1)} %param.1) | copy-start | bytes 12582916
  58.2 4.2 %collective-permute-start.7 = (bf16[4,256,256]{2,1,0:T(8,128)(2,1)S(1)}, bf16[4,256,256]{2,1,0:T(8,128)(2,1)S(1)}, u32[]{:S(2)}, u32[]{:S(2)}) collective-permute-start(bf16[4,256,256]{2,1,0:T(8,128)(2,1)S(1)} %broadcast_select_fusion.1.mine), channel_id=1, source_target_pairs={{0,1},{1,0},{2,3},{3,2},{4,5},{5,4},{6,7},{7,6},{8,9},{9,8},{10,11... | collective-permute-start | bytes 1572872 | tf_op jit(solution)/shard_map/corner1/ppermute | solution.py:254
  58.2 18.0 %collective-permute-start.8 = (bf16[4,256,256]{2,1,0:T(8,128)(2,1)}, bf16[4,256,256]{2,1,0:T(8,128)(2,1)S(1)}, u32[]{:S(2)}, u32[]{:S(2)}) collective-permute-start(bf16[4,256,256]{2,1,0:T(8,128)(2,1)} %get-tuple-element.54), channel_id=1, source_target_pairs={{8,16},{0,8},{9,17},{1,9},{10,18},{2,10},{11,19},{3,11},{12,20},{4... | collective-permute-start | bytes 1572872 | tf_op jit(solution)/shard_map/near4/ppermute | solution.py:286
  59.8 22.6 %collective-permute-start.9 = (bf16[7,256,256]{2,1,0:T(8,128)(2,1)}, bf16[7,256,256]{2,1,0:T(8,128)(2,1)S(1)}, u32[]{:S(2)}, u32[]{:S(2)}) collective-permute-start(bf16[7,256,256]{2,1,0:T(8,128)(2,1)} %collective-permute-done.4.refs_5_.refs_3_), channel_id=1, source_target_pairs={{24,16},{25,17},{26,18},{27,19},{28,20},{29,21},{30,22},{31,23}} | collective-permute-start | bytes 2752520 | tf_op jit(solution)/shard_map/back1/ppermute | solution.py:286
  60.5 20.2 %collective-permute-start.15 = (bf16[3,256,256]{2,1,0:T(8,128)(2,1)}, bf16[3,256,256]{2,1,0:T(8,128)(2,1)S(1)}, u32[]{:S(2)}, u32[]{:S(2)}) collective-permute-start(bf16[3,256,256]{2,1,0:T(8,128)(2,1)} %slice.54), channel_id=1, source_target_pairs={{8,16},{0,8},{9,17},{1,9},{10,18},{2,10},{11,19},{3,11},{12,20},{4... | collective-permute-start | bytes 1179656 | tf_op jit(solution)/shard_map/near1/ppermute | solution.py:286
  74.2 26.2 %collective-permute-start.10 = (bf16[4,256,256]{2,1,0:T(8,128)(2,1)}, bf16[4,256,256]{2,1,0:T(8,128)(2,1)S(1)}, u32[]{:S(2)}, u32[]{:S(2)}) collective-permute-start(bf16[4,256,256]{2,1,0:T(8,128)(2,1)} %get-tuple-element.37), channel_id=1, source_target_pairs={{8,16},{0,8},{9,17},{1,9},{10,18},{2,10},{11,19},{3,11},{12,20},{4... | collective-permute-start | bytes 1572872 | tf_op jit(solution)/shard_map/near8/ppermute | solution.py:286
  76.2 27.0 %collective-permute-start.13 = (bf16[4,256,256]{2,1,0:T(8,128)(2,1)S(1)}, bf16[4,256,256]{2,1,0:T(8,128)(2,1)S(1)}, u32[]{:S(2)}, u32[]{:S(2)}) collective-permute-start(bf16[4,256,256]{2,1,0:T(8,128)(2,1)S(1)} %collective-permute-done.8.refs_2_), channel_id=1, source_target_pairs={{16,24},{17,25},{18,26},{19,27},{20,28},{21,29},{22,30},{23,31}} | collective-permute-start | bytes 1572872 | tf_op jit(solution)/shard_map/on4/ppermute | solution.py:286
  76.9 40.0 %collective-permute-start.12 = (bf16[8,256,256]{2,1,0:T(8,128)(2,1)S(1)}, bf16[8,256,256]{2,1,0:T(8,128)(2,1)S(1)}, u32[]{:S(2)}, u32[]{:S(2)}) collective-permute-start(bf16[8,256,256]{2,1,0:T(8,128)(2,1)S(1)} %collective-permute-done.6.refs_3_), channel_id=1, source_target_pairs={{24,16},{25,17},{26,18},{27,19},{28,20},{29,21},{30,22},{31,23}} | collective-permute-start | bytes 3145736 | tf_op jit(solution)/shard_map/back8/ppermute | solution.py:286
  80.7 24.4 %collective-permute-start.16 = (bf16[3,256,256]{2,1,0:T(8,128)(2,1)S(1)}, bf16[3,256,256]{2,1,0:T(8,128)(2,1)S(1)}, u32[]{:S(2)}, u32[]{:S(2)}) collective-permute-start(bf16[3,256,256]{2,1,0:T(8,128)(2,1)S(1)} %collective-permute-done.15.refs_3_), channel_id=1, source_target_pairs={{16,24},{17,25},{18,26},{19,27},{20,28},{21,29},{22,30},{23,31}} | collective-permute-start | bytes 1179656 | tf_op jit(solution)/shard_map/on1/ppermute | solution.py:286
  96.1 14.2 %collective-permute-start.14 = (bf16[2,256,256]{2,1,0:T(8,128)(2,1)S(1)}, bf16[2,256,256]{2,1,0:T(8,128)(2,1)S(1)}, u32[]{:S(2)}, u32[]{:S(2)}) collective-permute-start(bf16[2,256,256]{2,1,0:T(8,128)(2,1)S(1)} %get-tuple-element.44), channel_id=1, source_target_pairs={{8,16},{0,8},{9,17},{1,9},{10,18},{2,10},{11,19},{3,11},{12,20},{4... | collective-permute-start | bytes 786440 | tf_op jit(solution)/shard_map/near12/ppermute | solution.py:286
  100.4 15.7 %collective-permute-start.11 = (bf16[2,256,256]{2,1,0:T(8,128)(2,1)S(1)}, bf16[2,256,256]{2,1,0:T(8,128)(2,1)S(1)}, u32[]{:S(2)}, u32[]{:S(2)}) collective-permute-start(bf16[2,256,256]{2,1,0:T(8,128)(2,1)S(1)} %get-tuple-element.38), channel_id=1, source_target_pairs={{8,16},{0,8},{9,17},{1,9},{10,18},{2,10},{11,19},{3,11},{12,20},{4... | collective-permute-start | bytes 786440 | tf_op jit(solution)/shard_map/near14/ppermute | solution.py:286
  103.2 13.6 %collective-permute-start.19 = (bf16[4,256,256]{2,1,0:T(8,128)(2,1)S(1)}, bf16[4,256,256]{2,1,0:T(8,128)(2,1)S(1)}, u32[]{:S(2)}, u32[]{:S(2)}) collective-permute-start(bf16[4,256,256]{2,1,0:T(8,128)(2,1)S(1)} %collective-permute-done.10.refs_2_), channel_id=1, source_target_pairs={{16,24},{17,25},{18,26},{19,27},{20,28},{21,29},{22,30},{23,31}} | collective-permute-start | bytes 1572872 | tf_op jit(solution)/shard_map/on8/ppermute | solution.py:286
  110.3 10.7 %collective-permute-start.18 = (bf16[2,256,256]{2,1,0:T(8,128)(2,1)S(1)}, bf16[2,256,256]{2,1,0:T(8,128)(2,1)S(1)}, u32[]{:S(2)}, u32[]{:S(2)}) collective-permute-start(bf16[2,256,256]{2,1,0:T(8,128)(2,1)S(1)} %collective-permute-done.14.refs_2_.refs_5_), channel_id=1, source_target_pairs={{16,24},{17,25},{18,26},{19,27},{20,28},{21,29},{22,30},{23,31}} | collective-permute-start | bytes 786440 | tf_op jit(solution)/shard_map/on12/ppermute | solution.py:286
  116.2 7.7 %collective-permute-start.17 = (bf16[2,256,256]{2,1,0:T(8,128)(2,1)S(1)}, bf16[2,256,256]{2,1,0:T(8,128)(2,1)S(1)}, u32[]{:S(2)}, u32[]{:S(2)}) collective-permute-start(bf16[2,256,256]{2,1,0:T(8,128)(2,1)S(1)} %collective-permute-done.11.refs_2_.refs_5_), channel_id=1, source_target_pairs={{16,24},{17,25},{18,26},{19,27},{20,28},{21,29},{22,30},{23,31}} | collective-permute-start | bytes 786440 | tf_op jit(solution)/shard_map/on14/ppermute | solution.py:286

commit v5 on v4

--- a/solution.py
+++ b/solution.py
@@ -25,38 +25,44 @@
     groups = NB // 8
     sub = lax.broadcasted_iota(jnp.int32, (8, 2 * NB), 0)
 
-    def group(g, tiles):
-        pivot = tiles[0]
-        cols = [lane(pivot, j) for j in range(8)]
-        upper, recips, rows, scale = {}, [], [], None
-        for j in range(8):
-            d = sublane(cols[j], j)
-            recips.append(1.0 / d)
-            factor = jnp.where(sub > j, cols[j] * recips[j], 0.0)
-            for l in range(j + 1, 8):
-                upper[j, l] = sublane(cols[l], j)
-                cols[l] = cols[l] - factor * upper[j, l]
-            rows.append(sublane(pivot, j))
-            pivot = pivot - factor * rows[j]
-            root = lax.rsqrt(d)
-            scale = root if scale is None else jnp.where(sub >= j, root, scale)
-        out = []
-        for i in range(1, groups):
-            live = i < groups - g
-            tile = tiles[i]
-            own = [lane(tile, j) for j in range(8)]
+    def step(count):
+        def group(g, tiles):
+            pivot = tiles[0]
+            cols = [lane(pivot, j) for j in range(8)]
+            upper, recips, rows, scale = {}, [], [], None
             for j in range(8):
-                factor = own[j] * recips[j]
+                d = sublane(cols[j], j)
+                recips.append(1.0 / d)
+                factor = jnp.where(sub > j, cols[j] * recips[j], 0.0)
                 for l in range(j + 1, 8):
-                    own[l] = own[l] - factor * upper[j, l]
-                tile = tile - jnp.where(live, factor, 0.0) * rows[j]
-            out.append(tile)
-        out.append(pivot * scale)
-        return tuple(pltpu.roll(t, 2 * NB - 8, 1) for t in out)
-
+                    upper[j, l] = sublane(cols[l], j)
+                    cols[l] = cols[l] - factor * upper[j, l]
+                rows.append(sublane(pivot, j))
+                pivot = pivot - factor * rows[j]
+                root = lax.rsqrt(d)
+                scale = root if scale is None else jnp.where(sub >= j, root, scale)
+            out = []
+            for i in range(1, count):
+                live = i < groups - g
+                tile = tiles[i]
+                own = [lane(tile, j) for j in range(8)]
+                for j in range(8):
+                    factor = own[j] * recips[j]
+                    for l in range(j + 1, 8):
+                        own[l] = own[l] - factor * upper[j, l]
+                    tile = tile - jnp.where(live, factor, 0.0) * rows[j]
+                out.append(tile)
+            out.append(pivot * scale)
+            return tuple(pltpu.roll(t, 2 * NB - 8, 1) for t in out)
+
+        return group
+
+    half = groups // 2
     tiles = tuple(wide[8 * i : 8 * i + 8] for i in range(groups))
-    tiles = lax.fori_loop(0, groups, group, tiles)
-    return jnp.concatenate(tiles, axis=0)[:, :NB]
+    tiles = lax.fori_loop(0, half, step(groups), tiles)
+    rest = lax.fori_loop(half, groups, step(groups - half), tiles[: groups - half])
+    done = [pltpu.roll(t, 2 * NB - 8 * (groups - half), 1) for t in tiles[groups - half :]]
+    return jnp.concatenate([*done, *rest], axis=0)[:, :NB]
 
 
 def eliminate(work, inverse):
@@ -210,8 +216,7 @@
                 tile = own[slot, b].astype(F32) - product[slot * size : (slot + 1) * size]
                 keep = (slot * n_row + my_row >= 2) & (col_tile >= 2)
                 tile = jnp.where(keep, tile, 0.0)
-                for h in range(halves):
-                    result[b, pl.ds(slot * size, size), h, :] = tile[:, h * 128 : (h + 1) * 128]
+                result[b, pl.ds(slot * size, size), :, :] = tile.reshape(size, halves, 128)
             pltpu.make_async_copy(result.at[b], out_ref.at[:, base + b], out_sem.at[b]).start()
         for b in range(width):
             pltpu.make_async_copy(result.at[b], out_ref.at[:, base + b], out_sem.at[b]).wait()

time: 128 us -> 124 us (0.969)
  the two profiles are of different devices: /device:TPU:0 before, /device:TPU:16 now
where the time goes in v5:
time: 124 us; the launch traced here: 123 us
  waiting for transfers between devices  42.3 us (34%)
  Pallas kernels  37.9 us (31%)
  starting transfers between devices  29.1 us (23%)
  local copies, waits for them, and re-layouts  9.11 us (7%)
  other arithmetic  3.94 us (3%)
    ppermute x17, waiting for transfers between devices, send(): return lax.ppermute(x, 'row', [p for p in pairs])  26.4 us
    ppermute x17, starting transfers between devices, send(): return lax.ppermute(x, 'row', [p for p in pairs])  22.8 us
    ppermute x2, waiting for transfers between devices, over_columns(): lax.ppermute(x, 'col', [(i, i + step) for i in range(step) if i + step <...  15.9 us
    pallas_call x5, Pallas kernels, update_chunk(): pl.pallas_call(body, in_specs=[any_spec] * n_any + [vmem_spec] * 6 + ([an...  14.1 us
    pallas_call x1, Pallas kernels, local(): vmem_call(second_factor, [square] * 3, scratch, 'second')  11.6 us
    pallas_call x1, Pallas kernels, local(): x0h, x0m = vmem_call(first_factor, [square] * 2, scratch, 'first')(*corners)  11.2 us
    ppermute x2, starting transfers between devices, over_columns(): lax.ppermute(x, 'col', [(i, i + step) for i in range(step) if i + step <...  6.29 us
    slice x5, local copies, waits for them, and re-layouts, local(): cut[start, count] = slab0[start:start + count]  3.89 us
  transfers between devices with their start and end apart: 20, of which 9 were waited for; matrix products, arithmetic and copies ran while one was open for 9% of the time, Pallas kernels for 29%

profile of v5, /device:TPU:16, one launch (start us, length us, event | category | flops | bytes accessed | tf_op | source)
XLA Modules:
  0.0 122.9 jit_solution(16519036376906495507)
XLA Ops:
  0.0 1.5 %slice.40 = bf16[1,1,256,1,1,256]{5,3,4,2,1,0:T(2,128)(2,1)S(1)} slice(bf16[2,1,256,16,1,256]{5,3,4,2,1,0:T(8,128)(2,1)} %param.1), slice={[0:1], [0:1], [0:256], [0:1], [0:1], [0:256]} | slice | bytes 262144 | tf_op jit(solution)/shard_map/slice | solution.py:283
  1.6 0.8 collective-permute-start
  2.4 0.8 collective-permute-start.1
  3.2 0.7 copy.19
  3.9 1.0 slice.52
  4.9 1.6 %collective-permute-start.4 = (bf16[7,256,256]{2,1,0:T(8,128)(2,1)}, bf16[7,256,256]{2,1,0:T(8,128)(2,1)}, u32[]{:S(2)}, u32[]{:S(2)}) collective-permute-start(bf16[7,256,256]{2,1,0:T(8,128)(2,1)} %slice.52), channel_id=1, source_target_pairs={{0,24},{8,0},{1,25},{9,1},{2,26},{10,2},{3,27},{11,3},{4,28},{12,4... | collective-permute-start | bytes 2752520 | tf_op jit(solution)/shard_map/far1/ppermute | solution.py:291
  6.5 0.3 slice.42
  6.8 1.0 slice.53
  7.8 0.8 slice.54
  8.7 1.3 %collective-permute-start.2 = (bf16[2,256,256]{2,1,0:T(8,128)(2,1)S(1)}, bf16[2,256,256]{2,1,0:T(8,128)(2,1)S(1)}, u32[]{:S(2)}, u32[]{:S(2)}) collective-permute-start(bf16[2,256,256]{2,1,0:T(8,128)(2,1)S(1)} %pad_maximum_fusion.1), channel_id=1, source_target_pairs={{24,16},{25,17},{26,18},{27,19},{28,20},{29,21},{30,22},{31,23}} | collective-permute-start | bytes 786440 | tf_op jit(solution)/shard_map/pair/ppermute | solution.py:291
  10.0 1.0 fusion.1
  11.1 9.4 %collective-permute-done.2 = bf16[2,256,256]{2,1,0:T(8,128)(2,1)S(1)} collective-permute-done((bf16[2,256,256]{2,1,0:T(8,128)(2,1)S(1)}, bf16[2,256,256]{2,1,0:T(8,128)(2,1)S(1)}, u32[]{:S(2)}, u32[]{:S(2)}) %collective-permute-start.2) | collective-permute-done | bytes 262176 | tf_op jit(solution)/shard_map/pair/ppermute | solution.py:291
  20.5 0.9 pad_maximum_fusion
  21.4 4.2 %collective-permute-start.3 = (bf16[4,256,256]{2,1,0:T(8,128)(2,1)}, bf16[4,256,256]{2,1,0:T(8,128)(2,1)}, u32[]{:S(2)}, u32[]{:S(2)}) collective-permute-start(bf16[4,256,256]{2,1,0:T(8,128)(2,1)} %pad_maximum_fusion), channel_id=1, source_target_pairs={{0,2},{1,3},{8,10},{9,11},{16,18},{17,19},{24,26},{25,27}} | collective-permute-start | bytes 1572872 | tf_op jit(solution)/shard_map/corner2/ppermute | solution.py:254
  25.6 0.7 collective-permute-start.6
  26.3 7.9 %collective-permute-done.3 = bf16[4,256,256]{2,1,0:T(8,128)(2,1)} collective-permute-done((bf16[4,256,256]{2,1,0:T(8,128)(2,1)}, bf16[4,256,256]{2,1,0:T(8,128)(2,1)}, u32[]{:S(2)}, u32[]{:S(2)}) %collective-permute-start.3) | collective-permute-done | bytes 524320 | tf_op jit(solution)/shard_map/corner2/ppermute | solution.py:254
  34.2 1.9 %broadcast_select_fusion = bf16[4,256,256]{2,1,0:T(8,128)(2,1)} fusion(bf16[4,256,256]{2,1,0:T(8,128)(2,1)} %collective-permute-done.3, bf16[4,256,256]{2,1,0:T(8,128)(2,1)} %pad_maximum_fusion, pred[]{:T(512)S(6)} %ge.7), kind=kLoop, calls=%fused_computation.3 | loop fusion | flops 262144 | bytes 1572865 | tf_op jit(solution)/shard_map/jit(_where)/select_n | solution.py:255
  36.1 2.1 %collective-permute-start.5 = (bf16[4,256,256]{2,1,0:T(8,128)(2,1)}, bf16[4,256,256]{2,1,0:T(8,128)(2,1)}, u32[]{:S(2)}, u32[]{:S(2)}) collective-permute-start(bf16[4,256,256]{2,1,0:T(8,128)(2,1)} %broadcast_select_fusion), channel_id=1, source_target_pairs={{0,4},{1,5},{2,6},{3,7},{8,12},{9,13},{10,14},{11,15},{16,20},{17,... | collective-permute-start | bytes 1572872 | tf_op jit(solution)/shard_map/corner4/ppermute | solution.py:254
  38.2 8.0 %collective-permute-done.5 = bf16[4,256,256]{2,1,0:T(8,128)(2,1)} collective-permute-done((bf16[4,256,256]{2,1,0:T(8,128)(2,1)}, bf16[4,256,256]{2,1,0:T(8,128)(2,1)}, u32[]{:S(2)}, u32[]{:S(2)}) %collective-permute-start.5) | collective-permute-done | bytes 524320 | tf_op jit(solution)/shard_map/corner4/ppermute | solution.py:254
  46.2 1.1 broadcast_select_fusion.1.mine
  47.4 1.3 %collective-permute-start.8 = (bf16[4,256,256]{2,1,0:T(8,128)(2,1)}, bf16[4,256,256]{2,1,0:T(8,128)(2,1)S(1)}, u32[]{:S(2)}, u32[]{:S(2)}) collective-permute-start(bf16[4,256,256]{2,1,0:T(8,128)(2,1)} %get-tuple-element.54), channel_id=1, source_target_pairs={{8,16},{0,8},{9,17},{1,9},{10,18},{2,10},{11,19},{3,11},{12,20},{4... | collective-permute-start | bytes 1572872 | tf_op jit(solution)/shard_map/near4/ppermute | solution.py:291
  48.7 1.3 %collective-permute-start.9 = (bf16[7,256,256]{2,1,0:T(8,128)(2,1)}, bf16[7,256,256]{2,1,0:T(8,128)(2,1)S(1)}, u32[]{:S(2)}, u32[]{:S(2)}) collective-permute-start(bf16[7,256,256]{2,1,0:T(8,128)(2,1)} %collective-permute-done.4.refs_5_.refs_3_), channel_id=1, source_target_pairs={{24,16},{25,17},{26,18},{27,19},{28,20},{29,21},{30,22},{31,23}} | collective-permute-start | bytes 2752520 | tf_op jit(solution)/shard_map/back1/ppermute | solution.py:291
  50.0 1.3 %collective-permute-start.15 = (bf16[3,256,256]{2,1,0:T(8,128)(2,1)}, bf16[3,256,256]{2,1,0:T(8,128)(2,1)S(1)}, u32[]{:S(2)}, u32[]{:S(2)}) collective-permute-start(bf16[3,256,256]{2,1,0:T(8,128)(2,1)} %slice.54), channel_id=1, source_target_pairs={{8,16},{0,8},{9,17},{1,9},{10,18},{2,10},{11,19},{3,11},{12,20},{4... | collective-permute-start | bytes 1179656 | tf_op jit(solution)/shard_map/near1/ppermute | solution.py:291
  51.3 11.2 %first.1 = (bf16[256,256]{1,0:T(8,128)(2,1)S(1)}, bf16[256,256]{1,0:T(8,128)(2,1)S(1)}) custom-call(bf16[4,256,256]{2,1,0:T(8,128)(2,1)S(1)} %broadcast_select_fusion.1.mine, bf16[4,256,256]{2,1,0:T(8,128)(2,1)S(1)} %collective-permute-done.7.other), custom_call_target="tpu_custom_call" | custom-call | tf_op jit(solution)/shard_map/first/pallas_call | solution.py:343
  62.5 1.3 %collective-permute-start.10 = (bf16[4,256,256]{2,1,0:T(8,128)(2,1)}, bf16[4,256,256]{2,1,0:T(8,128)(2,1)S(1)}, u32[]{:S(2)}, u32[]{:S(2)}) collective-permute-start(bf16[4,256,256]{2,1,0:T(8,128)(2,1)} %get-tuple-element.37), channel_id=1, source_target_pairs={{8,16},{0,8},{9,17},{1,9},{10,18},{2,10},{11,19},{3,11},{12,20},{4... | collective-permute-start | bytes 1572872 | tf_op jit(solution)/shard_map/near8/ppermute | solution.py:291
  63.8 6.3 %collective-permute-done.8.refs_2_ = bf16[4,256,256]{2,1,0:T(8,128)(2,1)S(1)} collective-permute-done((bf16[4,256,256]{2,1,0:T(8,128)(2,1)}, bf16[4,256,256]{2,1,0:T(8,128)(2,1)S(1)}, u32[]{:S(2)}, u32[]{:S(2)}) %collective-permute-start.8) | collective-permute-done | bytes 524320 | tf_op jit(solution)/shard_map/near4/ppermute | solution.py:291
  70.1 3.3 %collective-permute-start.13 = (bf16[4,256,256]{2,1,0:T(8,128)(2,1)S(1)}, bf16[4,256,256]{2,1,0:T(8,128)(2,1)S(1)}, u32[]{:S(2)}, u32[]{:S(2)}) collective-permute-start(bf16[4,256,256]{2,1,0:T(8,128)(2,1)S(1)} %collective-permute-done.8.refs_2_), channel_id=1, source_target_pairs={{16,24},{17,25},{18,26},{19,27},{20,28},{21,29},{22,30},{23,31}} | collective-permute-start | bytes 1572872 | tf_op jit(solution)/shard_map/on4/ppermute | solution.py:291
  73.4 1.3 %collective-permute-start.12 = (bf16[8,256,256]{2,1,0:T(8,128)(2,1)S(1)}, bf16[8,256,256]{2,1,0:T(8,128)(2,1)S(1)}, u32[]{:S(2)}, u32[]{:S(2)}) collective-permute-start(bf16[8,256,256]{2,1,0:T(8,128)(2,1)S(1)} %collective-permute-done.6.refs_3_), channel_id=1, source_target_pairs={{24,16},{25,17},{26,18},{27,19},{28,20},{29,21},{30,22},{31,23}} | collective-permute-start | bytes 3145736 | tf_op jit(solution)/shard_map/back8/ppermute | solution.py:291
  74.8 3.8 %collective-permute-done.15.refs_3_ = bf16[3,256,256]{2,1,0:T(8,128)(2,1)S(1)} collective-permute-done((bf16[3,256,256]{2,1,0:T(8,128)(2,1)}, bf16[3,256,256]{2,1,0:T(8,128)(2,1)S(1)}, u32[]{:S(2)}, u32[]{:S(2)}) %collective-permute-start.15) | collective-permute-done | bytes 393248 | tf_op jit(solution)/shard_map/near1/ppermute | solution.py:291
  78.6 1.3 %collective-permute-start.16 = (bf16[3,256,256]{2,1,0:T(8,128)(2,1)S(1)}, bf16[3,256,256]{2,1,0:T(8,128)(2,1)S(1)}, u32[]{:S(2)}, u32[]{:S(2)}) collective-permute-start(bf16[3,256,256]{2,1,0:T(8,128)(2,1)S(1)} %collective-permute-done.15.refs_3_), channel_id=1, source_target_pairs={{16,24},{17,25},{18,26},{19,27},{20,28},{21,29},{22,30},{23,31}} | collective-permute-start | bytes 1179656 | tf_op jit(solution)/shard_map/on1/ppermute | solution.py:291
  79.9 1.0 fusion.2
  80.9 11.6 %second.1 = (bf16[256,256]{1,0:T(8,128)(2,1)S(1)}, bf16[256,256]{1,0:T(8,128)(2,1)S(1)}, bf16[256,256]{1,0:T(8,128)(2,1)S(1)}) custom-call(bf16[256,256]{1,0:T(8,128)(2,1)S(1)} %get-tuple-element.43.x0h.refs_10_.refs_6_.refs_7_, bf16[256,256]{1,0:T(8,128)(2,1)S(1)} %get-tuple-element.34.x0m.refs_11_.refs_7_.refs_8_, ...), custom_call_target="tpu_custom_call" | custom-call | tf_op jit(solution)/shard_map/second/pallas_call | solution.py:351
  92.5 1.5 %copy.9 = bf16[2,1,256,16,1,256]{5,2,3,4,1,0:T(8,128)(2,1)S(1)} copy(bf16[2,1,256,16,1,256]{5,3,4,2,1,0:T(8,128)(2,1)S(1)} %copy-done.1) | data formatting | bytes 8388608 | tf_op jit(solution)/shard_map/optimization_barrier | solution.py:263
  94.0 1.3 %collective-permute-start.14 = (bf16[2,256,256]{2,1,0:T(8,128)(2,1)S(1)}, bf16[2,256,256]{2,1,0:T(8,128)(2,1)S(1)}, u32[]{:S(2)}, u32[]{:S(2)}) collective-permute-start(bf16[2,256,256]{2,1,0:T(8,128)(2,1)S(1)} %get-tuple-element.44), channel_id=1, source_target_pairs={{8,16},{0,8},{9,17},{1,9},{10,18},{2,10},{11,19},{3,11},{12,20},{4... | collective-permute-start | bytes 786440 | tf_op jit(solution)/shard_map/near12/ppermute | solution.py:291
  95.3 1.3 %collective-permute-start.11 = (bf16[2,256,256]{2,1,0:T(8,128)(2,1)S(1)}, bf16[2,256,256]{2,1,0:T(8,128)(2,1)S(1)}, u32[]{:S(2)}, u32[]{:S(2)}) collective-permute-start(bf16[2,256,256]{2,1,0:T(8,128)(2,1)S(1)} %get-tuple-element.38), channel_id=1, source_target_pairs={{8,16},{0,8},{9,17},{1,9},{10,18},{2,10},{11,19},{3,11},{12,20},{4... | collective-permute-start | bytes 786440 | tf_op jit(solution)/shard_map/near14/ppermute | solution.py:291
  96.7 1.3 %collective-permute-start.19 = (bf16[4,256,256]{2,1,0:T(8,128)(2,1)S(1)}, bf16[4,256,256]{2,1,0:T(8,128)(2,1)S(1)}, u32[]{:S(2)}, u32[]{:S(2)}) collective-permute-start(bf16[4,256,256]{2,1,0:T(8,128)(2,1)S(1)} %collective-permute-done.10.refs_2_), channel_id=1, source_target_pairs={{16,24},{17,25},{18,26},{19,27},{20,28},{21,29},{22,30},{23,31}} | collective-permute-start | bytes 1572872 | tf_op jit(solution)/shard_map/on8/ppermute | solution.py:291
  98.0 0.1 slice_bitcast_fusion.refs_1_
  98.1 1.0 rows.1.refs_15_.refs_11_.refs_12_
  99.1 3.8 %update.5.refs_12_ = f32[512,16,2,128]{3,2,1,0:T(2,128)} custom-call(bf16[16,256,256]{2,1,0:T(8,128)(2,1)S(1)} %bitcast.23, bf16[16,256,256]{2,1,0:T(8,128)(2,1)S(1)} %slice_bitcast_fusion.refs_1_, bf16[1,256,256]{2,1,0:T(8,128)(2,1)S(1)} %collective-permute-done.refs_2_, bf16[3,256,256]{2,1,0:T(8,128)(2,1)S(1)} %collective-permute-done.15.refs_3_, ...), custom_call_target="tpu_custom_call" | custom-call | tf_op jit(solution)/shard_map/update/pallas_call | solution.py:226
  102.9 2.3 %collective-permute-done.14.refs_2_.refs_5_ = bf16[2,256,256]{2,1,0:T(8,128)(2,1)S(1)} collective-permute-done((bf16[2,256,256]{2,1,0:T(8,128)(2,1)S(1)}, bf16[2,256,256]{2,1,0:T(8,128)(2,1)S(1)}, u32[]{:S(2)}, u32[]{:S(2)}) %collective-permute-start.14) | collective-permute-done | bytes 262176 | tf_op jit(solution)/shard_map/near12/ppermute | solution.py:291
  105.1 1.3 %collective-permute-start.18 = (bf16[2,256,256]{2,1,0:T(8,128)(2,1)S(1)}, bf16[2,256,256]{2,1,0:T(8,128)(2,1)S(1)}, u32[]{:S(2)}, u32[]{:S(2)}) collective-permute-start(bf16[2,256,256]{2,1,0:T(8,128)(2,1)S(1)} %collective-permute-done.14.refs_2_.refs_5_), channel_id=1, source_target_pairs={{16,24},{17,25},{18,26},{19,27},{20,28},{21,29},{22,30},{23,31}} | collective-permute-start | bytes 786440 | tf_op jit(solution)/shard_map/on12/ppermute | solution.py:291
  106.4 2.9 %update.6.refs_12_ = f32[512,16,2,128]{3,2,1,0:T(2,128)} custom-call(bf16[16,256,256]{2,1,0:T(8,128)(2,1)S(1)} %bitcast.24, bf16[16,256,256]{2,1,0:T(8,128)(2,1)S(1)} %slice_bitcast_fusion.refs_1_, bf16[4,256,256]{2,1,0:T(8,128)(2,1)S(1)} %collective-permute-done.8.refs_2_, ...), custom_call_target="tpu_custom_call", output_to_operand_aliasing={{}: (12, {})} | custom-call | tf_op jit(solution)/shard_map/update/pallas_call | solution.py:226
  109.5 1.3 %collective-permute-start.17 = (bf16[2,256,256]{2,1,0:T(8,128)(2,1)S(1)}, bf16[2,256,256]{2,1,0:T(8,128)(2,1)S(1)}, u32[]{:S(2)}, u32[]{:S(2)}) collective-permute-start(bf16[2,256,256]{2,1,0:T(8,128)(2,1)S(1)} %collective-permute-done.11.refs_2_.refs_5_), channel_id=1, source_target_pairs={{16,24},{17,25},{18,26},{19,27},{20,28},{21,29},{22,30},{23,31}} | collective-permute-start | bytes 786440 | tf_op jit(solution)/shard_map/on14/ppermute | solution.py:291
  110.8 2.9 %update.7.refs_13_ = f32[512,16,2,128]{3,2,1,0:T(2,128)} custom-call(bf16[16,256,256]{2,1,0:T(8,128)(2,1)S(1)} %bitcast.25, bf16[16,256,256]{2,1,0:T(8,128)(2,1)S(1)} %slice_bitcast_fusion.refs_1_, bf16[4,256,256]{2,1,0:T(8,128)(2,1)S(1)} %collective-permute-done.10.refs_2_, ...), custom_call_target="tpu_custom_call", output_to_operand_aliasing={{}: (12, {})} | custom-call | tf_op jit(solution)/shard_map/update/pallas_call | solution.py:226
  113.8 2.1 %collective-permute-done.18.refs_6_ = bf16[2,256,256]{2,1,0:T(8,128)(2,1)S(1)} collective-permute-done((bf16[2,256,256]{2,1,0:T(8,128)(2,1)S(1)}, bf16[2,256,256]{2,1,0:T(8,128)(2,1)S(1)}, u32[]{:S(2)}, u32[]{:S(2)}) %collective-permute-start.18) | collective-permute-done | bytes 262176 | tf_op jit(solution)/shard_map/on12/ppermute | solution.py:291
  115.9 2.2 %update.8.refs_13_ = f32[512,16,2,128]{3,2,1,0:T(2,128)} custom-call(bf16[16,256,256]{2,1,0:T(8,128)(2,1)S(1)} %bitcast.26, bf16[16,256,256]{2,1,0:T(8,128)(2,1)S(1)} %slice_bitcast_fusion.refs_1_, bf16[2,256,256]{2,1,0:T(8,128)(2,1)S(1)} %collective-permute-done.14.refs_2_.refs_5_, ...), custom_call_target="tpu_custom_call", output_to_operand_aliasing={{}: (13, {})} | custom-call | tf_op jit(solution)/shard_map/update/pallas_call | solution.py:226
  118.1 2.5 %collective-permute-done.17.refs_6_ = bf16[2,256,256]{2,1,0:T(8,128)(2,1)S(1)} collective-permute-done((bf16[2,256,256]{2,1,0:T(8,128)(2,1)S(1)}, bf16[2,256,256]{2,1,0:T(8,128)(2,1)S(1)}, u32[]{:S(2)}, u32[]{:S(2)}) %collective-permute-start.17) | collective-permute-done | bytes 262176 | tf_op jit(solution)/shard_map/on14/ppermute | solution.py:291
  120.6 2.2 %update.9 = f32[512,16,2,128]{3,2,1,0:T(2,128)} custom-call(bf16[16,256,256]{2,1,0:T(8,128)(2,1)S(1)} %bitcast.27, bf16[16,256,256]{2,1,0:T(8,128)(2,1)S(1)} %slice_bitcast_fusion.refs_1_, bf16[2,256,256]{2,1,0:T(8,128)(2,1)S(1)} %collective-permute-done.11.refs_2_.refs_5_, ...), custom_call_target="tpu_custom_call", output_to_operand_aliasing={{}: (13, {})} | custom-call | tf_op jit(solution)/shard_map/update/pallas_call | solution.py:226
  (27 shorter events, 0.5 us)
Async XLA Ops:
  0.0 3.2 %slice-start = ((bf16[2,1,256,16,1,256]{5,3,4,2,1,0:T(8,128)(2,1)}), bf16[1,1,256,16,1,256]{5,3,4,2,1,0:T(8,128)(2,1)S(1)}, s32[]{:S(2)}) async-start(bf16[2,1,256,16,1,256]{5,3,4,2,1,0:T(8,128)(2,1)} %param.1), calls=%async_computation | async-start | bytes 4194304 | tf_op jit(solution)/shard_map/slice | solution.py:270
  1.5 5.0 %copy-start = (bf16[2,1,256,16,1,256]{5,3,4,2,1,0:T(8,128)(2,1)S(1)}, bf16[2,1,256,16,1,256]{5,3,4,2,1,0:T(8,128)(2,1)}, u32[]{:S(2)}) copy-start(bf16[2,1,256,16,1,256]{5,3,4,2,1,0:T(8,128)(2,1)} %param.1) | copy-start | bytes 12582916
  1.6 7.1 %collective-permute-start = (bf16[1,256,256]{2,1,0:T(8,128)(2,1)S(1)}, bf16[1,256,256]{2,1,0:T(8,128)(2,1)S(1)}, u32[]{:S(2)}, u32[]{:S(2)}) collective-permute-start(bf16[1,256,256]{2,1,0:T(8,128)(2,1)S(1)} %bitcast.29), channel_id=1, source_target_pairs={{8,24},{0,8},{9,25},{1,9},{10,26},{2,10},{11,27},{3,11},{12,28},{4... | collective-permute-start | bytes 393224 | tf_op jit(solution)/shard_map/corner13/ppermute | solution.py:291
  2.4 6.3 %collective-permute-start.1 = (bf16[1,256,256]{2,1,0:T(8,128)(2,1)S(1)}, bf16[1,256,256]{2,1,0:T(8,128)(2,1)S(1)}, u32[]{:S(2)}, u32[]{:S(2)}) collective-permute-start(bf16[1,256,256]{2,1,0:T(8,128)(2,1)S(1)} %bitcast.30), channel_id=1, source_target_pairs={{0,24},{8,0},{1,25},{9,1},{2,26},{10,2},{3,27},{11,3},{4,28},{12,4... | collective-permute-start | bytes 393224 | tf_op jit(solution)/shard_map/far0/ppermute | solution.py:291
  4.9 31.2 %collective-permute-start.4 = (bf16[7,256,256]{2,1,0:T(8,128)(2,1)}, bf16[7,256,256]{2,1,0:T(8,128)(2,1)}, u32[]{:S(2)}, u32[]{:S(2)}) collective-permute-start(bf16[7,256,256]{2,1,0:T(8,128)(2,1)} %slice.52), channel_id=1, source_target_pairs={{0,24},{8,0},{1,25},{9,1},{2,26},{10,2},{3,27},{11,3},{4,28},{12,4... | collective-permute-start | bytes 2752520 | tf_op jit(solution)/shard_map/far1/ppermute | solution.py:291
  8.7 11.7 %collective-permute-start.2 = (bf16[2,256,256]{2,1,0:T(8,128)(2,1)S(1)}, bf16[2,256,256]{2,1,0:T(8,128)(2,1)S(1)}, u32[]{:S(2)}, u32[]{:S(2)}) collective-permute-start(bf16[2,256,256]{2,1,0:T(8,128)(2,1)S(1)} %pad_maximum_fusion.1), channel_id=1, source_target_pairs={{24,16},{25,17},{26,18},{27,19},{28,20},{29,21},{30,22},{31,23}} | collective-permute-start | bytes 786440 | tf_op jit(solution)/shard_map/pair/ppermute | solution.py:291
  20.5 0.9 copy-start.2
  21.4 12.8 %collective-permute-start.3 = (bf16[4,256,256]{2,1,0:T(8,128)(2,1)}, bf16[4,256,256]{2,1,0:T(8,128)(2,1)}, u32[]{:S(2)}, u32[]{:S(2)}) collective-permute-start(bf16[4,256,256]{2,1,0:T(8,128)(2,1)} %pad_maximum_fusion), channel_id=1, source_target_pairs={{0,2},{1,3},{8,10},{9,11},{16,18},{17,19},{24,26},{25,27}} | collective-permute-start | bytes 1572872 | tf_op jit(solution)/shard_map/corner2/ppermute | solution.py:254
  25.6 21.7 %collective-permute-start.6 = (bf16[8,256,256]{2,1,0:T(8,128)(2,1)}, bf16[8,256,256]{2,1,0:T(8,128)(2,1)S(1)}, u32[]{:S(2)}, u32[]{:S(2)}) collective-permute-start(bf16[8,256,256]{2,1,0:T(8,128)(2,1)} %slice.53), channel_id=1, source_target_pairs={{0,24},{8,0},{1,25},{9,1},{2,26},{10,2},{3,27},{11,3},{4,28},{12,4... | collective-permute-start | bytes 3145736 | tf_op jit(solution)/shard_map/far8/ppermute | solution.py:291
  36.1 10.1 %collective-permute-start.5 = (bf16[4,256,256]{2,1,0:T(8,128)(2,1)}, bf16[4,256,256]{2,1,0:T(8,128)(2,1)}, u32[]{:S(2)}, u32[]{:S(2)}) collective-permute-start(bf16[4,256,256]{2,1,0:T(8,128)(2,1)} %broadcast_select_fusion), channel_id=1, source_target_pairs={{0,4},{1,5},{2,6},{3,7},{8,12},{9,13},{10,14},{11,15},{16,20},{17,... | collective-permute-start | bytes 1572872 | tf_op jit(solution)/shard_map/corner4/ppermute | solution.py:254
  38.2 54.3 %copy-start.1 = (bf16[2,1,256,16,1,256]{5,3,4,2,1,0:T(8,128)(2,1)S(1)}, bf16[2,1,256,16,1,256]{5,3,4,2,1,0:T(8,128)(2,1)}, u32[]{:S(2)}) copy-start(bf16[2,1,256,16,1,256]{5,3,4,2,1,0:T(8,128)(2,1)} %param.1) | copy-start | bytes 12582916
  47.3 4.0 %collective-permute-start.7 = (bf16[4,256,256]{2,1,0:T(8,128)(2,1)S(1)}, bf16[4,256,256]{2,1,0:T(8,128)(2,1)S(1)}, u32[]{:S(2)}, u32[]{:S(2)}) collective-permute-start(bf16[4,256,256]{2,1,0:T(8,128)(2,1)S(1)} %broadcast_select_fusion.1.mine), channel_id=1, source_target_pairs={{0,1},{1,0},{2,3},{3,2},{4,5},{5,4},{6,7},{7,6},{8,9},{9,8},{10,11... | collective-permute-start | bytes 1572872 | tf_op jit(solution)/shard_map/corner1/ppermute | solution.py:259
  47.4 22.7 %collective-permute-start.8 = (bf16[4,256,256]{2,1,0:T(8,128)(2,1)}, bf16[4,256,256]{2,1,0:T(8,128)(2,1)S(1)}, u32[]{:S(2)}, u32[]{:S(2)}) collective-permute-start(bf16[4,256,256]{2,1,0:T(8,128)(2,1)} %get-tuple-element.54), channel_id=1, source_target_pairs={{8,16},{0,8},{9,17},{1,9},{10,18},{2,10},{11,19},{3,11},{12,20},{4... | collective-permute-start | bytes 1572872 | tf_op jit(solution)/shard_map/near4/ppermute | solution.py:291
  48.7 32.2 %collective-permute-start.9 = (bf16[7,256,256]{2,1,0:T(8,128)(2,1)}, bf16[7,256,256]{2,1,0:T(8,128)(2,1)S(1)}, u32[]{:S(2)}, u32[]{:S(2)}) collective-permute-start(bf16[7,256,256]{2,1,0:T(8,128)(2,1)} %collective-permute-done.4.refs_5_.refs_3_), channel_id=1, source_target_pairs={{24,16},{25,17},{26,18},{27,19},{28,20},{29,21},{30,22},{31,23}} | collective-permute-start | bytes 2752520 | tf_op jit(solution)/shard_map/back1/ppermute | solution.py:291
  50.0 28.6 %collective-permute-start.15 = (bf16[3,256,256]{2,1,0:T(8,128)(2,1)}, bf16[3,256,256]{2,1,0:T(8,128)(2,1)S(1)}, u32[]{:S(2)}, u32[]{:S(2)}) collective-permute-start(bf16[3,256,256]{2,1,0:T(8,128)(2,1)} %slice.54), channel_id=1, source_target_pairs={{8,16},{0,8},{9,17},{1,9},{10,18},{2,10},{11,19},{3,11},{12,20},{4... | collective-permute-start | bytes 1179656 | tf_op jit(solution)/shard_map/near1/ppermute | solution.py:291
  62.5 32.8 %collective-permute-start.10 = (bf16[4,256,256]{2,1,0:T(8,128)(2,1)}, bf16[4,256,256]{2,1,0:T(8,128)(2,1)S(1)}, u32[]{:S(2)}, u32[]{:S(2)}) collective-permute-start(bf16[4,256,256]{2,1,0:T(8,128)(2,1)} %get-tuple-element.37), channel_id=1, source_target_pairs={{8,16},{0,8},{9,17},{1,9},{10,18},{2,10},{11,19},{3,11},{12,20},{4... | collective-permute-start | bytes 1572872 | tf_op jit(solution)/shard_map/near8/ppermute | solution.py:291
  70.1 26.5 %collective-permute-start.13 = (bf16[4,256,256]{2,1,0:T(8,128)(2,1)S(1)}, bf16[4,256,256]{2,1,0:T(8,128)(2,1)S(1)}, u32[]{:S(2)}, u32[]{:S(2)}) collective-permute-start(bf16[4,256,256]{2,1,0:T(8,128)(2,1)S(1)} %collective-permute-done.8.refs_2_), channel_id=1, source_target_pairs={{16,24},{17,25},{18,26},{19,27},{20,28},{21,29},{22,30},{23,31}} | collective-permute-start | bytes 1572872 | tf_op jit(solution)/shard_map/on4/ppermute | solution.py:291
  73.4 37.4 %collective-permute-start.12 = (bf16[8,256,256]{2,1,0:T(8,128)(2,1)S(1)}, bf16[8,256,256]{2,1,0:T(8,128)(2,1)S(1)}, u32[]{:S(2)}, u32[]{:S(2)}) collective-permute-start(bf16[8,256,256]{2,1,0:T(8,128)(2,1)S(1)} %collective-permute-done.6.refs_3_), channel_id=1, source_target_pairs={{24,16},{25,17},{26,18},{27,19},{28,20},{29,21},{30,22},{31,23}} | collective-permute-start | bytes 3145736 | tf_op jit(solution)/shard_map/back8/ppermute | solution.py:291
  78.6 20.6 %collective-permute-start.16 = (bf16[3,256,256]{2,1,0:T(8,128)(2,1)S(1)}, bf16[3,256,256]{2,1,0:T(8,128)(2,1)S(1)}, u32[]{:S(2)}, u32[]{:S(2)}) collective-permute-start(bf16[3,256,256]{2,1,0:T(8,128)(2,1)S(1)} %collective-permute-done.15.refs_3_), channel_id=1, source_target_pairs={{16,24},{17,25},{18,26},{19,27},{20,28},{21,29},{22,30},{23,31}} | collective-permute-start | bytes 1179656 | tf_op jit(solution)/shard_map/on1/ppermute | solution.py:291
  94.0 11.1 %collective-permute-start.14 = (bf16[2,256,256]{2,1,0:T(8,128)(2,1)S(1)}, bf16[2,256,256]{2,1,0:T(8,128)(2,1)S(1)}, u32[]{:S(2)}, u32[]{:S(2)}) collective-permute-start(bf16[2,256,256]{2,1,0:T(8,128)(2,1)S(1)} %get-tuple-element.44), channel_id=1, source_target_pairs={{8,16},{0,8},{9,17},{1,9},{10,18},{2,10},{11,19},{3,11},{12,20},{4... | collective-permute-start | bytes 786440 | tf_op jit(solution)/shard_map/near12/ppermute | solution.py:291
  95.3 14.2 %collective-permute-start.11 = (bf16[2,256,256]{2,1,0:T(8,128)(2,1)S(1)}, bf16[2,256,256]{2,1,0:T(8,128)(2,1)S(1)}, u32[]{:S(2)}, u32[]{:S(2)}) collective-permute-start(bf16[2,256,256]{2,1,0:T(8,128)(2,1)S(1)} %get-tuple-element.38), channel_id=1, source_target_pairs={{8,16},{0,8},{9,17},{1,9},{10,18},{2,10},{11,19},{3,11},{12,20},{4... | collective-permute-start | bytes 786440 | tf_op jit(solution)/shard_map/near14/ppermute | solution.py:291
  96.7 14.2 %collective-permute-start.19 = (bf16[4,256,256]{2,1,0:T(8,128)(2,1)S(1)}, bf16[4,256,256]{2,1,0:T(8,128)(2,1)S(1)}, u32[]{:S(2)}, u32[]{:S(2)}) collective-permute-start(bf16[4,256,256]{2,1,0:T(8,128)(2,1)S(1)} %collective-permute-done.10.refs_2_), channel_id=1, source_target_pairs={{16,24},{17,25},{18,26},{19,27},{20,28},{21,29},{22,30},{23,31}} | collective-permute-start | bytes 1572872 | tf_op jit(solution)/shard_map/on8/ppermute | solution.py:291
  105.1 10.7 %collective-permute-start.18 = (bf16[2,256,256]{2,1,0:T(8,128)(2,1)S(1)}, bf16[2,256,256]{2,1,0:T(8,128)(2,1)S(1)}, u32[]{:S(2)}, u32[]{:S(2)}) collective-permute-start(bf16[2,256,256]{2,1,0:T(8,128)(2,1)S(1)} %collective-permute-done.14.refs_2_.refs_5_), channel_id=1, source_target_pairs={{16,24},{17,25},{18,26},{19,27},{20,28},{21,29},{22,30},{23,31}} | collective-permute-start | bytes 786440 | tf_op jit(solution)/shard_map/on12/ppermute | solution.py:291
  109.5 11.0 %collective-permute-start.17 = (bf16[2,256,256]{2,1,0:T(8,128)(2,1)S(1)}, bf16[2,256,256]{2,1,0:T(8,128)(2,1)S(1)}, u32[]{:S(2)}, u32[]{:S(2)}) collective-permute-start(bf16[2,256,256]{2,1,0:T(8,128)(2,1)S(1)} %collective-permute-done.11.refs_2_.refs_5_), channel_id=1, source_target_pairs={{16,24},{17,25},{18,26},{19,27},{20,28},{21,29},{22,30},{23,31}} | collective-permute-start | bytes 786440 | tf_op jit(solution)/shard_map/on14/ppermute | solution.py:291

commit v6 on v5

--- a/solution.py
+++ b/solution.py
@@ -336,7 +336,10 @@
     ready = [cut[s] for s in far_spans + near_spans[:3]]
     for s in far_spans[1:]:
         send_far(s)
-    corners = over_columns("corner", [[], *[[far[s]] for s in far_spans[1:3]]], after(payload, *ready))
+    slab1 = [after(gram, pair)[a, 0, :, :, 0, :].transpose(1, 0, 2) for a in range(1, slots)]
+    gates = [[], *[[far[s]] for s in far_spans[1:3]]]
+    gates[-1] += slab1
+    corners = over_columns("corner", gates, after(payload, *ready))
 
     square = jax.ShapeDtypeStruct((size, size), BF16)
     scratch = [pltpu.VMEM((size, size), F32), pltpu.VMEM((size, size), F32)]
@@ -358,8 +361,6 @@
     panels = jax.ShapeDtypeStruct((slots, size, 2 * size), BF16)
     rows_gate = [d[s] for d, k in ((on, near_spans[2:3]),) for s in k]
     rows = vmem_call(row_factor, panels, [], "rows")(after(x0h, *rows_gate), x0m, x1h, x1m, u01, *corners)
-    slab1 = [after(gram, x1h)[a, 0, :, :, 0, :].transpose(1, 0, 2) for a in range(1, slots)]
-
     def parts(ways, base, width):
         found = []
         for row, pieces in ways.items():

time: 124 us -> 121 us (0.976)
  waiting for transfers between devices: 42.3 us -> 37.3 us
  local copies, waits for them, and re-layouts: 9.11 us -> 10.4 us
    ppermute x2, waiting for transfers between devices: 15.9 us -> 12 us  [over_columns(): lax.ppermute(x, 'col', [(i, i + step) for i in range(step) if i + step <...]
    optimization_barrier x1, local copies, waits for them, and re-layouts: 1.52 us -> 3.7 us  [after(): return lax.optimization_barrier((x, *tokens))[0]]
  transfers between devices with their start and end apart: 20 -> 20, of which waited for: 9 -> 10; matrix products, arithmetic and copies ran while one was open for 9% -> 11% of each run, Pallas kernels for 29% -> 30%
where the time goes in v6:
time: 121 us; the launch traced here: 119 us
  Pallas kernels  37.8 us (31%)
  waiting for transfers between devices  37.3 us (31%)
  starting transfers between devices  29.3 us (24%)
  local copies, waits for them, and re-layouts  10.4 us (9%)
  other arithmetic  3.98 us (3%)
    ppermute x17, waiting for transfers between devices, send(): return lax.ppermute(x, 'row', [p for p in pairs])  25.3 us
    ppermute x17, starting transfers between devices, send(): return lax.ppermute(x, 'row', [p for p in pairs])  23 us
    pallas_call x5, Pallas kernels, update_chunk(): pl.pallas_call(body, in_specs=[any_spec] * n_any + [vmem_spec] * 6 + ([an...  14 us
    ppermute x2, waiting for transfers between devices, over_columns(): lax.ppermute(x, 'col', [(i, i + step) for i in range(step) if i + step <...  12 us
    pallas_call x1, Pallas kernels, local(): vmem_call(second_factor, [square] * 3, scratch, 'second')  11.6 us
    pallas_call x1, Pallas kernels, local(): x0h, x0m = vmem_call(first_factor, [square] * 2, scratch, 'first')(*corners)  11.2 us
    ppermute x2, starting transfers between devices, over_columns(): lax.ppermute(x, 'col', [(i, i + step) for i in range(step) if i + step <...  6.27 us
    slice x5, local copies, waits for them, and re-layouts, local(): cut[start, count] = slab0[start:start + count]  3.92 us
  transfers between devices with their start and end apart: 20, of which 10 were waited for; matrix products, arithmetic and copies ran while one was open for 11% of the time, Pallas kernels for 30%

profile of v6, /device:TPU:16, one launch (start us, length us, event | category | flops | bytes accessed | tf_op | source)
XLA Modules:
  0.0 119.4 jit_solution(18258324055054595170)
XLA Ops:
  0.0 1.5 %slice.40 = bf16[1,1,256,1,1,256]{5,3,4,2,1,0:T(2,128)(2,1)S(1)} slice(bf16[2,1,256,16,1,256]{5,3,4,2,1,0:T(8,128)(2,1)} %param.1), slice={[0:1], [0:1], [0:256], [0:1], [0:1], [0:256]} | slice | bytes 262144 | tf_op jit(solution)/shard_map/slice | solution.py:283
  1.6 0.8 collective-permute-start
  2.4 0.8 collective-permute-start.1
  3.2 0.7 copy.19
  3.9 1.0 slice.52
  4.9 1.6 %collective-permute-start.4 = (bf16[7,256,256]{2,1,0:T(8,128)(2,1)}, bf16[7,256,256]{2,1,0:T(8,128)(2,1)}, u32[]{:S(2)}, u32[]{:S(2)}) collective-permute-start(bf16[7,256,256]{2,1,0:T(8,128)(2,1)} %slice.52), channel_id=1, source_target_pairs={{0,24},{8,0},{1,25},{9,1},{2,26},{10,2},{3,27},{11,3},{4,28},{12,4... | collective-permute-start | bytes 2752520 | tf_op jit(solution)/shard_map/far1/ppermute | solution.py:291
  6.5 0.3 slice.45
  6.8 1.0 slice.56
  7.8 0.8 slice.57
  8.7 1.3 %collective-permute-start.2 = (bf16[2,256,256]{2,1,0:T(8,128)(2,1)S(1)}, bf16[2,256,256]{2,1,0:T(8,128)(2,1)S(1)}, u32[]{:S(2)}, u32[]{:S(2)}) collective-permute-start(bf16[2,256,256]{2,1,0:T(8,128)(2,1)S(1)} %pad_maximum_fusion.1), channel_id=1, source_target_pairs={{24,16},{25,17},{26,18},{27,19},{28,20},{29,21},{30,22},{31,23}} | collective-permute-start | bytes 786440 | tf_op jit(solution)/shard_map/pair/ppermute | solution.py:291
  10.0 1.1 fusion.1
  11.1 9.4 %collective-permute-done.2 = bf16[2,256,256]{2,1,0:T(8,128)(2,1)S(1)} collective-permute-done((bf16[2,256,256]{2,1,0:T(8,128)(2,1)S(1)}, bf16[2,256,256]{2,1,0:T(8,128)(2,1)S(1)}, u32[]{:S(2)}, u32[]{:S(2)}) %collective-permute-start.2) | collective-permute-done | bytes 262176 | tf_op jit(solution)/shard_map/pair/ppermute | solution.py:291
  20.5 0.9 pad_maximum_fusion
  21.4 4.2 %collective-permute-start.3 = (bf16[4,256,256]{2,1,0:T(8,128)(2,1)}, bf16[4,256,256]{2,1,0:T(8,128)(2,1)}, u32[]{:S(2)}, u32[]{:S(2)}) collective-permute-start(bf16[4,256,256]{2,1,0:T(8,128)(2,1)} %pad_maximum_fusion), channel_id=1, source_target_pairs={{0,2},{1,3},{8,10},{9,11},{16,18},{17,19},{24,26},{25,27}} | collective-permute-start | bytes 1572872 | tf_op jit(solution)/shard_map/corner2/ppermute | solution.py:254
  25.6 0.7 collective-permute-start.6
  26.3 7.9 %collective-permute-done.3 = bf16[4,256,256]{2,1,0:T(8,128)(2,1)} collective-permute-done((bf16[4,256,256]{2,1,0:T(8,128)(2,1)}, bf16[4,256,256]{2,1,0:T(8,128)(2,1)}, u32[]{:S(2)}, u32[]{:S(2)}) %collective-permute-start.3) | collective-permute-done | bytes 524320 | tf_op jit(solution)/shard_map/corner2/ppermute | solution.py:254
  34.3 1.9 %broadcast_select_fusion = bf16[4,256,256]{2,1,0:T(8,128)(2,1)} fusion(bf16[4,256,256]{2,1,0:T(8,128)(2,1)} %collective-permute-done.3, bf16[4,256,256]{2,1,0:T(8,128)(2,1)} %pad_maximum_fusion, pred[]{:T(512)S(6)} %ge.7), kind=kLoop, calls=%fused_computation.3 | loop fusion | flops 262144 | bytes 1572865 | tf_op jit(solution)/shard_map/jit(_where)/select_n | solution.py:255
  36.2 2.1 %collective-permute-start.5 = (bf16[4,256,256]{2,1,0:T(8,128)(2,1)}, bf16[4,256,256]{2,1,0:T(8,128)(2,1)}, u32[]{:S(2)}, u32[]{:S(2)}) collective-permute-start(bf16[4,256,256]{2,1,0:T(8,128)(2,1)} %broadcast_select_fusion), channel_id=1, source_target_pairs={{0,4},{1,5},{2,6},{3,7},{8,12},{9,13},{10,14},{11,15},{16,20},{17,... | collective-permute-start | bytes 1572872 | tf_op jit(solution)/shard_map/corner4/ppermute | solution.py:254
  38.2 3.7 %copy.8 = bf16[2,1,256,16,1,256]{5,2,3,4,1,0:T(8,128)(2,1)S(1)} copy(bf16[2,1,256,16,1,256]{5,3,4,2,1,0:T(8,128)(2,1)} %param.1) | data formatting | bytes 8388608 | tf_op jit(solution)/shard_map/optimization_barrier | solution.py:263
  42.1 4.1 %collective-permute-done.5 = bf16[4,256,256]{2,1,0:T(8,128)(2,1)} collective-permute-done((bf16[4,256,256]{2,1,0:T(8,128)(2,1)}, bf16[4,256,256]{2,1,0:T(8,128)(2,1)}, u32[]{:S(2)}, u32[]{:S(2)}) %collective-permute-start.5) | collective-permute-done | bytes 524320 | tf_op jit(solution)/shard_map/corner4/ppermute | solution.py:254
  46.2 1.1 broadcast_select_fusion.1.mine
  47.5 1.3 %collective-permute-start.9 = (bf16[4,256,256]{2,1,0:T(8,128)(2,1)S(1)}, bf16[4,256,256]{2,1,0:T(8,128)(2,1)S(1)}, u32[]{:S(2)}, u32[]{:S(2)}) collective-permute-start(bf16[4,256,256]{2,1,0:T(8,128)(2,1)S(1)} %copy-done.4), channel_id=1, source_target_pairs={{8,16},{0,8},{9,17},{1,9},{10,18},{2,10},{11,19},{3,11},{12,20},{4... | collective-permute-start | bytes 1572872 | tf_op jit(solution)/shard_map/near4/ppermute | solution.py:291
  48.8 1.3 %collective-permute-start.10 = (bf16[7,256,256]{2,1,0:T(8,128)(2,1)}, bf16[7,256,256]{2,1,0:T(8,128)(2,1)S(1)}, u32[]{:S(2)}, u32[]{:S(2)}) collective-permute-start(bf16[7,256,256]{2,1,0:T(8,128)(2,1)} %collective-permute-done.4.refs_5_.refs_3_), channel_id=1, source_target_pairs={{24,16},{25,17},{26,18},{27,19},{28,20},{29,21},{30,22},{31,23}} | collective-permute-start | bytes 2752520 | tf_op jit(solution)/shard_map/back1/ppermute | solution.py:291
  50.1 1.3 %collective-permute-start.15 = (bf16[3,256,256]{2,1,0:T(8,128)(2,1)S(1)}, bf16[3,256,256]{2,1,0:T(8,128)(2,1)S(1)}, u32[]{:S(2)}, u32[]{:S(2)}) collective-permute-start(bf16[3,256,256]{2,1,0:T(8,128)(2,1)S(1)} %copy-done.5), channel_id=1, source_target_pairs={{8,16},{0,8},{9,17},{1,9},{10,18},{2,10},{11,19},{3,11},{12,20},{4... | collective-permute-start | bytes 1179656 | tf_op jit(solution)/shard_map/near1/ppermute | solution.py:291
  51.4 11.2 %first.1 = (bf16[256,256]{1,0:T(8,128)(2,1)S(1)}, bf16[256,256]{1,0:T(8,128)(2,1)S(1)}) custom-call(bf16[4,256,256]{2,1,0:T(8,128)(2,1)S(1)} %broadcast_select_fusion.1.mine, bf16[4,256,256]{2,1,0:T(8,128)(2,1)S(1)} %collective-permute-done.7.other), custom_call_target="tpu_custom_call" | custom-call | tf_op jit(solution)/shard_map/first/pallas_call | solution.py:346
  62.6 1.3 %collective-permute-start.8 = (bf16[4,256,256]{2,1,0:T(8,128)(2,1)S(1)}, bf16[4,256,256]{2,1,0:T(8,128)(2,1)S(1)}, u32[]{:S(2)}, u32[]{:S(2)}) collective-permute-start(bf16[4,256,256]{2,1,0:T(8,128)(2,1)S(1)} %copy-done.3), channel_id=1, source_target_pairs={{8,16},{0,8},{9,17},{1,9},{10,18},{2,10},{11,19},{3,11},{12,20},{4... | collective-permute-start | bytes 1572872 | tf_op jit(solution)/shard_map/near8/ppermute | solution.py:291
  63.9 6.0 %collective-permute-done.9.refs_2_ = bf16[4,256,256]{2,1,0:T(8,128)(2,1)S(1)} collective-permute-done((bf16[4,256,256]{2,1,0:T(8,128)(2,1)S(1)}, bf16[4,256,256]{2,1,0:T(8,128)(2,1)S(1)}, u32[]{:S(2)}, u32[]{:S(2)}) %collective-permute-start.9) | collective-permute-done | bytes 524320 | tf_op jit(solution)/shard_map/near4/ppermute | solution.py:291
  69.9 3.5 %collective-permute-start.13 = (bf16[4,256,256]{2,1,0:T(8,128)(2,1)S(1)}, bf16[4,256,256]{2,1,0:T(8,128)(2,1)S(1)}, u32[]{:S(2)}, u32[]{:S(2)}) collective-permute-start(bf16[4,256,256]{2,1,0:T(8,128)(2,1)S(1)} %collective-permute-done.9.refs_2_), channel_id=1, source_target_pairs={{16,24},{17,25},{18,26},{19,27},{20,28},{21,29},{22,30},{23,31}} | collective-permute-start | bytes 1572872 | tf_op jit(solution)/shard_map/on4/ppermute | solution.py:291
  73.4 1.3 %collective-permute-start.12 = (bf16[8,256,256]{2,1,0:T(8,128)(2,1)S(1)}, bf16[8,256,256]{2,1,0:T(8,128)(2,1)S(1)}, u32[]{:S(2)}, u32[]{:S(2)}) collective-permute-start(bf16[8,256,256]{2,1,0:T(8,128)(2,1)S(1)} %collective-permute-done.6.refs_3_), channel_id=1, source_target_pairs={{24,16},{25,17},{26,18},{27,19},{28,20},{29,21},{30,22},{31,23}} | collective-permute-start | bytes 3145736 | tf_op jit(solution)/shard_map/back8/ppermute | solution.py:291
  74.7 3.6 %collective-permute-done.15.refs_3_ = bf16[3,256,256]{2,1,0:T(8,128)(2,1)S(1)} collective-permute-done((bf16[3,256,256]{2,1,0:T(8,128)(2,1)S(1)}, bf16[3,256,256]{2,1,0:T(8,128)(2,1)S(1)}, u32[]{:S(2)}, u32[]{:S(2)}) %collective-permute-start.15) | collective-permute-done | bytes 393248 | tf_op jit(solution)/shard_map/near1/ppermute | solution.py:291
  78.4 1.3 %collective-permute-start.16 = (bf16[3,256,256]{2,1,0:T(8,128)(2,1)S(1)}, bf16[3,256,256]{2,1,0:T(8,128)(2,1)S(1)}, u32[]{:S(2)}, u32[]{:S(2)}) collective-permute-start(bf16[3,256,256]{2,1,0:T(8,128)(2,1)S(1)} %collective-permute-done.15.refs_3_), channel_id=1, source_target_pairs={{16,24},{17,25},{18,26},{19,27},{20,28},{21,29},{22,30},{23,31}} | collective-permute-start | bytes 1179656 | tf_op jit(solution)/shard_map/on1/ppermute | solution.py:291
  79.7 0.5 collective-permute-done.10.refs_7_.refs_4_
  80.2 11.6 %second.1 = (bf16[256,256]{1,0:T(8,128)(2,1)S(1)}, bf16[256,256]{1,0:T(8,128)(2,1)S(1)}, bf16[256,256]{1,0:T(8,128)(2,1)S(1)}) custom-call(bf16[256,256]{1,0:T(8,128)(2,1)S(1)} %get-tuple-element.43.x0h.refs_10_.refs_6_.refs_7_, bf16[256,256]{1,0:T(8,128)(2,1)S(1)} %get-tuple-element.36.x0m.refs_11_.refs_7_.refs_8_, ...), custom_call_target="tpu_custom_call" | custom-call | tf_op jit(solution)/shard_map/second/pallas_call | solution.py:354
  91.8 1.3 %collective-permute-start.14 = (bf16[2,256,256]{2,1,0:T(8,128)(2,1)S(1)}, bf16[2,256,256]{2,1,0:T(8,128)(2,1)S(1)}, u32[]{:S(2)}, u32[]{:S(2)}) collective-permute-start(bf16[2,256,256]{2,1,0:T(8,128)(2,1)S(1)} %get-tuple-element.44), channel_id=1, source_target_pairs={{8,16},{0,8},{9,17},{1,9},{10,18},{2,10},{11,19},{3,11},{12,20},{4... | collective-permute-start | bytes 786440 | tf_op jit(solution)/shard_map/near12/ppermute | solution.py:291
  93.1 1.3 %collective-permute-start.19 = (bf16[4,256,256]{2,1,0:T(8,128)(2,1)S(1)}, bf16[4,256,256]{2,1,0:T(8,128)(2,1)S(1)}, u32[]{:S(2)}, u32[]{:S(2)}) collective-permute-start(bf16[4,256,256]{2,1,0:T(8,128)(2,1)S(1)} %collective-permute-done.8.refs_2_), channel_id=1, source_target_pairs={{16,24},{17,25},{18,26},{19,27},{20,28},{21,29},{22,30},{23,31}} | collective-permute-start | bytes 1572872 | tf_op jit(solution)/shard_map/on8/ppermute | solution.py:291
  94.5 1.3 %collective-permute-start.11 = (bf16[2,256,256]{2,1,0:T(8,128)(2,1)S(1)}, bf16[2,256,256]{2,1,0:T(8,128)(2,1)S(1)}, u32[]{:S(2)}, u32[]{:S(2)}) collective-permute-start(bf16[2,256,256]{2,1,0:T(8,128)(2,1)S(1)} %get-tuple-element.38), channel_id=1, source_target_pairs={{8,16},{0,8},{9,17},{1,9},{10,18},{2,10},{11,19},{3,11},{12,20},{4... | collective-permute-start | bytes 786440 | tf_op jit(solution)/shard_map/near14/ppermute | solution.py:291
  95.8 1.0 rows.1.refs_15_.refs_11_.refs_12_
  96.8 3.7 %update.5.refs_12_ = f32[512,16,2,128]{3,2,1,0:T(2,128)} custom-call(bf16[16,256,256]{2,1,0:T(8,128)(2,1)S(1)} %bitcast.23, bf16[16,256,256]{2,1,0:T(8,128)(2,1)S(1)} %slice_bitcast_fusion.refs_1_, bf16[1,256,256]{2,1,0:T(8,128)(2,1)S(1)} %collective-permute-done.refs_2_, bf16[3,256,256]{2,1,0:T(8,128)(2,1)S(1)} %collective-permute-done.15.refs_3_, ...), custom_call_target="tpu_custom_call" | custom-call | tf_op jit(solution)/shard_map/update/pallas_call | solution.py:226
  100.5 2.4 %collective-permute-done.14.refs_2_.refs_5_ = bf16[2,256,256]{2,1,0:T(8,128)(2,1)S(1)} collective-permute-done((bf16[2,256,256]{2,1,0:T(8,128)(2,1)S(1)}, bf16[2,256,256]{2,1,0:T(8,128)(2,1)S(1)}, u32[]{:S(2)}, u32[]{:S(2)}) %collective-permute-start.14) | collective-permute-done | bytes 262176 | tf_op jit(solution)/shard_map/near12/ppermute | solution.py:291
  102.9 1.3 %collective-permute-start.18 = (bf16[2,256,256]{2,1,0:T(8,128)(2,1)S(1)}, bf16[2,256,256]{2,1,0:T(8,128)(2,1)S(1)}, u32[]{:S(2)}, u32[]{:S(2)}) collective-permute-start(bf16[2,256,256]{2,1,0:T(8,128)(2,1)S(1)} %collective-permute-done.14.refs_2_.refs_5_), channel_id=1, source_target_pairs={{16,24},{17,25},{18,26},{19,27},{20,28},{21,29},{22,30},{23,31}} | collective-permute-start | bytes 786440 | tf_op jit(solution)/shard_map/on12/ppermute | solution.py:291
  104.2 2.9 %update.6.refs_12_ = f32[512,16,2,128]{3,2,1,0:T(2,128)} custom-call(bf16[16,256,256]{2,1,0:T(8,128)(2,1)S(1)} %bitcast.24, bf16[16,256,256]{2,1,0:T(8,128)(2,1)S(1)} %slice_bitcast_fusion.refs_1_, bf16[4,256,256]{2,1,0:T(8,128)(2,1)S(1)} %collective-permute-done.9.refs_2_, ...), custom_call_target="tpu_custom_call", output_to_operand_aliasing={{}: (12, {})} | custom-call | tf_op jit(solution)/shard_map/update/pallas_call | solution.py:226
  107.1 0.2 collective-permute-done.11.refs_2_.refs_5_
  107.3 1.3 %collective-permute-start.17 = (bf16[2,256,256]{2,1,0:T(8,128)(2,1)S(1)}, bf16[2,256,256]{2,1,0:T(8,128)(2,1)S(1)}, u32[]{:S(2)}, u32[]{:S(2)}) collective-permute-start(bf16[2,256,256]{2,1,0:T(8,128)(2,1)S(1)} %collective-permute-done.11.refs_2_.refs_5_), channel_id=1, source_target_pairs={{16,24},{17,25},{18,26},{19,27},{20,28},{21,29},{22,30},{23,31}} | collective-permute-start | bytes 786440 | tf_op jit(solution)/shard_map/on14/ppermute | solution.py:291
  108.6 2.9 %update.7.refs_13_ = f32[512,16,2,128]{3,2,1,0:T(2,128)} custom-call(bf16[16,256,256]{2,1,0:T(8,128)(2,1)S(1)} %bitcast.25, bf16[16,256,256]{2,1,0:T(8,128)(2,1)S(1)} %slice_bitcast_fusion.refs_1_, bf16[4,256,256]{2,1,0:T(8,128)(2,1)S(1)} %collective-permute-done.8.refs_2_, ...), custom_call_target="tpu_custom_call", output_to_operand_aliasing={{}: (12, {})} | custom-call | tf_op jit(solution)/shard_map/update/pallas_call | solution.py:226
  111.5 0.8 collective-permute-done.18.refs_6_
  112.3 2.2 %update.8.refs_13_ = f32[512,16,2,128]{3,2,1,0:T(2,128)} custom-call(bf16[16,256,256]{2,1,0:T(8,128)(2,1)S(1)} %bitcast.26, bf16[16,256,256]{2,1,0:T(8,128)(2,1)S(1)} %slice_bitcast_fusion.refs_1_, bf16[2,256,256]{2,1,0:T(8,128)(2,1)S(1)} %collective-permute-done.14.refs_2_.refs_5_, ...), custom_call_target="tpu_custom_call", output_to_operand_aliasing={{}: (13, {})} | custom-call | tf_op jit(solution)/shard_map/update/pallas_call | solution.py:226
  114.6 2.5 %collective-permute-done.17.refs_6_ = bf16[2,256,256]{2,1,0:T(8,128)(2,1)S(1)} collective-permute-done((bf16[2,256,256]{2,1,0:T(8,128)(2,1)S(1)}, bf16[2,256,256]{2,1,0:T(8,128)(2,1)S(1)}, u32[]{:S(2)}, u32[]{:S(2)}) %collective-permute-start.17) | collective-permute-done | bytes 262176 | tf_op jit(solution)/shard_map/on14/ppermute | solution.py:291
  117.0 2.2 %update.9 = f32[512,16,2,128]{3,2,1,0:T(2,128)} custom-call(bf16[16,256,256]{2,1,0:T(8,128)(2,1)S(1)} %bitcast.27, bf16[16,256,256]{2,1,0:T(8,128)(2,1)S(1)} %slice_bitcast_fusion.refs_1_, bf16[2,256,256]{2,1,0:T(8,128)(2,1)S(1)} %collective-permute-done.11.refs_2_.refs_5_, ...), custom_call_target="tpu_custom_call", output_to_operand_aliasing={{}: (13, {})} | custom-call | tf_op jit(solution)/shard_map/update/pallas_call | solution.py:226
  (33 shorter events, 0.5 us)
Async XLA Ops:
  0.0 3.2 %slice-start = ((bf16[2,1,256,16,1,256]{5,3,4,2,1,0:T(8,128)(2,1)}), bf16[1,1,256,16,1,256]{5,3,4,2,1,0:T(8,128)(2,1)S(1)}, s32[]{:S(2)}) async-start(bf16[2,1,256,16,1,256]{5,3,4,2,1,0:T(8,128)(2,1)} %param.1), calls=%async_computation | async-start | bytes 4194304 | tf_op jit(solution)/shard_map/slice | solution.py:270
  1.5 4.9 %copy-start = (bf16[2,1,256,16,1,256]{5,3,4,2,1,0:T(8,128)(2,1)S(1)}, bf16[2,1,256,16,1,256]{5,3,4,2,1,0:T(8,128)(2,1)}, u32[]{:S(2)}) copy-start(bf16[2,1,256,16,1,256]{5,3,4,2,1,0:T(8,128)(2,1)} %param.1) | copy-start | bytes 12582916
  1.6 7.1 %collective-permute-start = (bf16[1,256,256]{2,1,0:T(8,128)(2,1)S(1)}, bf16[1,256,256]{2,1,0:T(8,128)(2,1)S(1)}, u32[]{:S(2)}, u32[]{:S(2)}) collective-permute-start(bf16[1,256,256]{2,1,0:T(8,128)(2,1)S(1)} %bitcast.29), channel_id=1, source_target_pairs={{8,24},{0,8},{9,25},{1,9},{10,26},{2,10},{11,27},{3,11},{12,28},{4... | collective-permute-start | bytes 393224 | tf_op jit(solution)/shard_map/corner13/ppermute | solution.py:291
  2.4 6.3 %collective-permute-start.1 = (bf16[1,256,256]{2,1,0:T(8,128)(2,1)S(1)}, bf16[1,256,256]{2,1,0:T(8,128)(2,1)S(1)}, u32[]{:S(2)}, u32[]{:S(2)}) collective-permute-start(bf16[1,256,256]{2,1,0:T(8,128)(2,1)S(1)} %bitcast.30), channel_id=1, source_target_pairs={{0,24},{8,0},{1,25},{9,1},{2,26},{10,2},{3,27},{11,3},{4,28},{12,4... | collective-permute-start | bytes 393224 | tf_op jit(solution)/shard_map/far0/ppermute | solution.py:291
  4.9 31.3 %collective-permute-start.4 = (bf16[7,256,256]{2,1,0:T(8,128)(2,1)}, bf16[7,256,256]{2,1,0:T(8,128)(2,1)}, u32[]{:S(2)}, u32[]{:S(2)}) collective-permute-start(bf16[7,256,256]{2,1,0:T(8,128)(2,1)} %slice.52), channel_id=1, source_target_pairs={{0,24},{8,0},{1,25},{9,1},{2,26},{10,2},{3,27},{11,3},{4,28},{12,4... | collective-permute-start | bytes 2752520 | tf_op jit(solution)/shard_map/far1/ppermute | solution.py:291
  8.7 11.8 %collective-permute-start.2 = (bf16[2,256,256]{2,1,0:T(8,128)(2,1)S(1)}, bf16[2,256,256]{2,1,0:T(8,128)(2,1)S(1)}, u32[]{:S(2)}, u32[]{:S(2)}) collective-permute-start(bf16[2,256,256]{2,1,0:T(8,128)(2,1)S(1)} %pad_maximum_fusion.1), channel_id=1, source_target_pairs={{24,16},{25,17},{26,18},{27,19},{28,20},{29,21},{30,22},{31,23}} | collective-permute-start | bytes 786440 | tf_op jit(solution)/shard_map/pair/ppermute | solution.py:291
  20.5 0.9 copy-start.1
  21.4 12.8 %collective-permute-start.3 = (bf16[4,256,256]{2,1,0:T(8,128)(2,1)}, bf16[4,256,256]{2,1,0:T(8,128)(2,1)}, u32[]{:S(2)}, u32[]{:S(2)}) collective-permute-start(bf16[4,256,256]{2,1,0:T(8,128)(2,1)} %pad_maximum_fusion), channel_id=1, source_target_pairs={{0,2},{1,3},{8,10},{9,11},{16,18},{17,19},{24,26},{25,27}} | collective-permute-start | bytes 1572872 | tf_op jit(solution)/shard_map/corner2/ppermute | solution.py:254
  25.6 21.7 %collective-permute-start.6 = (bf16[8,256,256]{2,1,0:T(8,128)(2,1)}, bf16[8,256,256]{2,1,0:T(8,128)(2,1)S(1)}, u32[]{:S(2)}, u32[]{:S(2)}) collective-permute-start(bf16[8,256,256]{2,1,0:T(8,128)(2,1)} %slice.56), channel_id=1, source_target_pairs={{0,24},{8,0},{1,25},{9,1},{2,26},{10,2},{3,27},{11,3},{4,28},{12,4... | collective-permute-start | bytes 3145736 | tf_op jit(solution)/shard_map/far8/ppermute | solution.py:291
  36.2 10.1 %collective-permute-start.5 = (bf16[4,256,256]{2,1,0:T(8,128)(2,1)}, bf16[4,256,256]{2,1,0:T(8,128)(2,1)}, u32[]{:S(2)}, u32[]{:S(2)}) collective-permute-start(bf16[4,256,256]{2,1,0:T(8,128)(2,1)} %broadcast_select_fusion), channel_id=1, source_target_pairs={{0,4},{1,5},{2,6},{3,7},{8,12},{9,13},{10,14},{11,15},{16,20},{17,... | collective-permute-start | bytes 1572872 | tf_op jit(solution)/shard_map/corner4/ppermute | solution.py:254
  42.0 5.5 %copy-start.4 = (bf16[4,256,256]{2,1,0:T(8,128)(2,1)S(1)}, bf16[4,256,256]{2,1,0:T(8,128)(2,1)}, u32[]{:S(2)}) copy-start(bf16[4,256,256]{2,1,0:T(8,128)(2,1)} %get-tuple-element.53) | copy-start | bytes 1572868
  42.0 8.1 %copy-start.5 = (bf16[3,256,256]{2,1,0:T(8,128)(2,1)S(1)}, bf16[3,256,256]{2,1,0:T(8,128)(2,1)}, u32[]{:S(2)}) copy-start(bf16[3,256,256]{2,1,0:T(8,128)(2,1)} %slice.57) | copy-start | bytes 1179652
  42.0 20.6 %copy-start.3 = (bf16[4,256,256]{2,1,0:T(8,128)(2,1)S(1)}, bf16[4,256,256]{2,1,0:T(8,128)(2,1)}, u32[]{:S(2)}) copy-start(bf16[4,256,256]{2,1,0:T(8,128)(2,1)} %get-tuple-element.34) | copy-start | bytes 1572868
  42.0 53.8 %copy-start.2 = (bf16[2,256,256]{2,1,0:T(8,128)(2,1)S(1)}, bf16[2,256,256]{2,1,0:T(8,128)(2,1)}, u32[]{:S(2)}) copy-start(bf16[2,256,256]{2,1,0:T(8,128)(2,1)} %copy-done.1) | copy-start | bytes 786436
  47.4 4.0 %collective-permute-start.7 = (bf16[4,256,256]{2,1,0:T(8,128)(2,1)S(1)}, bf16[4,256,256]{2,1,0:T(8,128)(2,1)S(1)}, u32[]{:S(2)}, u32[]{:S(2)}) collective-permute-start(bf16[4,256,256]{2,1,0:T(8,128)(2,1)S(1)} %broadcast_select_fusion.1.mine), channel_id=1, source_target_pairs={{0,1},{1,0},{2,3},{3,2},{4,5},{5,4},{6,7},{7,6},{8,9},{9,8},{10,11... | collective-permute-start | bytes 1572872 | tf_op jit(solution)/shard_map/corner1/ppermute | solution.py:259
  47.5 22.5 %collective-permute-start.9 = (bf16[4,256,256]{2,1,0:T(8,128)(2,1)S(1)}, bf16[4,256,256]{2,1,0:T(8,128)(2,1)S(1)}, u32[]{:S(2)}, u32[]{:S(2)}) collective-permute-start(bf16[4,256,256]{2,1,0:T(8,128)(2,1)S(1)} %copy-done.4), channel_id=1, source_target_pairs={{8,16},{0,8},{9,17},{1,9},{10,18},{2,10},{11,19},{3,11},{12,20},{4... | collective-permute-start | bytes 1572872 | tf_op jit(solution)/shard_map/near4/ppermute | solution.py:291
  48.8 31.4 %collective-permute-start.10 = (bf16[7,256,256]{2,1,0:T(8,128)(2,1)}, bf16[7,256,256]{2,1,0:T(8,128)(2,1)S(1)}, u32[]{:S(2)}, u32[]{:S(2)}) collective-permute-start(bf16[7,256,256]{2,1,0:T(8,128)(2,1)} %collective-permute-done.4.refs_5_.refs_3_), channel_id=1, source_target_pairs={{24,16},{25,17},{26,18},{27,19},{28,20},{29,21},{30,22},{31,23}} | collective-permute-start | bytes 2752520 | tf_op jit(solution)/shard_map/back1/ppermute | solution.py:291
  50.1 28.3 %collective-permute-start.15 = (bf16[3,256,256]{2,1,0:T(8,128)(2,1)S(1)}, bf16[3,256,256]{2,1,0:T(8,128)(2,1)S(1)}, u32[]{:S(2)}, u32[]{:S(2)}) collective-permute-start(bf16[3,256,256]{2,1,0:T(8,128)(2,1)S(1)} %copy-done.5), channel_id=1, source_target_pairs={{8,16},{0,8},{9,17},{1,9},{10,18},{2,10},{11,19},{3,11},{12,20},{4... | collective-permute-start | bytes 1179656 | tf_op jit(solution)/shard_map/near1/ppermute | solution.py:291
  62.6 30.5 %collective-permute-start.8 = (bf16[4,256,256]{2,1,0:T(8,128)(2,1)S(1)}, bf16[4,256,256]{2,1,0:T(8,128)(2,1)S(1)}, u32[]{:S(2)}, u32[]{:S(2)}) collective-permute-start(bf16[4,256,256]{2,1,0:T(8,128)(2,1)S(1)} %copy-done.3), channel_id=1, source_target_pairs={{8,16},{0,8},{9,17},{1,9},{10,18},{2,10},{11,19},{3,11},{12,20},{4... | collective-permute-start | bytes 1572872 | tf_op jit(solution)/shard_map/near8/ppermute | solution.py:291
  69.9 24.5 %collective-permute-start.13 = (bf16[4,256,256]{2,1,0:T(8,128)(2,1)S(1)}, bf16[4,256,256]{2,1,0:T(8,128)(2,1)S(1)}, u32[]{:S(2)}, u32[]{:S(2)}) collective-permute-start(bf16[4,256,256]{2,1,0:T(8,128)(2,1)S(1)} %collective-permute-done.9.refs_2_), channel_id=1, source_target_pairs={{16,24},{17,25},{18,26},{19,27},{20,28},{21,29},{22,30},{23,31}} | collective-permute-start | bytes 1572872 | tf_op jit(solution)/shard_map/on4/ppermute | solution.py:291
  73.4 35.2 %collective-permute-start.12 = (bf16[8,256,256]{2,1,0:T(8,128)(2,1)S(1)}, bf16[8,256,256]{2,1,0:T(8,128)(2,1)S(1)}, u32[]{:S(2)}, u32[]{:S(2)}) collective-permute-start(bf16[8,256,256]{2,1,0:T(8,128)(2,1)S(1)} %collective-permute-done.6.refs_3_), channel_id=1, source_target_pairs={{24,16},{25,17},{26,18},{27,19},{28,20},{29,21},{30,22},{31,23}} | collective-permute-start | bytes 3145736 | tf_op jit(solution)/shard_map/back8/ppermute | solution.py:291
  78.4 18.4 %collective-permute-start.16 = (bf16[3,256,256]{2,1,0:T(8,128)(2,1)S(1)}, bf16[3,256,256]{2,1,0:T(8,128)(2,1)S(1)}, u32[]{:S(2)}, u32[]{:S(2)}) collective-permute-start(bf16[3,256,256]{2,1,0:T(8,128)(2,1)S(1)} %collective-permute-done.15.refs_3_), channel_id=1, source_target_pairs={{16,24},{17,25},{18,26},{19,27},{20,28},{21,29},{22,30},{23,31}} | collective-permute-start | bytes 1179656 | tf_op jit(solution)/shard_map/on1/ppermute | solution.py:291
  91.8 11.1 %collective-permute-start.14 = (bf16[2,256,256]{2,1,0:T(8,128)(2,1)S(1)}, bf16[2,256,256]{2,1,0:T(8,128)(2,1)S(1)}, u32[]{:S(2)}, u32[]{:S(2)}) collective-permute-start(bf16[2,256,256]{2,1,0:T(8,128)(2,1)S(1)} %get-tuple-element.44), channel_id=1, source_target_pairs={{8,16},{0,8},{9,17},{1,9},{10,18},{2,10},{11,19},{3,11},{12,20},{4... | collective-permute-start | bytes 786440 | tf_op jit(solution)/shard_map/near12/ppermute | solution.py:291
  93.1 15.5 %collective-permute-start.19 = (bf16[4,256,256]{2,1,0:T(8,128)(2,1)S(1)}, bf16[4,256,256]{2,1,0:T(8,128)(2,1)S(1)}, u32[]{:S(2)}, u32[]{:S(2)}) collective-permute-start(bf16[4,256,256]{2,1,0:T(8,128)(2,1)S(1)} %collective-permute-done.8.refs_2_), channel_id=1, source_target_pairs={{16,24},{17,25},{18,26},{19,27},{20,28},{21,29},{22,30},{23,31}} | collective-permute-start | bytes 1572872 | tf_op jit(solution)/shard_map/on8/ppermute | solution.py:291
  94.5 12.8 %collective-permute-start.11 = (bf16[2,256,256]{2,1,0:T(8,128)(2,1)S(1)}, bf16[2,256,256]{2,1,0:T(8,128)(2,1)S(1)}, u32[]{:S(2)}, u32[]{:S(2)}) collective-permute-start(bf16[2,256,256]{2,1,0:T(8,128)(2,1)S(1)} %get-tuple-element.38), channel_id=1, source_target_pairs={{8,16},{0,8},{9,17},{1,9},{10,18},{2,10},{11,19},{3,11},{12,20},{4... | collective-permute-start | bytes 786440 | tf_op jit(solution)/shard_map/near14/ppermute | solution.py:291
  102.9 9.4 %collective-permute-start.18 = (bf16[2,256,256]{2,1,0:T(8,128)(2,1)S(1)}, bf16[2,256,256]{2,1,0:T(8,128)(2,1)S(1)}, u32[]{:S(2)}, u32[]{:S(2)}) collective-permute-start(bf16[2,256,256]{2,1,0:T(8,128)(2,1)S(1)} %collective-permute-done.14.refs_2_.refs_5_), channel_id=1, source_target_pairs={{16,24},{17,25},{18,26},{19,27},{20,28},{21,29},{22,30},{23,31}} | collective-permute-start | bytes 786440 | tf_op jit(solution)/shard_map/on12/ppermute | solution.py:291
  107.3 9.7 %collective-permute-start.17 = (bf16[2,256,256]{2,1,0:T(8,128)(2,1)S(1)}, bf16[2,256,256]{2,1,0:T(8,128)(2,1)S(1)}, u32[]{:S(2)}, u32[]{:S(2)}) collective-permute-start(bf16[2,256,256]{2,1,0:T(8,128)(2,1)S(1)} %collective-permute-done.11.refs_2_.refs_5_), channel_id=1, source_target_pairs={{16,24},{17,25},{18,26},{19,27},{20,28},{21,29},{22,30},{23,31}} | collective-permute-start | bytes 786440 | tf_op jit(solution)/shard_map/on14/ppermute | solution.py:291

commit v7 on v6

--- a/solution.py
+++ b/solution.py
@@ -57,12 +57,13 @@
 
         return group
 
-    half = groups // 2
-    tiles = tuple(wide[8 * i : 8 * i + 8] for i in range(groups))
-    tiles = lax.fori_loop(0, half, step(groups), tiles)
-    rest = lax.fori_loop(half, groups, step(groups - half), tiles[: groups - half])
-    done = [pltpu.roll(t, 2 * NB - 8 * (groups - half), 1) for t in tiles[groups - half :]]
-    return jnp.concatenate([*done, *rest], axis=0)[:, :NB]
+    tiles, done, phase = tuple(wide[8 * i : 8 * i + 8] for i in range(groups)), [], groups // 4
+    for start in range(0, groups, phase):
+        left = groups - start
+        tiles = lax.fori_loop(start, start + phase, step(left), tiles)
+        done = [pltpu.roll(t, 2 * NB - 8 * phase, 1) for t in done] + list(tiles[left - phase :])
+        tiles = tiles[: left - phase]
+    return jnp.concatenate(done, axis=0)[:, :NB]
 
 
 def eliminate(work, inverse):
@@ -323,7 +324,7 @@
     bottom_piece = jnp.where(my_row == 0, far[corner_span], jnp.where(my_row == 1, corner_piece, on[corner_span]))
     pair = jnp.concatenate([top_piece, bottom_piece])
     got = send("pair", after(pair, *[cut[s] for s in far_spans[1:2]]), (3, 2))
-    back[corner_span], near[corner_span] = got[:1], got[1:]
+    back[corner_span], near[corner_span] = (got, 0), (got, 1)
     pair = jnp.where(my_row == 2, got, pair)
     for row in range(4, n_row):
         got = send(f"pair{row}", pair, (row - 1, row))
@@ -339,6 +340,7 @@
     slab1 = [after(gram, pair)[a, 0, :, :, 0, :].transpose(1, 0, 2) for a in range(1, slots)]
     gates = [[], *[[far[s]] for s in far_spans[1:3]]]
     gates[-1] += slab1
+    gates[1] += [cut[s] for s in near_spans[4:]]
     corners = over_columns("corner", gates, after(payload, *ready))
 
     square = jax.ShapeDtypeStruct((size, size), BF16)
@@ -365,9 +367,10 @@
         found = []
         for row, pieces in ways.items():
             for (start, count), array in sorted(pieces.items(), key=lambda item: item[0]):
+                array, shift = array if isinstance(array, tuple) else (array, 0)
                 lo, hi = max(start, base), min(start + count, base + width)
                 if lo < hi:
-                    found.append((row, array, lo - start, hi - lo))
+                    found.append((row, array, shift + lo - start, hi - lo))
         return found
 
     out = None

time: 121 us -> 121 us (level)
  transfers between devices with their start and end apart: 20 -> 20, of which waited for: 10 -> 10; matrix products, arithmetic and copies ran while one was open for 11% -> 11% of each run, Pallas kernels for 30% -> 29%
where the time goes in v7:
time: 121 us; the launch traced here: 119 us
  Pallas kernels  37.2 us (31%)
  waiting for transfers between devices  37.1 us (31%)
  starting transfers between devices  29.3 us (24%)
  local copies, waits for them, and re-layouts  11.1 us (9%)
  other arithmetic  3.94 us (3%)
    ppermute x17, waiting for transfers between devices, send(): return lax.ppermute(x, 'row', [p for p in pairs])  25.9 us
    ppermute x17, starting transfers between devices, send(): return lax.ppermute(x, 'row', [p for p in pairs])  22.9 us
    pallas_call x5, Pallas kernels, update_chunk(): pl.pallas_call(body, in_specs=[any_spec] * n_any + [vmem_spec] * 6 + ([an...  13.8 us
    pallas_call x1, Pallas kernels, local(): vmem_call(second_factor, [square] * 3, scratch, 'second')  11.4 us
    ppermute x2, waiting for transfers between devices, over_columns(): lax.ppermute(x, 'col', [(i, i + step) for i in range(step) if i + step <...  11.2 us
    pallas_call x1, Pallas kernels, local(): x0h, x0m = vmem_call(first_factor, [square] * 2, scratch, 'first')(*corners)  11 us
    ppermute x2, starting transfers between devices, over_columns(): lax.ppermute(x, 'col', [(i, i + step) for i in range(step) if i + step <...  6.27 us
    slice x5, local copies, waits for them, and re-layouts, local(): cut[start, count] = slab0[start:start + count]  4.69 us
  transfers between devices with their start and end apart: 20, of which 10 were waited for; matrix products, arithmetic and copies ran while one was open for 11% of the time, Pallas kernels for 29%

profile of v7, /device:TPU:16, one launch (start us, length us, event | category | flops | bytes accessed | tf_op | source)
XLA Modules:
  0.0 119.2 jit_solution(7995091966135277294)
XLA Ops:
  0.0 1.5 %slice.34 = bf16[1,1,256,1,1,256]{5,3,4,2,1,0:T(2,128)(2,1)S(1)} slice(bf16[2,1,256,16,1,256]{5,3,4,2,1,0:T(8,128)(2,1)} %param.1), slice={[0:1], [0:1], [0:256], [0:1], [0:1], [0:256]} | slice | bytes 262144 | tf_op jit(solution)/shard_map/slice | solution.py:284
  1.6 0.8 collective-permute-start
  2.4 0.8 collective-permute-start.1
  3.2 0.7 copy.19
  3.9 1.0 slice.44
  4.9 1.6 %collective-permute-start.4 = (bf16[7,256,256]{2,1,0:T(8,128)(2,1)}, bf16[7,256,256]{2,1,0:T(8,128)(2,1)}, u32[]{:S(2)}, u32[]{:S(2)}) collective-permute-start(bf16[7,256,256]{2,1,0:T(8,128)(2,1)} %slice.44), channel_id=1, source_target_pairs={{0,24},{8,0},{1,25},{9,1},{2,26},{10,2},{3,27},{11,3},{4,28},{12,4... | collective-permute-start | bytes 2752520 | tf_op jit(solution)/shard_map/far1/ppermute | solution.py:292
  6.5 0.3 slice.39
  6.8 1.0 slice.48
  7.8 0.8 slice.49
  8.8 1.3 %collective-permute-start.2 = (bf16[2,256,256]{2,1,0:T(8,128)(2,1)S(1)}, bf16[2,256,256]{2,1,0:T(8,128)(2,1)S(1)}, u32[]{:S(2)}, u32[]{:S(2)}) collective-permute-start(bf16[2,256,256]{2,1,0:T(8,128)(2,1)S(1)} %pad_maximum_fusion.1), channel_id=1, source_target_pairs={{24,16},{25,17},{26,18},{27,19},{28,20},{29,21},{30,22},{31,23}} | collective-permute-start | bytes 786440 | tf_op jit(solution)/shard_map/pair/ppermute | solution.py:292
  10.1 1.0 fusion.1
  11.1 9.4 %collective-permute-done.2.refs_6_ = bf16[2,256,256]{2,1,0:T(8,128)(2,1)S(1)} collective-permute-done((bf16[2,256,256]{2,1,0:T(8,128)(2,1)S(1)}, bf16[2,256,256]{2,1,0:T(8,128)(2,1)S(1)}, u32[]{:S(2)}, u32[]{:S(2)}) %collective-permute-start.2) | collective-permute-done | bytes 262176 | tf_op jit(solution)/shard_map/pair/ppermute | solution.py:292
  20.5 0.8 pad_maximum_fusion
  21.4 4.2 %collective-permute-start.3 = (bf16[4,256,256]{2,1,0:T(8,128)(2,1)}, bf16[4,256,256]{2,1,0:T(8,128)(2,1)}, u32[]{:S(2)}, u32[]{:S(2)}) collective-permute-start(bf16[4,256,256]{2,1,0:T(8,128)(2,1)} %pad_maximum_fusion), channel_id=1, source_target_pairs={{0,2},{1,3},{8,10},{9,11},{16,18},{17,19},{24,26},{25,27}} | collective-permute-start | bytes 1572872 | tf_op jit(solution)/shard_map/corner2/ppermute | solution.py:255
  25.6 0.7 collective-permute-start.6
  26.3 0.8 fusion
  27.1 7.1 %collective-permute-done.3 = bf16[4,256,256]{2,1,0:T(8,128)(2,1)} collective-permute-done((bf16[4,256,256]{2,1,0:T(8,128)(2,1)}, bf16[4,256,256]{2,1,0:T(8,128)(2,1)}, u32[]{:S(2)}, u32[]{:S(2)}) %collective-permute-start.3) | collective-permute-done | bytes 524320 | tf_op jit(solution)/shard_map/corner2/ppermute | solution.py:255
  34.2 1.9 %broadcast_select_fusion = bf16[4,256,256]{2,1,0:T(8,128)(2,1)} fusion(bf16[4,256,256]{2,1,0:T(8,128)(2,1)} %collective-permute-done.3, bf16[4,256,256]{2,1,0:T(8,128)(2,1)} %pad_maximum_fusion, pred[]{:T(512)S(6)} %ge.7), kind=kLoop, calls=%fused_computation.3 | loop fusion | flops 262144 | bytes 1572865 | tf_op jit(solution)/shard_map/jit(_where)/select_n | solution.py:256
  36.1 2.1 %collective-permute-start.5 = (bf16[4,256,256]{2,1,0:T(8,128)(2,1)}, bf16[4,256,256]{2,1,0:T(8,128)(2,1)}, u32[]{:S(2)}, u32[]{:S(2)}) collective-permute-start(bf16[4,256,256]{2,1,0:T(8,128)(2,1)} %broadcast_select_fusion), channel_id=1, source_target_pairs={{0,4},{1,5},{2,6},{3,7},{8,12},{9,13},{10,14},{11,15},{16,20},{17,... | collective-permute-start | bytes 1572872 | tf_op jit(solution)/shard_map/corner4/ppermute | solution.py:255
  38.2 3.7 %copy.8 = bf16[2,1,256,16,1,256]{5,2,3,4,1,0:T(8,128)(2,1)S(1)} copy(bf16[2,1,256,16,1,256]{5,3,4,2,1,0:T(8,128)(2,1)} %param.1) | data formatting | bytes 8388608 | tf_op jit(solution)/shard_map/optimization_barrier | solution.py:264
  42.1 4.1 %collective-permute-done.5 = bf16[4,256,256]{2,1,0:T(8,128)(2,1)} collective-permute-done((bf16[4,256,256]{2,1,0:T(8,128)(2,1)}, bf16[4,256,256]{2,1,0:T(8,128)(2,1)}, u32[]{:S(2)}, u32[]{:S(2)}) %collective-permute-start.5) | collective-permute-done | bytes 524320 | tf_op jit(solution)/shard_map/corner4/ppermute | solution.py:255
  46.2 1.1 broadcast_select_fusion.1.mine
  47.4 1.3 %collective-permute-start.9 = (bf16[4,256,256]{2,1,0:T(8,128)(2,1)S(1)}, bf16[4,256,256]{2,1,0:T(8,128)(2,1)S(1)}, u32[]{:S(2)}, u32[]{:S(2)}) collective-permute-start(bf16[4,256,256]{2,1,0:T(8,128)(2,1)S(1)} %copy-done.4), channel_id=1, source_target_pairs={{8,16},{0,8},{9,17},{1,9},{10,18},{2,10},{11,19},{3,11},{12,20},{4... | collective-permute-start | bytes 1572872 | tf_op jit(solution)/shard_map/near4/ppermute | solution.py:292
  48.7 1.3 %collective-permute-start.10 = (bf16[7,256,256]{2,1,0:T(8,128)(2,1)}, bf16[7,256,256]{2,1,0:T(8,128)(2,1)S(1)}, u32[]{:S(2)}, u32[]{:S(2)}) collective-permute-start(bf16[7,256,256]{2,1,0:T(8,128)(2,1)} %collective-permute-done.4.refs_5_.refs_3_), channel_id=1, source_target_pairs={{24,16},{25,17},{26,18},{27,19},{28,20},{29,21},{30,22},{31,23}} | collective-permute-start | bytes 2752520 | tf_op jit(solution)/shard_map/back1/ppermute | solution.py:292
  50.0 1.3 %collective-permute-start.15 = (bf16[3,256,256]{2,1,0:T(8,128)(2,1)S(1)}, bf16[3,256,256]{2,1,0:T(8,128)(2,1)S(1)}, u32[]{:S(2)}, u32[]{:S(2)}) collective-permute-start(bf16[3,256,256]{2,1,0:T(8,128)(2,1)S(1)} %copy-done.5), channel_id=1, source_target_pairs={{8,16},{0,8},{9,17},{1,9},{10,18},{2,10},{11,19},{3,11},{12,20},{4... | collective-permute-start | bytes 1179656 | tf_op jit(solution)/shard_map/near1/ppermute | solution.py:292
  51.3 11.0 %first.1 = (bf16[256,256]{1,0:T(8,128)(2,1)S(1)}, bf16[256,256]{1,0:T(8,128)(2,1)S(1)}) custom-call(bf16[4,256,256]{2,1,0:T(8,128)(2,1)S(1)} %broadcast_select_fusion.1.mine, bf16[4,256,256]{2,1,0:T(8,128)(2,1)S(1)} %collective-permute-done.7.other), custom_call_target="tpu_custom_call" | custom-call | tf_op jit(solution)/shard_map/first/pallas_call | solution.py:348
  62.3 1.3 %collective-permute-start.8 = (bf16[4,256,256]{2,1,0:T(8,128)(2,1)S(1)}, bf16[4,256,256]{2,1,0:T(8,128)(2,1)S(1)}, u32[]{:S(2)}, u32[]{:S(2)}) collective-permute-start(bf16[4,256,256]{2,1,0:T(8,128)(2,1)S(1)} %copy-done.3), channel_id=1, source_target_pairs={{8,16},{0,8},{9,17},{1,9},{10,18},{2,10},{11,19},{3,11},{12,20},{4... | collective-permute-start | bytes 1572872 | tf_op jit(solution)/shard_map/near8/ppermute | solution.py:292
  63.6 6.3 %collective-permute-done.9.refs_2_ = bf16[4,256,256]{2,1,0:T(8,128)(2,1)S(1)} collective-permute-done((bf16[4,256,256]{2,1,0:T(8,128)(2,1)S(1)}, bf16[4,256,256]{2,1,0:T(8,128)(2,1)S(1)}, u32[]{:S(2)}, u32[]{:S(2)}) %collective-permute-start.9) | collective-permute-done | bytes 524320 | tf_op jit(solution)/shard_map/near4/ppermute | solution.py:292
  69.9 3.3 %collective-permute-start.13 = (bf16[4,256,256]{2,1,0:T(8,128)(2,1)S(1)}, bf16[4,256,256]{2,1,0:T(8,128)(2,1)S(1)}, u32[]{:S(2)}, u32[]{:S(2)}) collective-permute-start(bf16[4,256,256]{2,1,0:T(8,128)(2,1)S(1)} %collective-permute-done.9.refs_2_), channel_id=1, source_target_pairs={{16,24},{17,25},{18,26},{19,27},{20,28},{21,29},{22,30},{23,31}} | collective-permute-start | bytes 1572872 | tf_op jit(solution)/shard_map/on4/ppermute | solution.py:292
  73.2 1.3 %collective-permute-start.12 = (bf16[8,256,256]{2,1,0:T(8,128)(2,1)S(1)}, bf16[8,256,256]{2,1,0:T(8,128)(2,1)S(1)}, u32[]{:S(2)}, u32[]{:S(2)}) collective-permute-start(bf16[8,256,256]{2,1,0:T(8,128)(2,1)S(1)} %collective-permute-done.6.refs_3_), channel_id=1, source_target_pairs={{24,16},{25,17},{26,18},{27,19},{28,20},{29,21},{30,22},{31,23}} | collective-permute-start | bytes 3145736 | tf_op jit(solution)/shard_map/back8/ppermute | solution.py:292
  74.5 3.8 %collective-permute-done.15.refs_3_ = bf16[3,256,256]{2,1,0:T(8,128)(2,1)S(1)} collective-permute-done((bf16[3,256,256]{2,1,0:T(8,128)(2,1)S(1)}, bf16[3,256,256]{2,1,0:T(8,128)(2,1)S(1)}, u32[]{:S(2)}, u32[]{:S(2)}) %collective-permute-start.15) | collective-permute-done | bytes 393248 | tf_op jit(solution)/shard_map/near1/ppermute | solution.py:292
  78.3 1.5 %collective-permute-start.16 = (bf16[3,256,256]{2,1,0:T(8,128)(2,1)S(1)}, bf16[3,256,256]{2,1,0:T(8,128)(2,1)S(1)}, u32[]{:S(2)}, u32[]{:S(2)}) collective-permute-start(bf16[3,256,256]{2,1,0:T(8,128)(2,1)S(1)} %collective-permute-done.15.refs_3_), channel_id=1, source_target_pairs={{16,24},{17,25},{18,26},{19,27},{20,28},{21,29},{22,30},{23,31}} | collective-permute-start | bytes 1179656 | tf_op jit(solution)/shard_map/on1/ppermute | solution.py:292
  79.8 0.3 collective-permute-done.10.refs_7_.refs_4_
  80.2 11.4 %second.1 = (bf16[256,256]{1,0:T(8,128)(2,1)S(1)}, bf16[256,256]{1,0:T(8,128)(2,1)S(1)}, bf16[256,256]{1,0:T(8,128)(2,1)S(1)}) custom-call(bf16[256,256]{1,0:T(8,128)(2,1)S(1)} %get-tuple-element.43.x0h.refs_9_.refs_6_.refs_7_, bf16[256,256]{1,0:T(8,128)(2,1)S(1)} %get-tuple-element.36.x0m.refs_10_.refs_7_.refs_8_, ...), custom_call_target="tpu_custom_call" | custom-call | tf_op jit(solution)/shard_map/second/pallas_call | solution.py:356
  91.6 1.3 %collective-permute-start.14 = (bf16[2,256,256]{2,1,0:T(8,128)(2,1)S(1)}, bf16[2,256,256]{2,1,0:T(8,128)(2,1)S(1)}, u32[]{:S(2)}, u32[]{:S(2)}) collective-permute-start(bf16[2,256,256]{2,1,0:T(8,128)(2,1)S(1)} %copy-done.7), channel_id=1, source_target_pairs={{8,16},{0,8},{9,17},{1,9},{10,18},{2,10},{11,19},{3,11},{12,20},{4... | collective-permute-start | bytes 786440 | tf_op jit(solution)/shard_map/near12/ppermute | solution.py:292
  92.9 1.3 %collective-permute-start.19 = (bf16[4,256,256]{2,1,0:T(8,128)(2,1)S(1)}, bf16[4,256,256]{2,1,0:T(8,128)(2,1)S(1)}, u32[]{:S(2)}, u32[]{:S(2)}) collective-permute-start(bf16[4,256,256]{2,1,0:T(8,128)(2,1)S(1)} %collective-permute-done.8.refs_2_), channel_id=1, source_target_pairs={{16,24},{17,25},{18,26},{19,27},{20,28},{21,29},{22,30},{23,31}} | collective-permute-start | bytes 1572872 | tf_op jit(solution)/shard_map/on8/ppermute | solution.py:292
  94.2 1.3 %collective-permute-start.11 = (bf16[2,256,256]{2,1,0:T(8,128)(2,1)S(1)}, bf16[2,256,256]{2,1,0:T(8,128)(2,1)S(1)}, u32[]{:S(2)}, u32[]{:S(2)}) collective-permute-start(bf16[2,256,256]{2,1,0:T(8,128)(2,1)S(1)} %copy-done.6), channel_id=1, source_target_pairs={{8,16},{0,8},{9,17},{1,9},{10,18},{2,10},{11,19},{3,11},{12,20},{4... | collective-permute-start | bytes 786440 | tf_op jit(solution)/shard_map/near14/ppermute | solution.py:292
  95.5 1.0 rows.1.refs_14_.refs_11_.refs_12_
  96.5 3.6 %update.5.refs_12_ = f32[512,16,2,128]{3,2,1,0:T(2,128)} custom-call(bf16[16,256,256]{2,1,0:T(8,128)(2,1)S(1)} %bitcast.23, bf16[16,256,256]{2,1,0:T(8,128)(2,1)S(1)} %slice_bitcast_fusion.refs_1_, bf16[1,256,256]{2,1,0:T(8,128)(2,1)S(1)} %collective-permute-done.refs_2_, bf16[3,256,256]{2,1,0:T(8,128)(2,1)S(1)} %collective-permute-done.15.refs_3_, ...), custom_call_target="tpu_custom_call" | custom-call | tf_op jit(solution)/shard_map/update/pallas_call | solution.py:227
  100.1 2.6 %collective-permute-done.14.refs_2_.refs_5_ = bf16[2,256,256]{2,1,0:T(8,128)(2,1)S(1)} collective-permute-done((bf16[2,256,256]{2,1,0:T(8,128)(2,1)S(1)}, bf16[2,256,256]{2,1,0:T(8,128)(2,1)S(1)}, u32[]{:S(2)}, u32[]{:S(2)}) %collective-permute-start.14) | collective-permute-done | bytes 262176 | tf_op jit(solution)/shard_map/near12/ppermute | solution.py:292
  102.7 1.3 %collective-permute-start.18 = (bf16[2,256,256]{2,1,0:T(8,128)(2,1)S(1)}, bf16[2,256,256]{2,1,0:T(8,128)(2,1)S(1)}, u32[]{:S(2)}, u32[]{:S(2)}) collective-permute-start(bf16[2,256,256]{2,1,0:T(8,128)(2,1)S(1)} %collective-permute-done.14.refs_2_.refs_5_), channel_id=1, source_target_pairs={{16,24},{17,25},{18,26},{19,27},{20,28},{21,29},{22,30},{23,31}} | collective-permute-start | bytes 786440 | tf_op jit(solution)/shard_map/on12/ppermute | solution.py:292
  104.0 2.9 %update.6.refs_12_ = f32[512,16,2,128]{3,2,1,0:T(2,128)} custom-call(bf16[16,256,256]{2,1,0:T(8,128)(2,1)S(1)} %bitcast.24, bf16[16,256,256]{2,1,0:T(8,128)(2,1)S(1)} %slice_bitcast_fusion.refs_1_, bf16[4,256,256]{2,1,0:T(8,128)(2,1)S(1)} %collective-permute-done.9.refs_2_, ...), custom_call_target="tpu_custom_call", output_to_operand_aliasing={{}: (12, {})} | custom-call | tf_op jit(solution)/shard_map/update/pallas_call | solution.py:227
  107.0 1.3 %collective-permute-start.17 = (bf16[2,256,256]{2,1,0:T(8,128)(2,1)S(1)}, bf16[2,256,256]{2,1,0:T(8,128)(2,1)S(1)}, u32[]{:S(2)}, u32[]{:S(2)}) collective-permute-start(bf16[2,256,256]{2,1,0:T(8,128)(2,1)S(1)} %collective-permute-done.11.refs_2_.refs_5_), channel_id=1, source_target_pairs={{16,24},{17,25},{18,26},{19,27},{20,28},{21,29},{22,30},{23,31}} | collective-permute-start | bytes 786440 | tf_op jit(solution)/shard_map/on14/ppermute | solution.py:292
  108.4 2.9 %update.7.refs_13_ = f32[512,16,2,128]{3,2,1,0:T(2,128)} custom-call(bf16[16,256,256]{2,1,0:T(8,128)(2,1)S(1)} %bitcast.25, bf16[16,256,256]{2,1,0:T(8,128)(2,1)S(1)} %slice_bitcast_fusion.refs_1_, bf16[4,256,256]{2,1,0:T(8,128)(2,1)S(1)} %collective-permute-done.8.refs_2_, ...), custom_call_target="tpu_custom_call", output_to_operand_aliasing={{}: (12, {})} | custom-call | tf_op jit(solution)/shard_map/update/pallas_call | solution.py:227
  111.3 0.8 collective-permute-done.18.refs_6_
  112.1 2.2 %update.8.refs_13_ = f32[512,16,2,128]{3,2,1,0:T(2,128)} custom-call(bf16[16,256,256]{2,1,0:T(8,128)(2,1)S(1)} %bitcast.26, bf16[16,256,256]{2,1,0:T(8,128)(2,1)S(1)} %slice_bitcast_fusion.refs_1_, bf16[2,256,256]{2,1,0:T(8,128)(2,1)S(1)} %collective-permute-done.14.refs_2_.refs_5_, ...), custom_call_target="tpu_custom_call", output_to_operand_aliasing={{}: (13, {})} | custom-call | tf_op jit(solution)/shard_map/update/pallas_call | solution.py:227
  114.3 2.5 %collective-permute-done.17.refs_6_ = bf16[2,256,256]{2,1,0:T(8,128)(2,1)S(1)} collective-permute-done((bf16[2,256,256]{2,1,0:T(8,128)(2,1)S(1)}, bf16[2,256,256]{2,1,0:T(8,128)(2,1)S(1)}, u32[]{:S(2)}, u32[]{:S(2)}) %collective-permute-start.17) | collective-permute-done | bytes 262176 | tf_op jit(solution)/shard_map/on14/ppermute | solution.py:292
  116.8 2.2 %update.9 = f32[512,16,2,128]{3,2,1,0:T(2,128)} custom-call(bf16[16,256,256]{2,1,0:T(8,128)(2,1)S(1)} %bitcast.27, bf16[16,256,256]{2,1,0:T(8,128)(2,1)S(1)} %slice_bitcast_fusion.refs_1_, bf16[2,256,256]{2,1,0:T(8,128)(2,1)S(1)} %collective-permute-done.11.refs_2_.refs_5_, ...), custom_call_target="tpu_custom_call", output_to_operand_aliasing={{}: (13, {})} | custom-call | tf_op jit(solution)/shard_map/update/pallas_call | solution.py:227
  (36 shorter events, 0.6 us)
Async XLA Ops:
  0.0 3.2 %slice-start = ((bf16[2,1,256,16,1,256]{5,3,4,2,1,0:T(8,128)(2,1)}), bf16[1,1,256,16,1,256]{5,3,4,2,1,0:T(8,128)(2,1)S(1)}, s32[]{:S(2)}) async-start(bf16[2,1,256,16,1,256]{5,3,4,2,1,0:T(8,128)(2,1)} %param.1), calls=%async_computation | async-start | bytes 4194304 | tf_op jit(solution)/shard_map/slice | solution.py:271
  1.5 4.9 %copy-start.2 = (bf16[2,1,256,16,1,256]{5,3,4,2,1,0:T(8,128)(2,1)S(1)}, bf16[2,1,256,16,1,256]{5,3,4,2,1,0:T(8,128)(2,1)}, u32[]{:S(2)}) copy-start(bf16[2,1,256,16,1,256]{5,3,4,2,1,0:T(8,128)(2,1)} %param.1) | copy-start | bytes 12582916
  1.6 7.1 %collective-permute-start = (bf16[1,256,256]{2,1,0:T(8,128)(2,1)S(1)}, bf16[1,256,256]{2,1,0:T(8,128)(2,1)S(1)}, u32[]{:S(2)}, u32[]{:S(2)}) collective-permute-start(bf16[1,256,256]{2,1,0:T(8,128)(2,1)S(1)} %bitcast.29), channel_id=1, source_target_pairs={{8,24},{0,8},{9,25},{1,9},{10,26},{2,10},{11,27},{3,11},{12,28},{4... | collective-permute-start | bytes 393224 | tf_op jit(solution)/shard_map/corner13/ppermute | solution.py:292
  2.4 6.3 %collective-permute-start.1 = (bf16[1,256,256]{2,1,0:T(8,128)(2,1)S(1)}, bf16[1,256,256]{2,1,0:T(8,128)(2,1)S(1)}, u32[]{:S(2)}, u32[]{:S(2)}) collective-permute-start(bf16[1,256,256]{2,1,0:T(8,128)(2,1)S(1)} %bitcast.30), channel_id=1, source_target_pairs={{0,24},{8,0},{1,25},{9,1},{2,26},{10,2},{3,27},{11,3},{4,28},{12,4... | collective-permute-start | bytes 393224 | tf_op jit(solution)/shard_map/far0/ppermute | solution.py:292
  4.9 31.2 %collective-permute-start.4 = (bf16[7,256,256]{2,1,0:T(8,128)(2,1)}, bf16[7,256,256]{2,1,0:T(8,128)(2,1)}, u32[]{:S(2)}, u32[]{:S(2)}) collective-permute-start(bf16[7,256,256]{2,1,0:T(8,128)(2,1)} %slice.44), channel_id=1, source_target_pairs={{0,24},{8,0},{1,25},{9,1},{2,26},{10,2},{3,27},{11,3},{4,28},{12,4... | collective-permute-start | bytes 2752520 | tf_op jit(solution)/shard_map/far1/ppermute | solution.py:292
  8.7 12.7 %copy-start = (bf16[1,256,256]{2,1,0:T(8,128)(2,1)}, bf16[1,256,256]{2,1,0:T(8,128)(2,1)S(1)}, u32[]{:S(2)}) copy-start(bf16[1,256,256]{2,1,0:T(8,128)(2,1)S(1)} %collective-permute-done.1.refs_4_) | copy-start | bytes 393220
  8.8 11.7 %collective-permute-start.2 = (bf16[2,256,256]{2,1,0:T(8,128)(2,1)S(1)}, bf16[2,256,256]{2,1,0:T(8,128)(2,1)S(1)}, u32[]{:S(2)}, u32[]{:S(2)}) collective-permute-start(bf16[2,256,256]{2,1,0:T(8,128)(2,1)S(1)} %pad_maximum_fusion.1), channel_id=1, source_target_pairs={{24,16},{25,17},{26,18},{27,19},{28,20},{29,21},{30,22},{31,23}} | collective-permute-start | bytes 786440 | tf_op jit(solution)/shard_map/pair/ppermute | solution.py:292
  21.4 12.8 %collective-permute-start.3 = (bf16[4,256,256]{2,1,0:T(8,128)(2,1)}, bf16[4,256,256]{2,1,0:T(8,128)(2,1)}, u32[]{:S(2)}, u32[]{:S(2)}) collective-permute-start(bf16[4,256,256]{2,1,0:T(8,128)(2,1)} %pad_maximum_fusion), channel_id=1, source_target_pairs={{0,2},{1,3},{8,10},{9,11},{16,18},{17,19},{24,26},{25,27}} | collective-permute-start | bytes 1572872 | tf_op jit(solution)/shard_map/corner2/ppermute | solution.py:255
  25.6 21.7 %collective-permute-start.6 = (bf16[8,256,256]{2,1,0:T(8,128)(2,1)}, bf16[8,256,256]{2,1,0:T(8,128)(2,1)S(1)}, u32[]{:S(2)}, u32[]{:S(2)}) collective-permute-start(bf16[8,256,256]{2,1,0:T(8,128)(2,1)} %slice.48), channel_id=1, source_target_pairs={{0,24},{8,0},{1,25},{9,1},{2,26},{10,2},{3,27},{11,3},{4,28},{12,4... | collective-permute-start | bytes 3145736 | tf_op jit(solution)/shard_map/far8/ppermute | solution.py:292
  36.1 10.1 %collective-permute-start.5 = (bf16[4,256,256]{2,1,0:T(8,128)(2,1)}, bf16[4,256,256]{2,1,0:T(8,128)(2,1)}, u32[]{:S(2)}, u32[]{:S(2)}) collective-permute-start(bf16[4,256,256]{2,1,0:T(8,128)(2,1)} %broadcast_select_fusion), channel_id=1, source_target_pairs={{0,4},{1,5},{2,6},{3,7},{8,12},{9,13},{10,14},{11,15},{16,20},{17,... | collective-permute-start | bytes 1572872 | tf_op jit(solution)/shard_map/corner4/ppermute | solution.py:255
  41.9 5.5 %copy-start.4 = (bf16[4,256,256]{2,1,0:T(8,128)(2,1)S(1)}, bf16[4,256,256]{2,1,0:T(8,128)(2,1)}, u32[]{:S(2)}) copy-start(bf16[4,256,256]{2,1,0:T(8,128)(2,1)} %get-tuple-element.53) | copy-start | bytes 1572868
  41.9 8.1 %copy-start.5 = (bf16[3,256,256]{2,1,0:T(8,128)(2,1)S(1)}, bf16[3,256,256]{2,1,0:T(8,128)(2,1)}, u32[]{:S(2)}) copy-start(bf16[3,256,256]{2,1,0:T(8,128)(2,1)} %slice.49) | copy-start | bytes 1179652
  41.9 20.4 %copy-start.3 = (bf16[4,256,256]{2,1,0:T(8,128)(2,1)S(1)}, bf16[4,256,256]{2,1,0:T(8,128)(2,1)}, u32[]{:S(2)}) copy-start(bf16[4,256,256]{2,1,0:T(8,128)(2,1)} %get-tuple-element.34) | copy-start | bytes 1572868
  41.9 49.6 %copy-start.7 = (bf16[2,256,256]{2,1,0:T(8,128)(2,1)S(1)}, bf16[2,256,256]{2,1,0:T(8,128)(2,1)}, u32[]{:S(2)}) copy-start(bf16[2,256,256]{2,1,0:T(8,128)(2,1)} %get-tuple-element.44) | copy-start | bytes 786436
  42.0 52.3 %copy-start.6 = (bf16[2,256,256]{2,1,0:T(8,128)(2,1)S(1)}, bf16[2,256,256]{2,1,0:T(8,128)(2,1)}, u32[]{:S(2)}) copy-start(bf16[2,256,256]{2,1,0:T(8,128)(2,1)} %get-tuple-element.38) | copy-start | bytes 786436
  42.0 54.6 %copy-start.1 = (bf16[1,256,256]{2,1,0:T(8,128)(2,1)S(1)}, bf16[1,256,256]{2,1,0:T(8,128)(2,1)}, u32[]{:S(2)}) copy-start(bf16[1,256,256]{2,1,0:T(8,128)(2,1)} %copy-done) | copy-start | bytes 393220
  47.3 4.0 %collective-permute-start.7 = (bf16[4,256,256]{2,1,0:T(8,128)(2,1)S(1)}, bf16[4,256,256]{2,1,0:T(8,128)(2,1)S(1)}, u32[]{:S(2)}, u32[]{:S(2)}) collective-permute-start(bf16[4,256,256]{2,1,0:T(8,128)(2,1)S(1)} %broadcast_select_fusion.1.mine), channel_id=1, source_target_pairs={{0,1},{1,0},{2,3},{3,2},{4,5},{5,4},{6,7},{7,6},{8,9},{9,8},{10,11... | collective-permute-start | bytes 1572872 | tf_op jit(solution)/shard_map/corner1/ppermute | solution.py:260
  47.4 22.5 %collective-permute-start.9 = (bf16[4,256,256]{2,1,0:T(8,128)(2,1)S(1)}, bf16[4,256,256]{2,1,0:T(8,128)(2,1)S(1)}, u32[]{:S(2)}, u32[]{:S(2)}) collective-permute-start(bf16[4,256,256]{2,1,0:T(8,128)(2,1)S(1)} %copy-done.4), channel_id=1, source_target_pairs={{8,16},{0,8},{9,17},{1,9},{10,18},{2,10},{11,19},{3,11},{12,20},{4... | collective-permute-start | bytes 1572872 | tf_op jit(solution)/shard_map/near4/ppermute | solution.py:292
  48.7 31.5 %collective-permute-start.10 = (bf16[7,256,256]{2,1,0:T(8,128)(2,1)}, bf16[7,256,256]{2,1,0:T(8,128)(2,1)S(1)}, u32[]{:S(2)}, u32[]{:S(2)}) collective-permute-start(bf16[7,256,256]{2,1,0:T(8,128)(2,1)} %collective-permute-done.4.refs_5_.refs_3_), channel_id=1, source_target_pairs={{24,16},{25,17},{26,18},{27,19},{28,20},{29,21},{30,22},{31,23}} | collective-permute-start | bytes 2752520 | tf_op jit(solution)/shard_map/back1/ppermute | solution.py:292
  50.0 28.3 %collective-permute-start.15 = (bf16[3,256,256]{2,1,0:T(8,128)(2,1)S(1)}, bf16[3,256,256]{2,1,0:T(8,128)(2,1)S(1)}, u32[]{:S(2)}, u32[]{:S(2)}) collective-permute-start(bf16[3,256,256]{2,1,0:T(8,128)(2,1)S(1)} %copy-done.5), channel_id=1, source_target_pairs={{8,16},{0,8},{9,17},{1,9},{10,18},{2,10},{11,19},{3,11},{12,20},{4... | collective-permute-start | bytes 1179656 | tf_op jit(solution)/shard_map/near1/ppermute | solution.py:292
  62.3 30.6 %collective-permute-start.8 = (bf16[4,256,256]{2,1,0:T(8,128)(2,1)S(1)}, bf16[4,256,256]{2,1,0:T(8,128)(2,1)S(1)}, u32[]{:S(2)}, u32[]{:S(2)}) collective-permute-start(bf16[4,256,256]{2,1,0:T(8,128)(2,1)S(1)} %copy-done.3), channel_id=1, source_target_pairs={{8,16},{0,8},{9,17},{1,9},{10,18},{2,10},{11,19},{3,11},{12,20},{4... | collective-permute-start | bytes 1572872 | tf_op jit(solution)/shard_map/near8/ppermute | solution.py:292
  69.9 24.3 %collective-permute-start.13 = (bf16[4,256,256]{2,1,0:T(8,128)(2,1)S(1)}, bf16[4,256,256]{2,1,0:T(8,128)(2,1)S(1)}, u32[]{:S(2)}, u32[]{:S(2)}) collective-permute-start(bf16[4,256,256]{2,1,0:T(8,128)(2,1)S(1)} %collective-permute-done.9.refs_2_), channel_id=1, source_target_pairs={{16,24},{17,25},{18,26},{19,27},{20,28},{21,29},{22,30},{23,31}} | collective-permute-start | bytes 1572872 | tf_op jit(solution)/shard_map/on4/ppermute | solution.py:292
  73.2 35.2 %collective-permute-start.12 = (bf16[8,256,256]{2,1,0:T(8,128)(2,1)S(1)}, bf16[8,256,256]{2,1,0:T(8,128)(2,1)S(1)}, u32[]{:S(2)}, u32[]{:S(2)}) collective-permute-start(bf16[8,256,256]{2,1,0:T(8,128)(2,1)S(1)} %collective-permute-done.6.refs_3_), channel_id=1, source_target_pairs={{24,16},{25,17},{26,18},{27,19},{28,20},{29,21},{30,22},{31,23}} | collective-permute-start | bytes 3145736 | tf_op jit(solution)/shard_map/back8/ppermute | solution.py:292
  78.3 18.2 %collective-permute-start.16 = (bf16[3,256,256]{2,1,0:T(8,128)(2,1)S(1)}, bf16[3,256,256]{2,1,0:T(8,128)(2,1)S(1)}, u32[]{:S(2)}, u32[]{:S(2)}) collective-permute-start(bf16[3,256,256]{2,1,0:T(8,128)(2,1)S(1)} %collective-permute-done.15.refs_3_), channel_id=1, source_target_pairs={{16,24},{17,25},{18,26},{19,27},{20,28},{21,29},{22,30},{23,31}} | collective-permute-start | bytes 1179656 | tf_op jit(solution)/shard_map/on1/ppermute | solution.py:292
  91.6 11.1 %collective-permute-start.14 = (bf16[2,256,256]{2,1,0:T(8,128)(2,1)S(1)}, bf16[2,256,256]{2,1,0:T(8,128)(2,1)S(1)}, u32[]{:S(2)}, u32[]{:S(2)}) collective-permute-start(bf16[2,256,256]{2,1,0:T(8,128)(2,1)S(1)} %copy-done.7), channel_id=1, source_target_pairs={{8,16},{0,8},{9,17},{1,9},{10,18},{2,10},{11,19},{3,11},{12,20},{4... | collective-permute-start | bytes 786440 | tf_op jit(solution)/shard_map/near12/ppermute | solution.py:292
  92.9 15.5 %collective-permute-start.19 = (bf16[4,256,256]{2,1,0:T(8,128)(2,1)S(1)}, bf16[4,256,256]{2,1,0:T(8,128)(2,1)S(1)}, u32[]{:S(2)}, u32[]{:S(2)}) collective-permute-start(bf16[4,256,256]{2,1,0:T(8,128)(2,1)S(1)} %collective-permute-done.8.refs_2_), channel_id=1, source_target_pairs={{16,24},{17,25},{18,26},{19,27},{20,28},{21,29},{22,30},{23,31}} | collective-permute-start | bytes 1572872 | tf_op jit(solution)/shard_map/on8/ppermute | solution.py:292
  94.2 12.8 %collective-permute-start.11 = (bf16[2,256,256]{2,1,0:T(8,128)(2,1)S(1)}, bf16[2,256,256]{2,1,0:T(8,128)(2,1)S(1)}, u32[]{:S(2)}, u32[]{:S(2)}) collective-permute-start(bf16[2,256,256]{2,1,0:T(8,128)(2,1)S(1)} %copy-done.6), channel_id=1, source_target_pairs={{8,16},{0,8},{9,17},{1,9},{10,18},{2,10},{11,19},{3,11},{12,20},{4... | collective-permute-start | bytes 786440 | tf_op jit(solution)/shard_map/near14/ppermute | solution.py:292
  102.7 9.4 %collective-permute-start.18 = (bf16[2,256,256]{2,1,0:T(8,128)(2,1)S(1)}, bf16[2,256,256]{2,1,0:T(8,128)(2,1)S(1)}, u32[]{:S(2)}, u32[]{:S(2)}) collective-permute-start(bf16[2,256,256]{2,1,0:T(8,128)(2,1)S(1)} %collective-permute-done.14.refs_2_.refs_5_), channel_id=1, source_target_pairs={{16,24},{17,25},{18,26},{19,27},{20,28},{21,29},{22,30},{23,31}} | collective-permute-start | bytes 786440 | tf_op jit(solution)/shard_map/on12/ppermute | solution.py:292
  107.0 9.7 %collective-permute-start.17 = (bf16[2,256,256]{2,1,0:T(8,128)(2,1)S(1)}, bf16[2,256,256]{2,1,0:T(8,128)(2,1)S(1)}, u32[]{:S(2)}, u32[]{:S(2)}) collective-permute-start(bf16[2,256,256]{2,1,0:T(8,128)(2,1)S(1)} %collective-permute-done.11.refs_2_.refs_5_), channel_id=1, source_target_pairs={{16,24},{17,25},{18,26},{19,27},{20,28},{21,29},{22,30},{23,31}} | collective-permute-start | bytes 786440 | tf_op jit(solution)/shard_map/on14/ppermute | solution.py:292

commit v8 on v7

--- a/solution.py
+++ b/solution.py
@@ -74,13 +74,14 @@
     for j in range(size // NB):
         lo, hi = j * NB, (j + 1) * NB
         own = inverse_factor(work[lo:hi, lo:hi])
-        right = jnp.dot(own, work[lo:hi, :], precision=HIGHEST, preferred_element_type=F32)
-        left = jnp.dot(own, inverse[lo:hi, :], precision=HIGHEST, preferred_element_type=F32)
-        inverse[lo:hi, :] = left
+        cut, top = hi // 128 * 128, -(-hi // 128) * 128
+        left = jnp.dot(own, inverse[lo:hi, :top], precision=HIGHEST, preferred_element_type=F32)
+        inverse[lo:hi, :top] = left
         if hi < size:
-            down = right[:, hi:].T
-            work[hi:, :] -= jnp.dot(down, right, precision=HIGHEST, preferred_element_type=F32)
-            inverse[hi:, :] -= jnp.dot(down, left, precision=HIGHEST, preferred_element_type=F32)
+            right = jnp.dot(own, work[lo:hi, cut:], precision=HIGHEST, preferred_element_type=F32)
+            down = right[:, hi - cut :].T
+            work[hi:, cut:] -= jnp.dot(down, right, precision=HIGHEST, preferred_element_type=F32)
+            inverse[hi:, :top] -= jnp.dot(down, left, precision=HIGHEST, preferred_element_type=F32)
 
 
 def split(x):

time: 121 us -> 120 us (level)
  no operation moved by 1% of the time
where the time goes in v8:
time: 120 us; the launch traced here: 119 us
  waiting for transfers between devices  37.6 us (31%)
  Pallas kernels  36.7 us (31%)
  starting transfers between devices  29 us (24%)
  local copies, waits for them, and re-layouts  11.1 us (9%)
  other arithmetic  3.94 us (3%)
    ppermute x17, waiting for transfers between devices, send(): return lax.ppermute(x, 'row', [p for p in pairs])  26.4 us
    ppermute x17, starting transfers between devices, send(): return lax.ppermute(x, 'row', [p for p in pairs])  22.7 us
    pallas_call x5, Pallas kernels, update_chunk(): pl.pallas_call(body, in_specs=[any_spec] * n_any + [vmem_spec] * 6 + ([an...  13.8 us
    ppermute x2, waiting for transfers between devices, over_columns(): lax.ppermute(x, 'col', [(i, i + step) for i in range(step) if i + step <...  11.2 us
    pallas_call x1, Pallas kernels, local(): vmem_call(second_factor, [square] * 3, scratch, 'second')  11.2 us
    pallas_call x1, Pallas kernels, local(): x0h, x0m = vmem_call(first_factor, [square] * 2, scratch, 'first')(*corners)  10.7 us
    ppermute x2, starting transfers between devices, over_columns(): lax.ppermute(x, 'col', [(i, i + step) for i in range(step) if i + step <...  6.27 us
    slice x5, local copies, waits for them, and re-layouts, local(): cut[start, count] = slab0[start:start + count]  4.69 us
  transfers between devices with their start and end apart: 20, of which 10 were waited for; matrix products, arithmetic and copies ran while one was open for 11% of the time, Pallas kernels for 29%

profile of v8, /device:TPU:16, one launch (start us, length us, event | category | flops | bytes accessed | tf_op | source)
XLA Modules:
  0.0 118.9 jit_solution(17849098148770939494)
XLA Ops:
  0.0 1.5 %slice.34 = bf16[1,1,256,1,1,256]{5,3,4,2,1,0:T(2,128)(2,1)S(1)} slice(bf16[2,1,256,16,1,256]{5,3,4,2,1,0:T(8,128)(2,1)} %param.1), slice={[0:1], [0:1], [0:256], [0:1], [0:1], [0:256]} | slice | bytes 262144 | tf_op jit(solution)/shard_map/slice | solution.py:285
  1.6 0.8 collective-permute-start
  2.4 0.8 collective-permute-start.1
  3.2 0.7 copy.19
  3.9 1.0 slice.44
  4.9 1.6 %collective-permute-start.4 = (bf16[7,256,256]{2,1,0:T(8,128)(2,1)}, bf16[7,256,256]{2,1,0:T(8,128)(2,1)}, u32[]{:S(2)}, u32[]{:S(2)}) collective-permute-start(bf16[7,256,256]{2,1,0:T(8,128)(2,1)} %slice.44), channel_id=1, source_target_pairs={{0,24},{8,0},{1,25},{9,1},{2,26},{10,2},{3,27},{11,3},{4,28},{12,4... | collective-permute-start | bytes 2752520 | tf_op jit(solution)/shard_map/far1/ppermute | solution.py:293
  6.5 0.3 slice.39
  6.8 1.0 slice.48
  7.8 0.8 slice.49
  8.8 1.3 %collective-permute-start.2 = (bf16[2,256,256]{2,1,0:T(8,128)(2,1)S(1)}, bf16[2,256,256]{2,1,0:T(8,128)(2,1)S(1)}, u32[]{:S(2)}, u32[]{:S(2)}) collective-permute-start(bf16[2,256,256]{2,1,0:T(8,128)(2,1)S(1)} %pad_maximum_fusion.1), channel_id=1, source_target_pairs={{24,16},{25,17},{26,18},{27,19},{28,20},{29,21},{30,22},{31,23}} | collective-permute-start | bytes 786440 | tf_op jit(solution)/shard_map/pair/ppermute | solution.py:293
  10.1 1.0 fusion.1
  11.1 9.4 %collective-permute-done.2.refs_6_ = bf16[2,256,256]{2,1,0:T(8,128)(2,1)S(1)} collective-permute-done((bf16[2,256,256]{2,1,0:T(8,128)(2,1)S(1)}, bf16[2,256,256]{2,1,0:T(8,128)(2,1)S(1)}, u32[]{:S(2)}, u32[]{:S(2)}) %collective-permute-start.2) | collective-permute-done | bytes 262176 | tf_op jit(solution)/shard_map/pair/ppermute | solution.py:293
  20.5 0.8 pad_maximum_fusion
  21.4 4.2 %collective-permute-start.3 = (bf16[4,256,256]{2,1,0:T(8,128)(2,1)}, bf16[4,256,256]{2,1,0:T(8,128)(2,1)}, u32[]{:S(2)}, u32[]{:S(2)}) collective-permute-start(bf16[4,256,256]{2,1,0:T(8,128)(2,1)} %pad_maximum_fusion), channel_id=1, source_target_pairs={{0,2},{1,3},{8,10},{9,11},{16,18},{17,19},{24,26},{25,27}} | collective-permute-start | bytes 1572872 | tf_op jit(solution)/shard_map/corner2/ppermute | solution.py:256
  25.6 0.7 collective-permute-start.6
  26.3 0.8 fusion
  27.1 7.1 %collective-permute-done.3 = bf16[4,256,256]{2,1,0:T(8,128)(2,1)} collective-permute-done((bf16[4,256,256]{2,1,0:T(8,128)(2,1)}, bf16[4,256,256]{2,1,0:T(8,128)(2,1)}, u32[]{:S(2)}, u32[]{:S(2)}) %collective-permute-start.3) | collective-permute-done | bytes 524320 | tf_op jit(solution)/shard_map/corner2/ppermute | solution.py:256
  34.2 1.9 %broadcast_select_fusion = bf16[4,256,256]{2,1,0:T(8,128)(2,1)} fusion(bf16[4,256,256]{2,1,0:T(8,128)(2,1)} %collective-permute-done.3, bf16[4,256,256]{2,1,0:T(8,128)(2,1)} %pad_maximum_fusion, pred[]{:T(512)S(6)} %ge.7), kind=kLoop, calls=%fused_computation.3 | loop fusion | flops 262144 | bytes 1572865 | tf_op jit(solution)/shard_map/jit(_where)/select_n | solution.py:257
  36.1 2.1 %collective-permute-start.5 = (bf16[4,256,256]{2,1,0:T(8,128)(2,1)}, bf16[4,256,256]{2,1,0:T(8,128)(2,1)}, u32[]{:S(2)}, u32[]{:S(2)}) collective-permute-start(bf16[4,256,256]{2,1,0:T(8,128)(2,1)} %broadcast_select_fusion), channel_id=1, source_target_pairs={{0,4},{1,5},{2,6},{3,7},{8,12},{9,13},{10,14},{11,15},{16,20},{17,... | collective-permute-start | bytes 1572872 | tf_op jit(solution)/shard_map/corner4/ppermute | solution.py:256
  38.2 3.7 %copy.8 = bf16[2,1,256,16,1,256]{5,2,3,4,1,0:T(8,128)(2,1)S(1)} copy(bf16[2,1,256,16,1,256]{5,3,4,2,1,0:T(8,128)(2,1)} %param.1) | data formatting | bytes 8388608 | tf_op jit(solution)/shard_map/optimization_barrier | solution.py:265
  42.1 4.1 %collective-permute-done.5 = bf16[4,256,256]{2,1,0:T(8,128)(2,1)} collective-permute-done((bf16[4,256,256]{2,1,0:T(8,128)(2,1)}, bf16[4,256,256]{2,1,0:T(8,128)(2,1)}, u32[]{:S(2)}, u32[]{:S(2)}) %collective-permute-start.5) | collective-permute-done | bytes 524320 | tf_op jit(solution)/shard_map/corner4/ppermute | solution.py:256
  46.2 1.1 broadcast_select_fusion.1.mine
  47.4 1.3 %collective-permute-start.9 = (bf16[4,256,256]{2,1,0:T(8,128)(2,1)S(1)}, bf16[4,256,256]{2,1,0:T(8,128)(2,1)S(1)}, u32[]{:S(2)}, u32[]{:S(2)}) collective-permute-start(bf16[4,256,256]{2,1,0:T(8,128)(2,1)S(1)} %copy-done.4), channel_id=1, source_target_pairs={{8,16},{0,8},{9,17},{1,9},{10,18},{2,10},{11,19},{3,11},{12,20},{4... | collective-permute-start | bytes 1572872 | tf_op jit(solution)/shard_map/near4/ppermute | solution.py:293
  48.7 1.3 %collective-permute-start.10 = (bf16[7,256,256]{2,1,0:T(8,128)(2,1)}, bf16[7,256,256]{2,1,0:T(8,128)(2,1)S(1)}, u32[]{:S(2)}, u32[]{:S(2)}) collective-permute-start(bf16[7,256,256]{2,1,0:T(8,128)(2,1)} %collective-permute-done.4.refs_5_.refs_3_), channel_id=1, source_target_pairs={{24,16},{25,17},{26,18},{27,19},{28,20},{29,21},{30,22},{31,23}} | collective-permute-start | bytes 2752520 | tf_op jit(solution)/shard_map/back1/ppermute | solution.py:293
  50.0 1.3 %collective-permute-start.15 = (bf16[3,256,256]{2,1,0:T(8,128)(2,1)S(1)}, bf16[3,256,256]{2,1,0:T(8,128)(2,1)S(1)}, u32[]{:S(2)}, u32[]{:S(2)}) collective-permute-start(bf16[3,256,256]{2,1,0:T(8,128)(2,1)S(1)} %copy-done.5), channel_id=1, source_target_pairs={{8,16},{0,8},{9,17},{1,9},{10,18},{2,10},{11,19},{3,11},{12,20},{4... | collective-permute-start | bytes 1179656 | tf_op jit(solution)/shard_map/near1/ppermute | solution.py:293
  51.3 10.7 %first.1 = (bf16[256,256]{1,0:T(8,128)(2,1)S(1)}, bf16[256,256]{1,0:T(8,128)(2,1)S(1)}) custom-call(bf16[4,256,256]{2,1,0:T(8,128)(2,1)S(1)} %broadcast_select_fusion.1.mine, bf16[4,256,256]{2,1,0:T(8,128)(2,1)S(1)} %collective-permute-done.7.other), custom_call_target="tpu_custom_call" | custom-call | tf_op jit(solution)/shard_map/first/pallas_call | solution.py:349
  62.0 1.3 %collective-permute-start.8 = (bf16[4,256,256]{2,1,0:T(8,128)(2,1)S(1)}, bf16[4,256,256]{2,1,0:T(8,128)(2,1)S(1)}, u32[]{:S(2)}, u32[]{:S(2)}) collective-permute-start(bf16[4,256,256]{2,1,0:T(8,128)(2,1)S(1)} %copy-done.3), channel_id=1, source_target_pairs={{8,16},{0,8},{9,17},{1,9},{10,18},{2,10},{11,19},{3,11},{12,20},{4... | collective-permute-start | bytes 1572872 | tf_op jit(solution)/shard_map/near8/ppermute | solution.py:293
  63.3 6.6 %collective-permute-done.9.refs_2_ = bf16[4,256,256]{2,1,0:T(8,128)(2,1)S(1)} collective-permute-done((bf16[4,256,256]{2,1,0:T(8,128)(2,1)S(1)}, bf16[4,256,256]{2,1,0:T(8,128)(2,1)S(1)}, u32[]{:S(2)}, u32[]{:S(2)}) %collective-permute-start.9) | collective-permute-done | bytes 524320 | tf_op jit(solution)/shard_map/near4/ppermute | solution.py:293
  69.9 3.0 %collective-permute-start.13 = (bf16[4,256,256]{2,1,0:T(8,128)(2,1)S(1)}, bf16[4,256,256]{2,1,0:T(8,128)(2,1)S(1)}, u32[]{:S(2)}, u32[]{:S(2)}) collective-permute-start(bf16[4,256,256]{2,1,0:T(8,128)(2,1)S(1)} %collective-permute-done.9.refs_2_), channel_id=1, source_target_pairs={{16,24},{17,25},{18,26},{19,27},{20,28},{21,29},{22,30},{23,31}} | collective-permute-start | bytes 1572872 | tf_op jit(solution)/shard_map/on4/ppermute | solution.py:293
  72.9 1.3 %collective-permute-start.12 = (bf16[8,256,256]{2,1,0:T(8,128)(2,1)S(1)}, bf16[8,256,256]{2,1,0:T(8,128)(2,1)S(1)}, u32[]{:S(2)}, u32[]{:S(2)}) collective-permute-start(bf16[8,256,256]{2,1,0:T(8,128)(2,1)S(1)} %collective-permute-done.6.refs_3_), channel_id=1, source_target_pairs={{24,16},{25,17},{26,18},{27,19},{28,20},{29,21},{30,22},{31,23}} | collective-permute-start | bytes 3145736 | tf_op jit(solution)/shard_map/back8/ppermute | solution.py:293
  74.2 4.1 %collective-permute-done.15.refs_3_ = bf16[3,256,256]{2,1,0:T(8,128)(2,1)S(1)} collective-permute-done((bf16[3,256,256]{2,1,0:T(8,128)(2,1)S(1)}, bf16[3,256,256]{2,1,0:T(8,128)(2,1)S(1)}, u32[]{:S(2)}, u32[]{:S(2)}) %collective-permute-start.15) | collective-permute-done | bytes 393248 | tf_op jit(solution)/shard_map/near1/ppermute | solution.py:293
  78.3 1.5 %collective-permute-start.16 = (bf16[3,256,256]{2,1,0:T(8,128)(2,1)S(1)}, bf16[3,256,256]{2,1,0:T(8,128)(2,1)S(1)}, u32[]{:S(2)}, u32[]{:S(2)}) collective-permute-start(bf16[3,256,256]{2,1,0:T(8,128)(2,1)S(1)} %collective-permute-done.15.refs_3_), channel_id=1, source_target_pairs={{16,24},{17,25},{18,26},{19,27},{20,28},{21,29},{22,30},{23,31}} | collective-permute-start | bytes 1179656 | tf_op jit(solution)/shard_map/on1/ppermute | solution.py:293
  79.8 0.3 collective-permute-done.10.refs_7_.refs_4_
  80.2 11.2 %second.1 = (bf16[256,256]{1,0:T(8,128)(2,1)S(1)}, bf16[256,256]{1,0:T(8,128)(2,1)S(1)}, bf16[256,256]{1,0:T(8,128)(2,1)S(1)}) custom-call(bf16[256,256]{1,0:T(8,128)(2,1)S(1)} %get-tuple-element.43.x0h.refs_9_.refs_6_.refs_7_, bf16[256,256]{1,0:T(8,128)(2,1)S(1)} %get-tuple-element.36.x0m.refs_10_.refs_7_.refs_8_, ...), custom_call_target="tpu_custom_call" | custom-call | tf_op jit(solution)/shard_map/second/pallas_call | solution.py:357
  91.4 1.3 %collective-permute-start.14 = (bf16[2,256,256]{2,1,0:T(8,128)(2,1)S(1)}, bf16[2,256,256]{2,1,0:T(8,128)(2,1)S(1)}, u32[]{:S(2)}, u32[]{:S(2)}) collective-permute-start(bf16[2,256,256]{2,1,0:T(8,128)(2,1)S(1)} %copy-done.7), channel_id=1, source_target_pairs={{8,16},{0,8},{9,17},{1,9},{10,18},{2,10},{11,19},{3,11},{12,20},{4... | collective-permute-start | bytes 786440 | tf_op jit(solution)/shard_map/near12/ppermute | solution.py:293
  92.7 1.3 %collective-permute-start.19 = (bf16[4,256,256]{2,1,0:T(8,128)(2,1)S(1)}, bf16[4,256,256]{2,1,0:T(8,128)(2,1)S(1)}, u32[]{:S(2)}, u32[]{:S(2)}) collective-permute-start(bf16[4,256,256]{2,1,0:T(8,128)(2,1)S(1)} %collective-permute-done.8.refs_2_), channel_id=1, source_target_pairs={{16,24},{17,25},{18,26},{19,27},{20,28},{21,29},{22,30},{23,31}} | collective-permute-start | bytes 1572872 | tf_op jit(solution)/shard_map/on8/ppermute | solution.py:293
  94.0 1.3 %collective-permute-start.11 = (bf16[2,256,256]{2,1,0:T(8,128)(2,1)S(1)}, bf16[2,256,256]{2,1,0:T(8,128)(2,1)S(1)}, u32[]{:S(2)}, u32[]{:S(2)}) collective-permute-start(bf16[2,256,256]{2,1,0:T(8,128)(2,1)S(1)} %copy-done.6), channel_id=1, source_target_pairs={{8,16},{0,8},{9,17},{1,9},{10,18},{2,10},{11,19},{3,11},{12,20},{4... | collective-permute-start | bytes 786440 | tf_op jit(solution)/shard_map/near14/ppermute | solution.py:293
  95.3 0.9 rows.1.refs_14_.refs_11_.refs_12_
  96.3 3.6 %update.5.refs_12_ = f32[512,16,2,128]{3,2,1,0:T(2,128)} custom-call(bf16[16,256,256]{2,1,0:T(8,128)(2,1)S(1)} %bitcast.23, bf16[16,256,256]{2,1,0:T(8,128)(2,1)S(1)} %slice_bitcast_fusion.refs_1_, bf16[1,256,256]{2,1,0:T(8,128)(2,1)S(1)} %collective-permute-done.refs_2_, bf16[3,256,256]{2,1,0:T(8,128)(2,1)S(1)} %collective-permute-done.15.refs_3_, ...), custom_call_target="tpu_custom_call" | custom-call | tf_op jit(solution)/shard_map/update/pallas_call | solution.py:228
  99.9 2.6 %collective-permute-done.14.refs_2_.refs_5_ = bf16[2,256,256]{2,1,0:T(8,128)(2,1)S(1)} collective-permute-done((bf16[2,256,256]{2,1,0:T(8,128)(2,1)S(1)}, bf16[2,256,256]{2,1,0:T(8,128)(2,1)S(1)}, u32[]{:S(2)}, u32[]{:S(2)}) %collective-permute-start.14) | collective-permute-done | bytes 262176 | tf_op jit(solution)/shard_map/near12/ppermute | solution.py:293
  102.5 1.3 %collective-permute-start.18 = (bf16[2,256,256]{2,1,0:T(8,128)(2,1)S(1)}, bf16[2,256,256]{2,1,0:T(8,128)(2,1)S(1)}, u32[]{:S(2)}, u32[]{:S(2)}) collective-permute-start(bf16[2,256,256]{2,1,0:T(8,128)(2,1)S(1)} %collective-permute-done.14.refs_2_.refs_5_), channel_id=1, source_target_pairs={{16,24},{17,25},{18,26},{19,27},{20,28},{21,29},{22,30},{23,31}} | collective-permute-start | bytes 786440 | tf_op jit(solution)/shard_map/on12/ppermute | solution.py:293
  103.8 2.9 %update.6.refs_12_ = f32[512,16,2,128]{3,2,1,0:T(2,128)} custom-call(bf16[16,256,256]{2,1,0:T(8,128)(2,1)S(1)} %bitcast.24, bf16[16,256,256]{2,1,0:T(8,128)(2,1)S(1)} %slice_bitcast_fusion.refs_1_, bf16[4,256,256]{2,1,0:T(8,128)(2,1)S(1)} %collective-permute-done.9.refs_2_, ...), custom_call_target="tpu_custom_call", output_to_operand_aliasing={{}: (12, {})} | custom-call | tf_op jit(solution)/shard_map/update/pallas_call | solution.py:228
  106.8 1.3 %collective-permute-start.17 = (bf16[2,256,256]{2,1,0:T(8,128)(2,1)S(1)}, bf16[2,256,256]{2,1,0:T(8,128)(2,1)S(1)}, u32[]{:S(2)}, u32[]{:S(2)}) collective-permute-start(bf16[2,256,256]{2,1,0:T(8,128)(2,1)S(1)} %collective-permute-done.11.refs_2_.refs_5_), channel_id=1, source_target_pairs={{16,24},{17,25},{18,26},{19,27},{20,28},{21,29},{22,30},{23,31}} | collective-permute-start | bytes 786440 | tf_op jit(solution)/shard_map/on14/ppermute | solution.py:293
  108.1 2.9 %update.7.refs_13_ = f32[512,16,2,128]{3,2,1,0:T(2,128)} custom-call(bf16[16,256,256]{2,1,0:T(8,128)(2,1)S(1)} %bitcast.25, bf16[16,256,256]{2,1,0:T(8,128)(2,1)S(1)} %slice_bitcast_fusion.refs_1_, bf16[4,256,256]{2,1,0:T(8,128)(2,1)S(1)} %collective-permute-done.8.refs_2_, ...), custom_call_target="tpu_custom_call", output_to_operand_aliasing={{}: (12, {})} | custom-call | tf_op jit(solution)/shard_map/update/pallas_call | solution.py:228
  111.1 0.8 collective-permute-done.18.refs_6_
  111.9 2.2 %update.8.refs_13_ = f32[512,16,2,128]{3,2,1,0:T(2,128)} custom-call(bf16[16,256,256]{2,1,0:T(8,128)(2,1)S(1)} %bitcast.26, bf16[16,256,256]{2,1,0:T(8,128)(2,1)S(1)} %slice_bitcast_fusion.refs_1_, bf16[2,256,256]{2,1,0:T(8,128)(2,1)S(1)} %collective-permute-done.14.refs_2_.refs_5_, ...), custom_call_target="tpu_custom_call", output_to_operand_aliasing={{}: (13, {})} | custom-call | tf_op jit(solution)/shard_map/update/pallas_call | solution.py:228
  114.1 2.5 %collective-permute-done.17.refs_6_ = bf16[2,256,256]{2,1,0:T(8,128)(2,1)S(1)} collective-permute-done((bf16[2,256,256]{2,1,0:T(8,128)(2,1)S(1)}, bf16[2,256,256]{2,1,0:T(8,128)(2,1)S(1)}, u32[]{:S(2)}, u32[]{:S(2)}) %collective-permute-start.17) | collective-permute-done | bytes 262176 | tf_op jit(solution)/shard_map/on14/ppermute | solution.py:293
  116.6 2.2 %update.9 = f32[512,16,2,128]{3,2,1,0:T(2,128)} custom-call(bf16[16,256,256]{2,1,0:T(8,128)(2,1)S(1)} %bitcast.27, bf16[16,256,256]{2,1,0:T(8,128)(2,1)S(1)} %slice_bitcast_fusion.refs_1_, bf16[2,256,256]{2,1,0:T(8,128)(2,1)S(1)} %collective-permute-done.11.refs_2_.refs_5_, ...), custom_call_target="tpu_custom_call", output_to_operand_aliasing={{}: (13, {})} | custom-call | tf_op jit(solution)/shard_map/update/pallas_call | solution.py:228
  (36 shorter events, 0.6 us)
Async XLA Ops:
  0.0 3.2 %slice-start = ((bf16[2,1,256,16,1,256]{5,3,4,2,1,0:T(8,128)(2,1)}), bf16[1,1,256,16,1,256]{5,3,4,2,1,0:T(8,128)(2,1)S(1)}, s32[]{:S(2)}) async-start(bf16[2,1,256,16,1,256]{5,3,4,2,1,0:T(8,128)(2,1)} %param.1), calls=%async_computation | async-start | bytes 4194304 | tf_op jit(solution)/shard_map/slice | solution.py:272
  1.5 4.9 %copy-start.2 = (bf16[2,1,256,16,1,256]{5,3,4,2,1,0:T(8,128)(2,1)S(1)}, bf16[2,1,256,16,1,256]{5,3,4,2,1,0:T(8,128)(2,1)}, u32[]{:S(2)}) copy-start(bf16[2,1,256,16,1,256]{5,3,4,2,1,0:T(8,128)(2,1)} %param.1) | copy-start | bytes 12582916
  1.6 7.1 %collective-permute-start = (bf16[1,256,256]{2,1,0:T(8,128)(2,1)S(1)}, bf16[1,256,256]{2,1,0:T(8,128)(2,1)S(1)}, u32[]{:S(2)}, u32[]{:S(2)}) collective-permute-start(bf16[1,256,256]{2,1,0:T(8,128)(2,1)S(1)} %bitcast.29), channel_id=1, source_target_pairs={{8,24},{0,8},{9,25},{1,9},{10,26},{2,10},{11,27},{3,11},{12,28},{4... | collective-permute-start | bytes 393224 | tf_op jit(solution)/shard_map/corner13/ppermute | solution.py:293
  2.4 6.3 %collective-permute-start.1 = (bf16[1,256,256]{2,1,0:T(8,128)(2,1)S(1)}, bf16[1,256,256]{2,1,0:T(8,128)(2,1)S(1)}, u32[]{:S(2)}, u32[]{:S(2)}) collective-permute-start(bf16[1,256,256]{2,1,0:T(8,128)(2,1)S(1)} %bitcast.30), channel_id=1, source_target_pairs={{0,24},{8,0},{1,25},{9,1},{2,26},{10,2},{3,27},{11,3},{4,28},{12,4... | collective-permute-start | bytes 393224 | tf_op jit(solution)/shard_map/far0/ppermute | solution.py:293
  4.9 31.2 %collective-permute-start.4 = (bf16[7,256,256]{2,1,0:T(8,128)(2,1)}, bf16[7,256,256]{2,1,0:T(8,128)(2,1)}, u32[]{:S(2)}, u32[]{:S(2)}) collective-permute-start(bf16[7,256,256]{2,1,0:T(8,128)(2,1)} %slice.44), channel_id=1, source_target_pairs={{0,24},{8,0},{1,25},{9,1},{2,26},{10,2},{3,27},{11,3},{4,28},{12,4... | collective-permute-start | bytes 2752520 | tf_op jit(solution)/shard_map/far1/ppermute | solution.py:293
  8.7 12.7 %copy-start = (bf16[1,256,256]{2,1,0:T(8,128)(2,1)}, bf16[1,256,256]{2,1,0:T(8,128)(2,1)S(1)}, u32[]{:S(2)}) copy-start(bf16[1,256,256]{2,1,0:T(8,128)(2,1)S(1)} %collective-permute-done.1.refs_4_) | copy-start | bytes 393220
  8.8 11.7 %collective-permute-start.2 = (bf16[2,256,256]{2,1,0:T(8,128)(2,1)S(1)}, bf16[2,256,256]{2,1,0:T(8,128)(2,1)S(1)}, u32[]{:S(2)}, u32[]{:S(2)}) collective-permute-start(bf16[2,256,256]{2,1,0:T(8,128)(2,1)S(1)} %pad_maximum_fusion.1), channel_id=1, source_target_pairs={{24,16},{25,17},{26,18},{27,19},{28,20},{29,21},{30,22},{31,23}} | collective-permute-start | bytes 786440 | tf_op jit(solution)/shard_map/pair/ppermute | solution.py:293
  21.4 12.8 %collective-permute-start.3 = (bf16[4,256,256]{2,1,0:T(8,128)(2,1)}, bf16[4,256,256]{2,1,0:T(8,128)(2,1)}, u32[]{:S(2)}, u32[]{:S(2)}) collective-permute-start(bf16[4,256,256]{2,1,0:T(8,128)(2,1)} %pad_maximum_fusion), channel_id=1, source_target_pairs={{0,2},{1,3},{8,10},{9,11},{16,18},{17,19},{24,26},{25,27}} | collective-permute-start | bytes 1572872 | tf_op jit(solution)/shard_map/corner2/ppermute | solution.py:256
  25.6 21.7 %collective-permute-start.6 = (bf16[8,256,256]{2,1,0:T(8,128)(2,1)}, bf16[8,256,256]{2,1,0:T(8,128)(2,1)S(1)}, u32[]{:S(2)}, u32[]{:S(2)}) collective-permute-start(bf16[8,256,256]{2,1,0:T(8,128)(2,1)} %slice.48), channel_id=1, source_target_pairs={{0,24},{8,0},{1,25},{9,1},{2,26},{10,2},{3,27},{11,3},{4,28},{12,4... | collective-permute-start | bytes 3145736 | tf_op jit(solution)/shard_map/far8/ppermute | solution.py:293
  36.1 10.1 %collective-permute-start.5 = (bf16[4,256,256]{2,1,0:T(8,128)(2,1)}, bf16[4,256,256]{2,1,0:T(8,128)(2,1)}, u32[]{:S(2)}, u32[]{:S(2)}) collective-permute-start(bf16[4,256,256]{2,1,0:T(8,128)(2,1)} %broadcast_select_fusion), channel_id=1, source_target_pairs={{0,4},{1,5},{2,6},{3,7},{8,12},{9,13},{10,14},{11,15},{16,20},{17,... | collective-permute-start | bytes 1572872 | tf_op jit(solution)/shard_map/corner4/ppermute | solution.py:256
  41.9 5.5 %copy-start.4 = (bf16[4,256,256]{2,1,0:T(8,128)(2,1)S(1)}, bf16[4,256,256]{2,1,0:T(8,128)(2,1)}, u32[]{:S(2)}) copy-start(bf16[4,256,256]{2,1,0:T(8,128)(2,1)} %get-tuple-element.53) | copy-start | bytes 1572868
  41.9 8.1 %copy-start.5 = (bf16[3,256,256]{2,1,0:T(8,128)(2,1)S(1)}, bf16[3,256,256]{2,1,0:T(8,128)(2,1)}, u32[]{:S(2)}) copy-start(bf16[3,256,256]{2,1,0:T(8,128)(2,1)} %slice.49) | copy-start | bytes 1179652
  41.9 20.1 %copy-start.3 = (bf16[4,256,256]{2,1,0:T(8,128)(2,1)S(1)}, bf16[4,256,256]{2,1,0:T(8,128)(2,1)}, u32[]{:S(2)}) copy-start(bf16[4,256,256]{2,1,0:T(8,128)(2,1)} %get-tuple-element.34) | copy-start | bytes 1572868
  41.9 49.4 %copy-start.7 = (bf16[2,256,256]{2,1,0:T(8,128)(2,1)S(1)}, bf16[2,256,256]{2,1,0:T(8,128)(2,1)}, u32[]{:S(2)}) copy-start(bf16[2,256,256]{2,1,0:T(8,128)(2,1)} %get-tuple-element.44) | copy-start | bytes 786436
  42.0 52.1 %copy-start.6 = (bf16[2,256,256]{2,1,0:T(8,128)(2,1)S(1)}, bf16[2,256,256]{2,1,0:T(8,128)(2,1)}, u32[]{:S(2)}) copy-start(bf16[2,256,256]{2,1,0:T(8,128)(2,1)} %get-tuple-element.38) | copy-start | bytes 786436
  42.0 54.3 %copy-start.1 = (bf16[1,256,256]{2,1,0:T(8,128)(2,1)S(1)}, bf16[1,256,256]{2,1,0:T(8,128)(2,1)}, u32[]{:S(2)}) copy-start(bf16[1,256,256]{2,1,0:T(8,128)(2,1)} %copy-done) | copy-start | bytes 393220
  47.3 4.0 %collective-permute-start.7 = (bf16[4,256,256]{2,1,0:T(8,128)(2,1)S(1)}, bf16[4,256,256]{2,1,0:T(8,128)(2,1)S(1)}, u32[]{:S(2)}, u32[]{:S(2)}) collective-permute-start(bf16[4,256,256]{2,1,0:T(8,128)(2,1)S(1)} %broadcast_select_fusion.1.mine), channel_id=1, source_target_pairs={{0,1},{1,0},{2,3},{3,2},{4,5},{5,4},{6,7},{7,6},{8,9},{9,8},{10,11... | collective-permute-start | bytes 1572872 | tf_op jit(solution)/shard_map/corner1/ppermute | solution.py:261
  47.4 22.5 %collective-permute-start.9 = (bf16[4,256,256]{2,1,0:T(8,128)(2,1)S(1)}, bf16[4,256,256]{2,1,0:T(8,128)(2,1)S(1)}, u32[]{:S(2)}, u32[]{:S(2)}) collective-permute-start(bf16[4,256,256]{2,1,0:T(8,128)(2,1)S(1)} %copy-done.4), channel_id=1, source_target_pairs={{8,16},{0,8},{9,17},{1,9},{10,18},{2,10},{11,19},{3,11},{12,20},{4... | collective-permute-start | bytes 1572872 | tf_op jit(solution)/shard_map/near4/ppermute | solution.py:293
  48.7 31.5 %collective-permute-start.10 = (bf16[7,256,256]{2,1,0:T(8,128)(2,1)}, bf16[7,256,256]{2,1,0:T(8,128)(2,1)S(1)}, u32[]{:S(2)}, u32[]{:S(2)}) collective-permute-start(bf16[7,256,256]{2,1,0:T(8,128)(2,1)} %collective-permute-done.4.refs_5_.refs_3_), channel_id=1, source_target_pairs={{24,16},{25,17},{26,18},{27,19},{28,20},{29,21},{30,22},{31,23}} | collective-permute-start | bytes 2752520 | tf_op jit(solution)/shard_map/back1/ppermute | solution.py:293
  50.0 28.3 %collective-permute-start.15 = (bf16[3,256,256]{2,1,0:T(8,128)(2,1)S(1)}, bf16[3,256,256]{2,1,0:T(8,128)(2,1)S(1)}, u32[]{:S(2)}, u32[]{:S(2)}) collective-permute-start(bf16[3,256,256]{2,1,0:T(8,128)(2,1)S(1)} %copy-done.5), channel_id=1, source_target_pairs={{8,16},{0,8},{9,17},{1,9},{10,18},{2,10},{11,19},{3,11},{12,20},{4... | collective-permute-start | bytes 1179656 | tf_op jit(solution)/shard_map/near1/ppermute | solution.py:293
  62.0 30.6 %collective-permute-start.8 = (bf16[4,256,256]{2,1,0:T(8,128)(2,1)S(1)}, bf16[4,256,256]{2,1,0:T(8,128)(2,1)S(1)}, u32[]{:S(2)}, u32[]{:S(2)}) collective-permute-start(bf16[4,256,256]{2,1,0:T(8,128)(2,1)S(1)} %copy-done.3), channel_id=1, source_target_pairs={{8,16},{0,8},{9,17},{1,9},{10,18},{2,10},{11,19},{3,11},{12,20},{4... | collective-permute-start | bytes 1572872 | tf_op jit(solution)/shard_map/near8/ppermute | solution.py:293
  69.9 24.1 %collective-permute-start.13 = (bf16[4,256,256]{2,1,0:T(8,128)(2,1)S(1)}, bf16[4,256,256]{2,1,0:T(8,128)(2,1)S(1)}, u32[]{:S(2)}, u32[]{:S(2)}) collective-permute-start(bf16[4,256,256]{2,1,0:T(8,128)(2,1)S(1)} %collective-permute-done.9.refs_2_), channel_id=1, source_target_pairs={{16,24},{17,25},{18,26},{19,27},{20,28},{21,29},{22,30},{23,31}} | collective-permute-start | bytes 1572872 | tf_op jit(solution)/shard_map/on4/ppermute | solution.py:293
  72.9 35.2 %collective-permute-start.12 = (bf16[8,256,256]{2,1,0:T(8,128)(2,1)S(1)}, bf16[8,256,256]{2,1,0:T(8,128)(2,1)S(1)}, u32[]{:S(2)}, u32[]{:S(2)}) collective-permute-start(bf16[8,256,256]{2,1,0:T(8,128)(2,1)S(1)} %collective-permute-done.6.refs_3_), channel_id=1, source_target_pairs={{24,16},{25,17},{26,18},{27,19},{28,20},{29,21},{30,22},{31,23}} | collective-permute-start | bytes 3145736 | tf_op jit(solution)/shard_map/back8/ppermute | solution.py:293
  78.3 17.9 %collective-permute-start.16 = (bf16[3,256,256]{2,1,0:T(8,128)(2,1)S(1)}, bf16[3,256,256]{2,1,0:T(8,128)(2,1)S(1)}, u32[]{:S(2)}, u32[]{:S(2)}) collective-permute-start(bf16[3,256,256]{2,1,0:T(8,128)(2,1)S(1)} %collective-permute-done.15.refs_3_), channel_id=1, source_target_pairs={{16,24},{17,25},{18,26},{19,27},{20,28},{21,29},{22,30},{23,31}} | collective-permute-start | bytes 1179656 | tf_op jit(solution)/shard_map/on1/ppermute | solution.py:293
  91.4 11.1 %collective-permute-start.14 = (bf16[2,256,256]{2,1,0:T(8,128)(2,1)S(1)}, bf16[2,256,256]{2,1,0:T(8,128)(2,1)S(1)}, u32[]{:S(2)}, u32[]{:S(2)}) collective-permute-start(bf16[2,256,256]{2,1,0:T(8,128)(2,1)S(1)} %copy-done.7), channel_id=1, source_target_pairs={{8,16},{0,8},{9,17},{1,9},{10,18},{2,10},{11,19},{3,11},{12,20},{4... | collective-permute-start | bytes 786440 | tf_op jit(solution)/shard_map/near12/ppermute | solution.py:293
  92.7 15.5 %collective-permute-start.19 = (bf16[4,256,256]{2,1,0:T(8,128)(2,1)S(1)}, bf16[4,256,256]{2,1,0:T(8,128)(2,1)S(1)}, u32[]{:S(2)}, u32[]{:S(2)}) collective-permute-start(bf16[4,256,256]{2,1,0:T(8,128)(2,1)S(1)} %collective-permute-done.8.refs_2_), channel_id=1, source_target_pairs={{16,24},{17,25},{18,26},{19,27},{20,28},{21,29},{22,30},{23,31}} | collective-permute-start | bytes 1572872 | tf_op jit(solution)/shard_map/on8/ppermute | solution.py:293
  94.0 12.8 %collective-permute-start.11 = (bf16[2,256,256]{2,1,0:T(8,128)(2,1)S(1)}, bf16[2,256,256]{2,1,0:T(8,128)(2,1)S(1)}, u32[]{:S(2)}, u32[]{:S(2)}) collective-permute-start(bf16[2,256,256]{2,1,0:T(8,128)(2,1)S(1)} %copy-done.6), channel_id=1, source_target_pairs={{8,16},{0,8},{9,17},{1,9},{10,18},{2,10},{11,19},{3,11},{12,20},{4... | collective-permute-start | bytes 786440 | tf_op jit(solution)/shard_map/near14/ppermute | solution.py:293
  102.5 9.4 %collective-permute-start.18 = (bf16[2,256,256]{2,1,0:T(8,128)(2,1)S(1)}, bf16[2,256,256]{2,1,0:T(8,128)(2,1)S(1)}, u32[]{:S(2)}, u32[]{:S(2)}) collective-permute-start(bf16[2,256,256]{2,1,0:T(8,128)(2,1)S(1)} %collective-permute-done.14.refs_2_.refs_5_), channel_id=1, source_target_pairs={{16,24},{17,25},{18,26},{19,27},{20,28},{21,29},{22,30},{23,31}} | collective-permute-start | bytes 786440 | tf_op jit(solution)/shard_map/on12/ppermute | solution.py:293
  106.8 9.7 %collective-permute-start.17 = (bf16[2,256,256]{2,1,0:T(8,128)(2,1)S(1)}, bf16[2,256,256]{2,1,0:T(8,128)(2,1)S(1)}, u32[]{:S(2)}, u32[]{:S(2)}) collective-permute-start(bf16[2,256,256]{2,1,0:T(8,128)(2,1)S(1)} %collective-permute-done.11.refs_2_.refs_5_), channel_id=1, source_target_pairs={{16,24},{17,25},{18,26},{19,27},{20,28},{21,29},{22,30},{23,31}} | collective-permute-start | bytes 786440 | tf_op jit(solution)/shard_map/on14/ppermute | solution.py:293
